TPU v7x, 32 devices: a whole 2x2x4 slice. The times are simulated.
32 devices in a mesh: tok: 8 (over z, x), head: 4 (over y, core).
Axes of the slice: x: 2, y: 2, z: 4, core: 2. Of those that a mesh axis runs over, the one named last changes fastest.
Arguments:
- tokens: bfloat16 [2048, 2048], P(('tok', 'head')), may hold values from -6 to 6
- lengths: int32 [8, 4], P('tok'), may hold values from 1 to 128, 256 in all within a row
- routes: int32 [2048, 8], P('tok'), may hold values from 0 to 15, all different within a row; in each aligned block of 64 rows (0 to 63, 64 to 127, ...) at most 48 rows name the same one
- prefix_kv: bfloat16 [8, 2048, 2, 2048], P('tok', 'head'), may hold values from -6 to 6
- attn_gain: float32 [2048], replicated, may hold values from 0.25 to 1.75
- w_qkv: bfloat16 [2048, 3, 2048], P(None, None, 'head'), may hold values from -0.19605908 to 0.19605908
- w_out: bfloat16 [2048, 2048], P('head'), may hold values from -0.125 to 0.125
- moe_gain: float32 [2048], replicated, may hold values from 0.25 to 1.75
- w_router: bfloat16 [2048, 16], replicated, may hold values from -0.24977002 to 0.24977002
- w_gate: bfloat16 [16, 2048, 1024], P('tok', None, 'head'), may hold values from -0.125 to 0.125
- w_up: bfloat16 [16, 2048, 1024], P('tok', None, 'head'), may hold values from -0.125 to 0.125
- w_down: bfloat16 [16, 1024, 2048], P('tok', 'head'), may hold values from -0.25 to 0.25
Outputs:
- layer_out: bfloat16 [2048, 2048], P(('tok', 'head'))
Inputs may be any that keep to these rules, and one draw needn't show every extreme that they name: lengths[i] are the suffix lengths of the 4 requests of the i-th group of 256 tokens, in order; they sum to 256 and the largest in every row is 128. `routes`: each token names 8 different experts; among the 64 tokens of one device (aligned blocks of rows) no expert is named more than 48 times, a bound that some block reaches.
All inputs are finite; a program needn't handle non-finite values.
Results may differ from a plain program's by a relative error of at most 0.007.
Values may be sent and summed in bfloat16 or wider, within the bound.
No kernel may reach another device: no remote copies, remote signals or barrier semaphores. Data moves between devices by JAX's collectives and lax.ppermute only.
A program may use at most 192 MiB of HBM per device.

v0:
```python
import jax
import jax.numpy as jnp
from jax import lax
from jax.sharding import PartitionSpec as P

HD = 128
PREFIX = 2048


rope_base = 10000.0
norm_eps = 1e-06


def rms_scale(values, gain):
    mean_sq = jnp.mean(values * values, axis=-1, keepdims=True)
    return (values * lax.rsqrt(mean_sq + norm_eps) * gain).astype(jnp.bfloat16)


def rotate(vectors, position):
    half = vectors.shape[-1] // 2
    freq = rope_base ** (-(jnp.arange(half).astype(jnp.float32) * 2.0) / vectors.shape[-1])
    angle = position[:, None].astype(jnp.float32) * freq[None, :]
    cosine = jnp.cos(angle)[:, None, :]
    sine = jnp.sin(angle)[:, None, :]
    first = vectors[..., :half]
    second = vectors[..., half:]
    return jnp.concatenate(
        [first * cosine - second * sine, second * cosine + first * sine], axis=-1
    )


def request_layout(lengths_row, rows, prefix):
    ends = jnp.cumsum(lengths_row)
    index = jnp.arange(rows)
    passed = (index[:, None] >= ends[None, :]).astype(jnp.int32)
    segment = jnp.sum(passed, axis=1)
    offset = index - jnp.sum(passed * lengths_row[None, :], axis=1)
    return (segment, prefix + offset)


def attend(query, key_all, value_all, segment, prefix):
    rows = query.shape[0]
    scores = jnp.einsum("qhd,khd->hqk", query, key_all, preferred_element_type=jnp.float32)
    scores = scores * query.shape[-1] ** (-0.5)
    allowed = jnp.concatenate(
        [jnp.ones((rows, prefix), bool), segment[:, None] == segment[None, :]], axis=1
    )
    scores = jnp.where(allowed[None], scores, -1e30)
    top = jnp.max(scores, axis=-1, keepdims=True)
    expo = jnp.exp(scores - top)
    weights = (expo / jnp.sum(expo, axis=-1, keepdims=True)).astype(jnp.bfloat16)
    mixed = jnp.einsum("hqk,khd->qhd", weights, value_all, preferred_element_type=jnp.float32)
    return mixed.astype(jnp.bfloat16).reshape(rows, -1)


def route_weights(logits, chosen_routes):
    picked = jnp.take_along_axis(logits, chosen_routes, axis=1)
    return jax.nn.softmax(picked, axis=-1)


def ranks_of(blocks, experts):
    onehot = (blocks[..., None] == jnp.arange(experts)).astype(jnp.int32)
    running = jnp.cumsum(onehot, axis=1)
    return jnp.sum(running * onehot, axis=-1) - 1


def expert_work(received, gate_w, up_w, down_w):
    gate = jnp.einsum("slcd,ldf->slcf", received, gate_w, preferred_element_type=jnp.float32)
    up = jnp.einsum("slcd,ldf->slcf", received, up_w, preferred_element_type=jnp.float32)
    act = (jax.nn.silu(gate) * up).astype(jnp.bfloat16)
    return jnp.einsum("slcf,lfd->slcd", act, down_w, preferred_element_type=jnp.float32).astype(
        jnp.bfloat16
    )


def on_device(
    tokens,
    lengths,
    routes,
    prefix_kv,
    attn_gain,
    w_qkv,
    w_out,
    moe_gain,
    w_router,
    w_gate,
    w_up,
    w_down,
):
    tok_dev, width = tokens.shape
    heads_dev = lax.axis_size("head")
    groups = lax.axis_size("tok")
    head_index = lax.axis_index("head")
    local_width = w_qkv.shape[2]
    heads_local = local_width // HD
    normed = rms_scale(tokens.astype(jnp.float32), attn_gain)
    flat_qkv = w_qkv.reshape(width, 3 * local_width)
    qkv = jnp.dot(
        lax.all_gather(normed, "head", axis=0, tiled=True),
        flat_qkv,
        preferred_element_type=jnp.float32,
    )
    rows = qkv.shape[0]
    qkv = qkv.reshape(rows, 3, heads_local, HD)
    segment, position = request_layout(lengths[0], rows, PREFIX)
    query = rotate(qkv[:, 0], position).astype(jnp.bfloat16)
    key_new = rotate(qkv[:, 1], position).astype(jnp.bfloat16)
    value_new = qkv[:, 2].astype(jnp.bfloat16)
    cached = lax.all_to_all(prefix_kv, "head", split_axis=3, concat_axis=1, tiled=True)
    key_all = jnp.concatenate([cached[0, :, 0].reshape(-1, heads_local, HD), key_new], axis=0)
    value_all = jnp.concatenate([cached[0, :, 1].reshape(-1, heads_local, HD), value_new], axis=0)
    mixed = attend(query, key_all, value_all, segment, PREFIX)
    attn = lax.psum_scatter(
        jnp.dot(mixed, w_out, preferred_element_type=jnp.float32),
        "head",
        scatter_dimension=0,
        tiled=True,
    )
    resid = tokens.astype(jnp.float32) + attn
    normed2 = rms_scale(resid, moe_gain)
    experts_dev = w_gate.shape[0]
    experts = experts_dev * groups
    topk = routes.shape[1]
    cap = tok_dev * topk * 3 // (2 * experts)
    own_routes = lax.dynamic_slice_in_dim(routes, head_index * tok_dev, tok_dev, 0)
    logits = jnp.dot(normed2, w_router, preferred_element_type=jnp.float32)
    weights = route_weights(logits, own_routes)
    flat = own_routes.reshape(-1)
    rank = ranks_of(flat.reshape(1, -1), experts).reshape(-1)
    slot = flat * cap + rank
    owner = jnp.arange(flat.shape[0]) // topk
    table = jnp.full((experts * cap,), tok_dev, jnp.int32).at[slot].set(owner)
    padded = jnp.concatenate([normed2, jnp.zeros((1, width), jnp.bfloat16)], axis=0)
    outgoing = padded[table].reshape(groups, experts_dev, cap, width)
    widened = lax.all_gather(
        lax.all_to_all(outgoing, "tok", split_axis=0, concat_axis=0, tiled=True)[:, None],
        "head",
        axis=1,
        tiled=True,
    )
    merged = widened.reshape((-1,) + widened.shape[2:])
    returned = lax.all_to_all(
        expert_work(merged, w_gate, w_up, w_down),
        ("tok", "head"),
        split_axis=0,
        concat_axis=0,
        tiled=True,
    )
    summed = jnp.sum(
        returned.reshape(groups, heads_dev, experts_dev, cap, width).astype(jnp.float32), axis=1
    )
    picked = summed.reshape(experts * cap, width)[slot].reshape(tok_dev, topk, width)
    moe = jnp.sum(picked * weights[:, :, None], axis=1)
    return (resid + moe).astype(jnp.bfloat16)


def solution(mesh):
    placed = (
        P(("tok", "head"), None),
        P("tok", None),
        P("tok", None),
        P("tok", "head", None, None),
        P(),
        P(None, None, "head"),
        P("head", None),
        P(),
        P(),
        P("tok", None, "head"),
        P("tok", None, "head"),
        P("tok", "head", None),
    )
    return jax.shard_map(
        on_device, mesh=mesh, in_specs=placed, out_specs=P(("tok", "head"), None), check_vma=False
    )
```

profile of v0, /device:TPU:0, one launch (start us, length us, event | category | flops | bytes accessed | tf_op | source)
XLA Modules:
  0.0 670.4 jit_solution(16879038816807130966)
XLA Ops:
  6.5 16.1 %copy.57 = bf16[1,512,2,2048]{1,2,0,3:T(2,128)(2,1)} copy(bf16[1,512,2,2048]{3,2,1,0:T(2,128)(2,1)} %param.15) | data formatting | bytes 8388608 | tf_op args[3]
  22.6 5.0 all-to-all-start
  28.8 8.8 %copy.59 = bf16[2048,3,512]{0,2,1:T(8,128)(2,1)} copy(bf16[2048,3,512]{2,0,1:T(8,128)(2,1)} %param.17) | data formatting | bytes 12582912 | tf_op args[5]
  38.5 17.2 %all-gather.4.cloned.1.call-done = bf16[256,2048]{1,0:T(8,128)(2,1)} async-done(((bf16[64,2048]{1,0:T(8,128)(2,1)}), bf16[256,2048]{1,0:T(8,128)(2,1)}) %all-gather.4.cloned.1.call-update) | async-done | bytes 1048592 | tf_op jit(solution)/shard_map/all_gather | solution.py:99
  55.7 5.0 fusion.37
  63.2 18.9 %all-to-all-done = bf16[1,512,2,2048]{1,2,0,3:T(2,128)(2,1)} async-done(((bf16[1,512,2,2048]{1,2,0,3:T(2,128)(2,1)}), bf16[1,512,2,2048]{1,2,0,3:T(2,128)(2,1)}, u32[]{:S(2)}, u32[]{:S(2)}) %all-to-all-start) | async-done | bytes 4194336 | tf_op jit(solution)/shard_map/all_to_all | solution.py:109
  82.1 7.5 %copy.88 = bf16[1,512,2,4,512]{1,3,4,2,0:T(4,128)(2,1)} copy(bf16[1,512,2,4,512]{1,2,4,3,0:T(2,128)(2,1)} %bitcast) | data formatting | bytes 8388608 | tf_op jit(solution)/shard_map/all_to_all | solution.py:109
  89.6 7.7 %all_to_all.22 = bf16[1,2048,2,512]{1,3,2,0:T(8,128)(2,1)} reshape(bf16[1,4,512,2,512]{2,1,4,3,0:T(4,128)(2,1)} %bitcast.106) | data formatting | bytes 8388608 | tf_op jit(solution)/shard_map/all_to_all | solution.py:109
  97.3 4.9 fusion.65
  102.2 3.9 copy.60
  106.2 8.9 %fusion.66 = (f32[4,256]{1,0:T(4,128)S(1)}, f32[4,256,2304]{2,1,0:T(8,128)}) fusion(pred[256,2304]{1,0:T(8,128)(4,1)S(1)} %concatenate.21, bf16[256,4,128]{2,0,1:T(8,128)(2,1)S(1)} %copy.61, bf16[2048,4,128]{2,0,1:T(8,128)(2,1)} %copy.60, bf16[256,4,64]{0,2,1:T(8,128)(2,1)} %get-tuple-element.12, bf16[256,4,64]{0,2,1:T(8,128)(2,1)} %get-tuple-element.11), kind=kOutput, calls=%fused_computation.107 | convolution fusion | flops 618662144 | bytes 12652544 | tf_op jit(solution)/shard_map/sub | solution.py:50
  115.0 6.2 fusion.34
  128.1 28.1 %reduce-scatter.2.cloned.1.call-done = f32[64,2048]{1,0:T(8,128)} async-done(((f32[256,2048]{1,0:T(8,128)}), f32[64,2048]{1,0:T(8,128)}) %reduce-scatter.2.cloned.1.call-update) | async-done | bytes 524304 | tf_op jit(solution)/shard_map/reduce_scatter | solution.py:113
  158.6 4.3 gather_fusion
  162.9 76.3 %all_to_all.28 = bf16[8,2,48,2048]{3,2,1,0:T(8,128)(2,1)} all-to-all(bf16[8,2,48,2048]{3,2,1,0:T(8,128)(2,1)} %bitcast.107), channel_id=1, replica_groups=mesh['tok'=8,'head'=4] {'tok'}, dimensions={0} | all-to-all | bytes 6291456 | tf_op jit(solution)/shard_map/all_to_all | solution.py:136
  239.2 80.3 %all-gather.6.cloned.1.call-done = bf16[8,8,48,2048]{3,2,1,0:T(8,128)(2,1)} async-done(((bf16[8,2,48,2048]{3,2,1,0:T(8,128)(2,1)}), bf16[8,8,48,2048]{3,2,1,0:T(8,128)(2,1)}) %all-gather.6.cloned.1.call-update) | async-done | bytes 12582928 | tf_op jit(solution)/shard_map/all_gather | solution.py:135
  319.5 10.4 %fusion.1 = f32[2,32,48,256]{3,2,1,0:T(8,128)} fusion(bf16[32,2,48,2048]{3,2,1,0:T(8,128)(2,1)} %bitcast.122, bf16[2,2048,256]{2,1,0:T(8,128)(2,1)} %param.22), kind=kOutput, calls=%fused_computation.7 | convolution fusion | flops 3221225472 | bytes 17825792 | tf_op jit(solution)/shard_map/slcd,ldf->slcf/dot_general | solution.py:69
  329.9 19.0 %convert_bitcast_fusion = bf16[32,2,48,2048]{3,2,0,1:T(8,128)(2,1)} fusion(bf16[2,256,2048]{2,1,0:T(8,128)(2,1)S(1)} %copy-done, f32[2,32,48,256]{3,2,1,0:T(8,128)} %fusion.1, bf16[2,2048,256]{2,1,0:T(8,128)(2,1)} %param.21, bf16[32,2,48,2048]{3,2,1,0:T(8,128)(2,1)} %bitcast.123), kind=kOutput, calls=%fused_computation.6 | convolution fusion | flops 6453460992 | bytes 32505856 | tf_op jit(solution)/shard_map/slcf,lfd->slcd/dot_general | solution.py:71
  348.9 10.8 %copy.69 = bf16[32,2,48,2048]{3,2,1,0:T(8,128)(2,1)} copy(bf16[32,2,48,2048]{3,2,0,1:T(8,128)(2,1)} %convert_bitcast_fusion) | data formatting | bytes 25165824 | tf_op jit(solution)/shard_map/convert_element_type | solution.py:71
  359.7 5.0 all-to-all-start.2
  365.0 3.9 gather_fusion.2
  369.4 270.6 %all-to-all-done.2 = bf16[32,2,48,2048]{3,2,1,0:T(8,128)(2,1)} async-done(((bf16[32,2,48,2048]{3,2,1,0:T(8,128)(2,1)}), bf16[32,2,48,2048]{3,2,1,0:T(8,128)(2,1)}, u32[]{:S(2)}, u32[]{:S(2)}) %all-to-all-start.2) | async-done | bytes 12582944 | tf_op jit(solution)/shard_map/all_to_all | solution.py:142
  640.0 11.1 %convert_reduce_fusion = f32[8,2,48,2048]{3,2,1,0:T(8,128)} fusion(bf16[32,2,48,2048]{3,2,1,0:T(8,128)(2,1)} %all-to-all-done.2), kind=kLoop, calls=%fused_computation.5 | loop fusion | flops 11010048 | bytes 18874368 | tf_op jit(solution)/shard_map/reduce_sum | solution.py:149
  651.1 8.3 %gather_fusion.1 = f32[512,2048]{1,0:T(8,128)} fusion(f32[768,2048]{1,0:T(8,128)} %bitcast.105, s32[1024]{0:T(1024)S(1)} %pad_clamp_fusion), kind=kCustom, calls=%fused_computation.1 | custom fusion | bytes 8390656 | tf_op jit(solution)/shard_map/gather | solution.py:152
  (79 shorter events, 18.7 us)
Async XLA Ops:
  6.5 323.4 %copy-start = (bf16[2,256,2048]{2,1,0:T(8,128)(2,1)S(1)}, bf16[2,256,2048]{2,1,0:T(8,128)(2,1)}, u32[]{:S(2)}) copy-start(bf16[2,256,2048]{2,1,0:T(8,128)(2,1)} %param.23) | copy-start | bytes 6291460
  22.6 5.1 copy-start.2
  22.6 5.2 copy-start.7
  22.6 59.5 %all-to-all-start = ((bf16[1,512,2,2048]{1,2,0,3:T(2,128)(2,1)}), bf16[1,512,2,2048]{1,2,0,3:T(2,128)(2,1)}, u32[]{:S(2)}, u32[]{:S(2)}) async-start(bf16[1,512,2,2048]{1,2,0,3:T(2,128)(2,1)} %copy.57), calls=%async_computation | async-start | bytes 8388608 | tf_op jit(solution)/shard_map/all_to_all | solution.py:109
  27.6 28.0 %all-gather.4.cloned.1.call-start = ((), (), s32[]{:S(2)}) async-start(), calls=%async_computation.4 | async-start | bytes 1310720 | tf_op jit(solution)/shard_map/all_gather | solution.py:99
  28.7 8.9 %copy-start.10 = (s32[1,4]{1,0:T(1,128)S(1)}, s32[1,4]{1,0:T(1,128)}, u32[]{:S(2)}) copy-start(s32[1,4]{1,0:T(1,128)} %param.13) | copy-start | bytes 52
  28.7 127.4 %reduce-scatter.2.cloned.1.call-start = ((), (), s32[]{:S(2)}) async-start(), calls=%async_computation.5 | async-start | bytes 2621440 | tf_op jit(solution)/shard_map/reduce_scatter | solution.py:113
  60.7 1.2 copy-start.5
  115.0 6.2 copy-start.4
  121.3 2.2 copy-start.9
  121.3 36.1 %copy-start.8 = (f32[2048]{0:T(1024)S(1)}, f32[2048]{0:T(1024)}, u32[]{:S(2)}) copy-start(f32[2048]{0:T(1024)} %param.19) | copy-start | bytes 24580
  123.4 196.1 %all-gather.6.cloned.1.call-start = ((), (), s32[]{:S(2)}) async-start(), calls=%async_computation.6 | async-start | bytes 15728640 | tf_op jit(solution)/shard_map/all_gather | solution.py:135
  359.7 5.1 copy-start.6
  359.7 280.3 %all-to-all-start.2 = ((bf16[32,2,48,2048]{3,2,1,0:T(8,128)(2,1)}), bf16[32,2,48,2048]{3,2,1,0:T(8,128)(2,1)}, u32[]{:S(2)}, u32[]{:S(2)}) async-start(bf16[32,2,48,2048]{3,2,1,0:T(8,128)(2,1)} %copy.69), calls=%async_computation.3 | async-start | bytes 25165824 | tf_op jit(solution)/shard_map/all_to_all | solution.py:142
  651.1 12.8 %copy-start.1 = (bf16[2,256,2048]{2,1,0:T(8,128)(2,1)S(1)}, bf16[2,256,2048]{2,1,0:T(8,128)(2,1)}, u32[]{:S(2)}) copy-start(bf16[2,256,2048]{2,1,0:T(8,128)(2,1)} %param.23) | copy-start | bytes 6291460
  659.4 3.7 copy-start.3
Sparse Core Ops, SparseCore 0:
  30.0 25.5 all-gather.3
  123.5 32.5 reduce-scatter.1
  239.3 80.1 all-gather.5
where the time goes:
time: 679 us; the launch traced here: 670 us
  waiting for transfers between devices  415 us (61%)
  local copies, waits for them, and re-layouts  81.2 us (12%)
  blocking collectives  76.3 us (11%)
  matrix products  51.8 us (8%)
  other arithmetic  22.4 us (3%)
  between operations  13.4 us (2%)
  starting transfers between devices  10.1 us (1%)
    all_to_all x1, waiting for transfers between devices, on_device(): lax.all_to_all(expert_work(merged, w_gate, w_up, w_down), ('tok', 'head')...  271 us
    all_gather x1, waiting for transfers between devices, on_device(): lax.all_gather(lax.all_to_all(outgoing, 'tok', split_axis=0, concat_axis=...  80.3 us
    all_to_all x1, blocking collectives, on_device(): lax.all_to_all(outgoing, 'tok', split_axis=0, concat_axis=0, tiled=True)  76.3 us
    reduce_scatter x1, waiting for transfers between devices, on_device(): lax.psum_scatter(jnp.dot(mixed, w_out, preferred_element_type=jnp.float32...  28.1 us
    unnamed x25, local copies, waits for them, and re-layouts  25.1 us
    dot_general x1, matrix products, expert_work(): jnp.einsum('slcf,lfd->slcd', act, down_w, preferred_element_type=jnp.floa...  19 us
    all_to_all x1, waiting for transfers between devices, on_device(): lax.all_to_all(prefix_kv, 'head', split_axis=3, concat_axis=1, tiled=True)  18.9 us
    all_gather x1, waiting for transfers between devices, on_device(): lax.all_gather(normed, 'head', axis=0, tiled=True)  17.2 us
  transfers between devices with their start and end apart: 5, of which 5 were waited for; matrix products, arithmetic and copies ran while one was open for 4% of the time, Pallas kernels for 0%

commit v1 on v0

v1 whole, which is shorter than its diff:
```python
import functools

import jax
import jax.numpy as jnp
from jax import lax
from jax.experimental import pallas as pl
from jax.experimental.pallas import tpu as pltpu
from jax.sharding import PartitionSpec as P

HD = 128
PREFIX = 2048
LANES = 128
LOG2E = 1.4426950408889634
rope_base = 10000.0
norm_eps = 1e-06
BF = jnp.bfloat16
F32 = jnp.float32


def params(mib):
    return pltpu.CompilerParams(vmem_limit_bytes=mib << 20)


def cost(flops, moved, exps=0):
    return pl.CostEstimate(flops=flops, bytes_accessed=moved, transcendentals=exps)


def whole(shape):
    return pl.BlockSpec(shape, lambda *_: (0,) * len(shape))


def swap(value, axis, bit):
    size = lax.axis_size(axis)
    return lax.ppermute(value, axis, [(i, i ^ bit) for i in range(size)])


move_x = functools.partial(swap, axis="tok", bit=1)
move_y = functools.partial(swap, axis="head", bit=2)
move_c = functools.partial(swap, axis="head", bit=1)


def from_z(value, k):
    size = lax.axis_size("tok")
    return lax.ppermute(value, "tok", [(i, (i - 2 * k) % size) for i in range(size)])


def to_z(value, k):
    return from_z(value, -k)


def project_kernel(t0, t1, t2, t3, gain, cosine, sine, w, q, k, v, normed):
    part = pl.program_id(0)
    rows = t0.shape[0]

    @pl.when(part == 0)
    def _():
        for i, ref in enumerate((t0, t1, t2, t3)):
            values = ref[...].astype(F32)
            mean_sq = jnp.mean(values * values, axis=-1, keepdims=True)
            scaled = values * lax.rsqrt(mean_sq + norm_eps) * gain[...]
            normed[pl.ds(i * rows, rows), :] = scaled.astype(BF)

    out = jnp.dot(normed[...], w[0], preferred_element_type=F32)

    def rotated(ref):
        for h in range(out.shape[1] // HD):
            one = out[:, h * HD : (h + 1) * HD]
            turned = one * cosine[...] + pltpu.roll(one, HD // 2, 1) * sine[...]
            ref[:, h * HD : (h + 1) * HD] = turned.astype(BF)

    @pl.when(part == 0)
    def _():
        rotated(q)

    @pl.when(part == 1)
    def _():
        rotated(k)

    @pl.when(part == 2)
    def _():
        v[...] = out.astype(BF)


def project(blocks, gain, cosine, sine, w):
    rows, width = blocks[0].shape
    total, local = 4 * rows, w.shape[2]
    shape = jax.ShapeDtypeStruct((total, local), BF)
    return pl.pallas_call(
        project_kernel,
        grid=(3,),
        out_shape=(shape,) * 3,
        in_specs=[whole((rows, width))] * 4
        + [whole((1, width)), whole((total, HD)), whole((total, HD))]
        + [pl.BlockSpec((1, width, local), lambda i: (i, 0, 0))],
        out_specs=(whole((total, local)),) * 3,
        scratch_shapes=[pltpu.VMEM((total, width), BF)],
        compiler_params=params(32),
        cost_estimate=cost(6 * total * width * local, 6 * width * local),
        name="project",
    )(*blocks, gain, cosine, sine, w)


def scores_of(q, keys):
    return lax.dot_general(q, keys, (((1,), (1,)), ((), ())), preferred_element_type=F32)


def attend_pieces(q, pieces):
    scale = HD**-0.5
    scores = []
    for keys, _, allowed in pieces:
        one = scores_of(q, keys)
        scores.append(one if allowed is None else jnp.where(allowed, one, -1e30))
    top = functools.reduce(jnp.maximum, [jnp.max(s, axis=-1, keepdims=True) for s in scores])
    total, mixed = 0.0, 0.0
    for s, (_, values, _) in zip(scores, pieces):
        expo = jnp.exp2((s - top) * (scale * LOG2E))
        total = total + jnp.sum(expo, axis=-1, keepdims=True)
        mixed = mixed + jnp.dot(expo.astype(BF), values, preferred_element_type=F32)
    return mixed / total, top * scale + jnp.log(total)


def own_kernel(group, q, kv_here, kv_there, k, v, seg_row, seg_col, out, stats):
    h = pl.program_id(0)
    same = seg_row[...] == seg_col[...]
    mixed, level = attend_pieces(
        q[...],
        [
            (kv_here[0, :, 0, :], kv_here[0, :, 1, :], None),
            (kv_there[:, 0, :], kv_there[:, 1, :], None),
            (k[...], v[...], same),
        ],
    )
    out[...] = mixed
    lane = lax.broadcasted_iota(jnp.int32, stats.shape, 1)

    @pl.when(h == 0)
    def _():
        stats[...] = jnp.zeros_like(stats)

    stats[...] = jnp.where(lane == h, level, stats[...])


def guest_kernel(group, q, kv_here, kv_there, out):
    h = pl.program_id(0)
    local = out.shape[1] - LANES
    mixed, level = attend_pieces(
        q[...],
        [
            (kv_here[0, :, 0, :], kv_here[0, :, 1, :], None),
            (kv_there[:, 0, :], kv_there[:, 1, :], None),
        ],
    )
    out[:, pl.ds(pl.multiple_of(h * HD, HD), HD)] = mixed.astype(BF)
    lane = lax.broadcasted_iota(jnp.int32, (out.shape[0], LANES), 1)

    @pl.when(h == 0)
    def _():
        out[:, local:] = jnp.zeros((out.shape[0], LANES), BF)

    tail = out[:, local:].astype(F32)
    rest = jnp.broadcast_to(level, tail.shape)
    for i in range(3):
        piece = rest.astype(BF).astype(F32)
        tail = jnp.where(lane == 3 * h + i, piece, tail)
        rest = rest - piece
    out[:, local:] = tail.astype(BF)


def kv_specs(depth, first):
    return [
        pl.BlockSpec((1, depth, 2, HD), lambda i, g: (0, 0, 0, g[0] * 4 + i)),
        pl.BlockSpec((depth, 2, HD), lambda i, g: (0, 0, first + i)),
    ]


def attend_own(group, q, kv, kv_there, k, v, seg_row, seg_col):
    rows, local = q.shape
    heads, depth = local // HD, kv.shape[1]
    block = pl.BlockSpec((rows, HD), lambda i, g: (0, i))
    keys = 2 * depth + rows
    return pl.pallas_call(
        own_kernel,
        grid_spec=pltpu.PrefetchScalarGridSpec(
            num_scalar_prefetch=1,
            grid=(heads,),
            in_specs=[block]
            + kv_specs(depth, 0)
            + [block, block, whole((rows, 1)), whole((1, rows))],
            out_specs=(block, whole((rows, LANES))),
        ),
        out_shape=(
            jax.ShapeDtypeStruct((rows, local), F32),
            jax.ShapeDtypeStruct((rows, LANES), F32),
        ),
        compiler_params=params(32),
        cost_estimate=cost(4 * rows * keys * local, 4 * keys * local, rows * keys * heads),
        name="attend_own",
    )(group, q, kv, kv_there, k, v, seg_row, seg_col)


def attend_guest(group, q, kv, kv_there):
    rows, local = q.shape
    heads, depth = local // HD, kv.shape[1]
    keys = 2 * depth
    return pl.pallas_call(
        guest_kernel,
        grid_spec=pltpu.PrefetchScalarGridSpec(
            num_scalar_prefetch=1,
            grid=(heads,),
            in_specs=[pl.BlockSpec((rows, HD), lambda i, g: (0, i))] + kv_specs(depth, heads),
            out_specs=whole((rows, local + LANES)),
        ),
        out_shape=jax.ShapeDtypeStruct((rows, local + LANES), BF),
        compiler_params=params(32),
        cost_estimate=cost(4 * rows * keys * local, 4 * keys * local, rows * keys * heads),
        name="attend_guest",
    )(group, q, kv, kv_there)


def join_kernel(own, own_stats, guest, w, keep, send):
    local = own.shape[1]
    dev = keep.shape[0] // 2
    heads = []
    for h in range(local // HD):
        cols = slice(h * HD, (h + 1) * HD)
        first = own_stats[:, h : h + 1]
        second = functools.reduce(
            jnp.add, [guest[:, local + 3 * h + i : local + 3 * h + i + 1].astype(F32) for i in range(3)]
        )
        top = jnp.maximum(first, second)
        a, b = jnp.exp(first - top), jnp.exp(second - top)
        heads.append(((own[:, cols] * a + guest[:, cols].astype(F32) * b) / (a + b)).astype(BF))
    mixed = jnp.concatenate(heads, axis=1)
    out = jnp.dot(mixed, w[...], preferred_element_type=F32)
    for i in range(2):
        keep[pl.ds(i * dev, dev), :] = out[2 * i * dev : (2 * i + 1) * dev]
        send[pl.ds(i * dev, dev), :] = out[(2 * i + 1) * dev : (2 * i + 2) * dev].astype(BF)


def join(own, own_stats, guest, w):
    rows, local = own.shape
    width = w.shape[1]
    return pl.pallas_call(
        join_kernel,
        out_shape=(
            jax.ShapeDtypeStruct((rows // 2, width), F32),
            jax.ShapeDtypeStruct((rows // 2, width), BF),
        ),
        compiler_params=params(32),
        cost_estimate=cost(2 * rows * local * width, 2 * local * width + 6 * rows * width // 2),
        name="join",
    )(own, own_stats, guest, w)


def entry_kernel(me, tokens, keep, arrived, gain, w_router, routes, resid, message):
    width = tokens.shape[1]
    experts = w_router.shape[1]
    values = tokens[...].astype(F32) + keep[...] + arrived[...].astype(F32)
    resid[...] = values
    mean_sq = jnp.mean(values * values, axis=-1, keepdims=True)
    normed = (values * lax.rsqrt(mean_sq + norm_eps) * gain[...]).astype(BF)
    message[:, :width] = normed
    logits = jnp.dot(normed, w_router[...], preferred_element_type=F32)
    lane = lax.broadcasted_iota(jnp.int32, logits.shape, 1)
    chosen = lane < 0
    for i in range(routes.shape[1]):
        chosen = chosen | (lane == routes[:, i : i + 1])
    logits = jnp.where(chosen, logits, -jnp.inf)
    expo = jnp.exp(logits - jnp.max(logits, axis=-1, keepdims=True))
    share = expo / jnp.sum(expo, axis=-1, keepdims=True)
    high = share.astype(BF)
    low = (share - high.astype(F32)).astype(BF)
    message[:, width:] = jnp.zeros((tokens.shape[0], LANES), BF)
    message[:, width : width + experts] = high
    message[:, width + LANES // 2 : width + LANES // 2 + experts] = low


def entry(me, tokens, keep, arrived, gain, w_router, routes):
    rows, width = tokens.shape
    experts, topk = w_router.shape[1], routes.shape[1]
    return pl.pallas_call(
        entry_kernel,
        grid_spec=pltpu.PrefetchScalarGridSpec(
            num_scalar_prefetch=1,
            grid=(1,),
            in_specs=[
                whole((rows, width)),
                whole((rows, width)),
                whole((rows, width)),
                whole((1, width)),
                whole((width, experts)),
                pl.BlockSpec((rows, topk), lambda i, m: (m[0], 0)),
            ],
            out_specs=(whole((rows, width)), whole((rows, width + LANES))),
        ),
        out_shape=(
            jax.ShapeDtypeStruct((rows, width), F32),
            jax.ShapeDtypeStruct((rows, width + LANES), BF),
        ),
        compiler_params=params(32),
        cost_estimate=cost(2 * rows * width * LANES, 12 * rows * width),
        name="entry",
    )(me, tokens, keep, arrived, gain, w_router, routes)


def expert_kernel(sizes, tile, group, *refs):
    count = len(sizes)
    pieces, (gate, up, down), out = refs[:count], refs[count : count + 3], refs[count + 3]
    held, sems = refs[count + 4 :]
    width = gate.shape[1]
    step = pl.program_id(0)

    @pl.when(step == 0)
    def _():
        start = 0
        for ref, size in zip(pieces, sizes):
            done = 0
            while done < size:
                take = min(size - done, tile - (start + done) % tile)
                pltpu.make_async_copy(
                    ref.at[pl.ds(done, take)],
                    held.at[pl.ds(start + done, take)],
                    sems.at[(start + done) // tile],
                ).start()
                done += take
            start += size

    here = pl.ds(pl.multiple_of(step * tile, tile), tile)
    pltpu.make_async_copy(held.at[here], held.at[here], sems.at[step]).wait()
    rows = held[here, :width]
    tail = held[here, width:].astype(F32)
    lane = lax.broadcasted_iota(jnp.int32, tail.shape, 1)
    result = None
    for e in range(gate.shape[0]):
        index = group[0] * gate.shape[0] + e
        hit = (lane == index) | (lane == index + LANES // 2)
        share = jnp.sum(jnp.where(hit, tail, 0.0), axis=1, keepdims=True)
        g = jnp.dot(rows, gate[e], preferred_element_type=F32)
        u = jnp.dot(rows, up[e], preferred_element_type=F32)
        act = (g * jax.nn.sigmoid(g) * u * share).astype(BF)
        one = jnp.dot(act, down[e], preferred_element_type=F32)
        result = one if result is None else result + one
    out[...] = result.astype(BF)


def expert_work(group, pieces, gate, up, down, tile=256):
    sizes = [p.shape[0] for p in pieces]
    total = sum(sizes)
    tile = min(tile, total)
    wide, width = pieces[0].shape[1], gate.shape[1]
    flops = 6 * total * gate.shape[0] * width * gate.shape[2]
    return pl.pallas_call(
        functools.partial(expert_kernel, sizes, tile),
        grid_spec=pltpu.PrefetchScalarGridSpec(
            num_scalar_prefetch=1,
            grid=(total // tile,),
            in_specs=[pl.BlockSpec(memory_space=pl.ANY)] * len(pieces)
            + [whole(gate.shape), whole(up.shape), whole(down.shape)],
            out_specs=pl.BlockSpec((tile, width), lambda i, g: (i, 0)),
            scratch_shapes=[
                pltpu.VMEM((total, wide), BF),
                pltpu.SemaphoreType.DMA((total // tile,)),
            ],
        ),
        out_shape=jax.ShapeDtypeStruct((total, width), BF),
        compiler_params=params(48),
        cost_estimate=cost(flops, 4 * total * width + 6 * gate.size),
        name="experts",
    )(group, *pieces, gate, up, down)


def add_bf(*values):
    return functools.reduce(jnp.add, [v.astype(F32) for v in values]).astype(BF)


def gather_level(rows):
    half = rows.shape[1] // 2
    by_y, by_x = move_y(rows), move_x(rows)
    corner_a, corner_b = move_y(by_x[:, :half]), move_x(by_y[:, half:])
    return [rows, by_y, by_x, corner_a, corner_b]


def flat(value):
    return value.reshape(-1, value.shape[-1])


def reduce_level(count, half, kept, sent):
    total = add_bf(kept, move_c(sent))
    width = total.shape[1]
    n = count * 2 * half
    here, by_y, by_x = (total[i * n : (i + 1) * n].reshape(count, 2, half, width) for i in range(3))
    corner_a = total[3 * n : 3 * n + n // 2].reshape(count, half, width)
    corner_b = total[3 * n + n // 2 :].reshape(count, half, width)
    got_a, got_b = move_y(corner_a), move_x(corner_b)
    to_x = jnp.stack([add_bf(by_x[:, 0], got_a), by_x[:, 1]], axis=1)
    to_y = jnp.stack([by_y[:, 0], add_bf(by_y[:, 1], got_b)], axis=1)
    got_x, got_y = move_x(to_x), move_y(to_y)
    return functools.reduce(jnp.add, [v.astype(F32) for v in (here, got_x, got_y)])


def mixture(group, resid, message, gate, up, down):
    rows, width = resid.shape
    depth = lax.axis_size("tok") // 2
    column = [message] + [from_z(message, k) for k in range(1, depth)]
    pieces = gather_level(jnp.stack(column))
    theirs = [flat(move_c(p)) for p in pieces]
    pieces = [flat(p) for p in pieces]
    sent = expert_work(group, theirs, gate, up, down)
    kept = expert_work(group, pieces, gate, up, down)
    sums = reduce_level(depth, rows // 2, kept, sent).reshape(depth, rows, width)
    total = resid + sums[0]
    for k in range(1, depth):
        total = total + to_z(sums[k].astype(BF), k).astype(F32)
    return total.astype(BF)


def request_layout(lengths_row, index):
    ends = jnp.cumsum(lengths_row)
    passed = (index[:, None] >= ends[None, :]).astype(jnp.int32)
    segment = jnp.sum(passed, axis=1)
    offset = index - jnp.sum(passed * lengths_row[None, :], axis=1)
    return segment, PREFIX + offset


def rotation(position):
    half = HD // 2
    freq = rope_base ** (-(jnp.arange(half).astype(F32) * 2.0) / HD)
    angle = position[:, None].astype(F32) * freq[None, :]
    cosine, sine = jnp.cos(angle), jnp.sin(angle)
    return jnp.concatenate([cosine, cosine], 1), jnp.concatenate([-sine, sine], 1)


def on_device(
    tokens, lengths, routes, prefix_kv, attn_gain, w_qkv, w_out, moe_gain, w_router, w_gate, w_up, w_down
):
    dev, width = tokens.shape
    local = w_qkv.shape[2]
    me = lax.axis_index("head")
    group = lax.axis_index("tok").astype(jnp.int32).reshape(1)

    by_c, by_y = move_c(tokens), move_y(tokens)
    blocks = [tokens, by_c, by_y, move_c(by_y)]

    def columns(who):
        return lax.dynamic_slice_in_dim(prefix_kv[0], who * local, local, 2)

    kv_there = move_c(jnp.concatenate([columns(me ^ 1), columns(me ^ 3)], axis=2))

    index = ((me ^ jnp.arange(4))[:, None] * dev + jnp.arange(dev)[None, :]).reshape(-1)
    segment, position = request_layout(lengths[0], index)
    cosine, sine = rotation(position)

    q, k, v = project(
        blocks, attn_gain.reshape(1, -1), cosine, sine, jnp.transpose(w_qkv, (1, 0, 2))
    )
    guest_q = move_y(q)
    mine = me.astype(jnp.int32).reshape(1)
    own, own_stats = attend_own(
        mine, q, prefix_kv, kv_there, k, v, segment.reshape(-1, 1), segment.reshape(1, -1)
    )
    guest = move_y(attend_guest(mine ^ 2, guest_q, prefix_kv, kv_there))
    keep, send = join(own, own_stats, guest, w_out)
    chip = keep + move_c(send).astype(F32)
    arrived = move_y(chip[dev:].astype(BF))
    resid, message = entry(
        mine, tokens, chip[:dev], arrived, moe_gain.reshape(1, -1), w_router, routes
    )
    return mixture(group, resid, message, w_gate, w_up, w_down)


def solution(mesh):
    placed = (
        P(("tok", "head"), None),
        P("tok", None),
        P("tok", None),
        P("tok", "head", None, None),
        P(),
        P(None, None, "head"),
        P("head", None),
        P(),
        P(),
        P("tok", None, "head"),
        P("tok", None, "head"),
        P("tok", "head", None),
    )
    return jax.shard_map(
        on_device, mesh=mesh, in_specs=placed, out_specs=P(("tok", "head"), None), check_vma=False
    )
```

time: 679 us -> 233 us (0.34)
  waiting for transfers between devices: 415 us -> 129 us
  blocking collectives: 76.3 us -> 0 us
  local copies, waits for them, and re-layouts: 81.2 us -> 13.1 us
  matrix products: 51.8 us -> 0 us
  Pallas kernels: 0 us -> 48 us
  starting transfers between devices: 10.1 us -> 27.8 us
  between operations: 13.4 us -> 0.39 us
  other arithmetic: 22.4 us -> 10.6 us
    all_to_all x2 -> x0, waiting for transfers between devices: 289 us -> none  [the longest x1 271 us: on_device(): lax.all_to_all(expert_work(merged, w_gate, w_up, w_down), ('tok', 'head')...]
    ppermute x0 -> x28, waiting for transfers between devices: none -> 129 us  [the longest x22 94.8 us: swap(): return lax.ppermute(value, axis, [(i, i ^ bit) for i in range(size)])]
    all_gather x2 -> x0, waiting for transfers between devices: 97.5 us -> none  [the longest x1 80.3 us: on_device(): lax.all_gather(lax.all_to_all(outgoing, 'tok', split_axis=0, concat_axis=...]
    all_to_all x1 -> x0, blocking collectives: 76.3 us -> none  [on_device(): lax.all_to_all(outgoing, 'tok', split_axis=0, concat_axis=0, tiled=True)]
    pallas_call x0 -> x7, Pallas kernels: none -> 48 us  [the longest x2 24.9 us: expert_work(): pl.pallas_call(functools.partial(expert_kernel, sizes, tile), grid_spec=p...]
    dot_general x6 -> x0, matrix products: 42.9 us -> none  [the longest x1 19 us: expert_work(): jnp.einsum('slcf,lfd->slcd', act, down_w, preferred_element_type=jnp.floa...]
    reduce_scatter x1 -> x0, waiting for transfers between devices: 28.1 us -> none  [on_device(): lax.psum_scatter(jnp.dot(mixed, w_out, preferred_element_type=jnp.float32...]
    ppermute x0 -> x28, starting transfers between devices: none -> 27.8 us  [the longest x22 15.8 us: swap(): return lax.ppermute(value, axis, [(i, i ^ bit) for i in range(size)])]
  transfers between devices with their start and end apart: 5 -> 28, of which waited for: 5 -> 18; matrix products, arithmetic and copies ran while one was open for 4% -> 1% of each run, Pallas kernels for 0% -> 10%
where the time goes in v1:
time: 233 us; the launch traced here: 229 us
  waiting for transfers between devices  129 us (55%)
  Pallas kernels  48 us (21%)
  starting transfers between devices  27.8 us (12%)
  local copies, waits for them, and re-layouts  13.1 us (6%)
  other arithmetic  10.6 us (5%)
    ppermute x22, waiting for transfers between devices, swap(): return lax.ppermute(value, axis, [(i, i ^ bit) for i in range(size)])  94.8 us
    ppermute x6, waiting for transfers between devices, from_z(): lax.ppermute(value, 'tok', [(i, (i - 2 * k) % size) for i in range(size)])  34.5 us
    pallas_call x2, Pallas kernels, expert_work(): pl.pallas_call(functools.partial(expert_kernel, sizes, tile), grid_spec=p...  24.9 us
    ppermute x22, starting transfers between devices, swap(): return lax.ppermute(value, axis, [(i, i ^ bit) for i in range(size)])  15.8 us
    ppermute x6, starting transfers between devices, from_z(): lax.ppermute(value, 'tok', [(i, (i - 2 * k) % size) for i in range(size)])  12 us
    pallas_call x1, Pallas kernels, attend_own(): pl.pallas_call(own_kernel, grid_spec=pltpu.PrefetchScalarGridSpec(num_sca...  9.02 us
    pallas_call x1, Pallas kernels, attend_guest(): pl.pallas_call(guest_kernel, grid_spec=pltpu.PrefetchScalarGridSpec(num_s...  8.7 us
    unnamed x32, local copies, waits for them, and re-layouts  8.09 us
  transfers between devices with their start and end apart: 28, of which 18 were waited for; matrix products, arithmetic and copies ran while one was open for 1% of the time, Pallas kernels for 10%

profile of v1, /device:TPU:0, one launch (start us, length us, event | category | flops | bytes accessed | tf_op | source)
XLA Modules:
  0.0 229.1 jit_solution(13724445898141943504)
XLA Ops:
  0.0 3.0 %dynamic-slice_bitcast_fusion.1 = (bf16[512,2,512]{2,1,0:T(2,128)(2,1)S(1)}, bf16[512,2,512]{2,1,0:T(2,128)(2,1)S(1)}) fusion(bf16[1,512,2,2048]{3,2,1,0:T(2,128)(2,1)} %kv_here.3, s32[]{:T(128)S(6)} %select_n.6, s32[]{:T(128)S(6)} %select_n.7), kind=kLoop, calls=%fused_computation.13 | loop fusion | bytes 4194312 | tf_op jit(solution)/shard_map/dynamic_slice | solution.py:445
  3.0 3.2 %pad_maximum_fusion = bf16[512,2,1024]{2,1,0:T(2,128)(2,1)} fusion(bf16[512,2,512]{2,1,0:T(2,128)(2,1)S(1)} %get-tuple-element.33, bf16[512,2,512]{2,1,0:T(2,128)(2,1)S(1)} %get-tuple-element.32), kind=kLoop, calls=%fused_computation.1 | loop fusion | flops 4194304 | bytes 4194304 | tf_op jit(solution)/shard_map/concatenate | solution.py:447
  6.7 2.5 %collective-permute-start.1 = (bf16[64,2048]{1,0:T(8,128)(2,1)S(1)}, bf16[64,2048]{1,0:T(8,128)(2,1)S(1)}, u32[]{:S(2)}, u32[]{:S(2)}) collective-permute-start(bf16[64,2048]{1,0:T(8,128)(2,1)S(1)} %copy-done.4), channel_id=1, source_target_pairs={{0,2},{1,3},{2,0},{3,1},{4,6},{5,7},{6,4},{7,5},{8,10},{9,11},{10,... | collective-permute-start | bytes 786440 | tf_op jit(solution)/shard_map/ppermute | solution.py:34
  9.9 6.3 %collective-permute-done.1.t2 = bf16[64,2048]{1,0:T(8,128)(2,1)S(1)} collective-permute-done((bf16[64,2048]{1,0:T(8,128)(2,1)S(1)}, bf16[64,2048]{1,0:T(8,128)(2,1)S(1)}, u32[]{:S(2)}, u32[]{:S(2)}) %collective-permute-start.1) | collective-permute-done | bytes 262176 | tf_op jit(solution)/shard_map/ppermute | solution.py:34
  17.8 2.8 %copy-done.2 = bf16[2048,3,512]{2,0,1:T(8,128)(2,1)S(1)} copy-done((bf16[2048,3,512]{2,0,1:T(8,128)(2,1)S(1)}, bf16[2048,3,512]{2,0,1:T(8,128)(2,1)}, u32[]{:S(2)}) %copy-start.2) | copy-done | bytes 6291480
  20.5 3.0 %project.1 = (bf16[256,512]{1,0:T(8,128)(2,1)S(1)}, bf16[256,512]{1,0:T(8,128)(2,1)S(1)}, bf16[256,512]{1,0:T(8,128)(2,1)S(1)}) custom-call(bf16[64,2048]{1,0:T(8,128)(2,1)S(1)} %copy-done.4, bf16[64,2048]{1,0:T(8,128)(2,1)S(1)} %collective-permute-done.t1, bf16[64,2048]{1,0:T(8,128)(2,1)S(1)} %collective-permute-done.1.t2, ...), custom_call_target="tpu_custom_call" | custom-call | flops 1610612736 | bytes 6291456 | tf_op jit(solution)/shard_map/project/pallas_call | solution.py:88
  26.0 6.6 %collective-permute-done.4.q = bf16[256,512]{1,0:T(8,128)(2,1)S(1)} collective-permute-done((bf16[256,512]{1,0:T(8,128)(2,1)S(1)}, bf16[256,512]{1,0:T(8,128)(2,1)S(1)}, u32[]{:S(2)}, u32[]{:S(2)}) %collective-permute-start.4) | collective-permute-done | bytes 262176 | tf_op jit(solution)/shard_map/ppermute | solution.py:34
  32.6 8.7 %attend_guest.1 = bf16[256,640]{1,0:T(8,128)(2,1)S(1)} custom-call(s32[1]{0:T(128)S(6)} %xor.23.group, bf16[256,512]{1,0:T(8,128)(2,1)S(1)} %collective-permute-done.4.q, bf16[1,512,2,2048]{3,2,1,0:T(2,128)(2,1)S(1)} %copy-done, bf16[512,2,1024]{2,1,0:T(2,128)(2,1)S(1)} %collective-permute-done.3.kv_there), custom_call_target="tpu_custom_call" | custom-call | flops 536870912 | bytes 2097152 | tf_op jit(solution)/shard_map/attend_guest/pallas_call | solution.py:205
  47.4 9.0 %attend_own.1 = (f32[256,512]{1,0:T(8,128)S(1)}, f32[256,128]{1,0:T(8,128)S(1)}) custom-call(s32[1]{0:T(128)} %bitcast.group.me, bf16[256,512]{1,0:T(8,128)(2,1)S(1)} %get-tuple-element.14.q, bf16[1,512,2,2048]{3,2,1,0:T(2,128)(2,1)S(1)} %copy-done.1, bf16[512,2,1024]{2,1,0:T(2,128)(2,1)S(1)} %collective-permute-done.3.kv_there, ...), custom_call_target="tpu_custom_call" | custom-call | flops 671088640 | bytes 2621440 | tf_op jit(solution)/shard_map/attend_own/pallas_call | solution.py:181
  61.1 7.6 %collective-permute-done.7.arrived = bf16[64,2048]{1,0:T(8,128)(2,1)S(1)} collective-permute-done((bf16[64,2048]{1,0:T(8,128)(2,1)S(1)}, bf16[64,2048]{1,0:T(8,128)(2,1)S(1)}, u32[]{:S(2)}, u32[]{:S(2)}) %collective-permute-start.7) | collective-permute-done | bytes 262176 | tf_op jit(solution)/shard_map/ppermute | solution.py:34
  69.4 3.6 %collective-permute-start.8 = (bf16[64,2176]{1,0:T(8,128)(2,1)S(1)}, bf16[64,2176]{1,0:T(8,128)(2,1)S(1)}, u32[]{:S(2)}, u32[]{:S(2)}) collective-permute-start(bf16[64,2176]{1,0:T(8,128)(2,1)S(1)} %get-tuple-element.22), channel_id=1, source_target_pairs={{0,24},{4,28},{8,0},{12,4},{16,8},{20,12},{24,16},{28,20},{1,25},{... | collective-permute-start | bytes 835592 | tf_op jit(solution)/shard_map/ppermute | solution.py:44
  74.0 6.1 %collective-permute-done.8 = bf16[64,2176]{1,0:T(8,128)(2,1)S(1)} collective-permute-done((bf16[64,2176]{1,0:T(8,128)(2,1)S(1)}, bf16[64,2176]{1,0:T(8,128)(2,1)S(1)}, u32[]{:S(2)}, u32[]{:S(2)}) %collective-permute-start.8) | collective-permute-done | bytes 278560 | tf_op jit(solution)/shard_map/ppermute | solution.py:44
  80.1 16.0 %collective-permute-done.9 = bf16[64,2176]{1,0:T(8,128)(2,1)S(1)} collective-permute-done((bf16[64,2176]{1,0:T(8,128)(2,1)S(1)}, bf16[64,2176]{1,0:T(8,128)(2,1)S(1)}, u32[]{:S(2)}, u32[]{:S(2)}) %collective-permute-start.9) | collective-permute-done | bytes 278560 | tf_op jit(solution)/shard_map/ppermute | solution.py:44
  98.4 22.9 %collective-permute-done.12 = bf16[4,64,2176]{2,1,0:T(8,128)(2,1)S(1)} collective-permute-done((bf16[4,64,2176]{2,1,0:T(8,128)(2,1)S(1)}, bf16[4,64,2176]{2,1,0:T(8,128)(2,1)S(1)}, u32[]{:S(2)}, u32[]{:S(2)}) %collective-permute-start.12) | collective-permute-done | bytes 1114144 | tf_op jit(solution)/shard_map/ppermute | solution.py:34
  125.2 9.2 %collective-permute-done.13 = bf16[4,32,2176]{2,1,0:T(8,128)(2,1)S(1)} collective-permute-done((bf16[4,32,2176]{2,1,0:T(8,128)(2,1)S(1)}, bf16[4,32,2176]{2,1,0:T(8,128)(2,1)S(1)}, u32[]{:S(2)}, u32[]{:S(2)}) %collective-permute-start.13) | collective-permute-done | bytes 557088 | tf_op jit(solution)/shard_map/ppermute | solution.py:34
  137.9 13.0 %experts.3 = bf16[1024,2048]{1,0:T(8,128)(2,1)} custom-call(s32[1]{0:T(128)} %bitcast.11.group, bf16[256,2176]{1,0:T(8,128)(2,1)} %bitcast.21.refs_0_, bf16[256,2176]{1,0:T(8,128)(2,1)} %bitcast.22.refs_1_, bf16[256,2176]{1,0:T(8,128)(2,1)} %bitcast.23.refs_2_, bf16[128,2176]{1,0:T(8,128)(2,1)} %bitcast.24.refs_3_, bf16[128,2176]{1,0:T(8,128)(2,1)} %bitcast.25.refs_4_, ...), custom_call_target="tpu_custom_call" | custom-call | flops 6442450944 | bytes 14680064 | tf_op jit(solution)/shard_map/experts/pallas_call | solution.py:352
  151.1 11.9 %experts.2 = bf16[1024,2048]{1,0:T(8,128)(2,1)} custom-call(s32[1]{0:T(128)} %bitcast.11.group, bf16[256,2176]{1,0:T(8,128)(2,1)S(1)} %bitcast.70, bf16[256,2176]{1,0:T(8,128)(2,1)} %bitcast.17.refs_1_, bf16[256,2176]{1,0:T(8,128)(2,1)S(1)} %bitcast.72, bf16[128,2176]{1,0:T(8,128)(2,1)S(1)} %bitcast.77, bf16[128,2176]{1,0:T(8,128)(2,1)} %bitcast.20.refs_4_, ...), custom_call_target="tpu_custom_call" | custom-call | flops 6442450944 | bytes 14680064 | tf_op jit(solution)/shard_map/experts/pallas_call | solution.py:352
  163.0 4.1 %add_convert_fusion = bf16[1024,2048]{1,0:T(8,128)(2,1)S(1)} fusion(bf16[1024,2048]{1,0:T(8,128)(2,1)S(1)} %collective-permute-done.20, bf16[1024,2048]{1,0:T(8,128)(2,1)} %experts.2), kind=kLoop, calls=%fused_computation | loop fusion | flops 8388608 | bytes 12582912 | tf_op jit(solution)/shard_map/convert_element_type | solution.py:373
  170.3 11.6 %collective-permute-done.21 = bf16[4,32,2048]{2,1,0:T(8,128)(2,1)S(1)} collective-permute-done((bf16[4,32,2048]{2,1,0:T(8,128)(2,1)S(1)}, bf16[4,32,2048]{2,1,0:T(8,128)(2,1)S(1)}, u32[]{:S(2)}, u32[]{:S(2)}) %collective-permute-start.21) | collective-permute-done | bytes 524320 | tf_op jit(solution)/shard_map/ppermute | solution.py:34
  184.9 21.9 %collective-permute-done.22 = bf16[4,2,32,2048]{3,2,0,1:T(8,128)(2,1)S(1)} collective-permute-done((bf16[4,2,32,2048]{3,2,0,1:T(8,128)(2,1)S(1)}, bf16[4,2,32,2048]{3,2,0,1:T(8,128)(2,1)S(1)}, u32[]{:S(2)}, u32[]{:S(2)}) %collective-permute-start.22) | collective-permute-done | bytes 1048608 | tf_op jit(solution)/shard_map/ppermute | solution.py:34
  208.5 2.6 %collective-permute-start.25 = (bf16[64,2048]{1,0:T(8,128)(2,1)S(1)}, bf16[64,2048]{1,0:T(8,128)(2,1)S(1)}, u32[]{:S(2)}, u32[]{:S(2)}) collective-permute-start(bf16[64,2048]{1,0:T(8,128)(2,1)S(1)} %bitcast.90), channel_id=1, source_target_pairs={{0,8},{4,12},{8,16},{12,20},{16,24},{20,28},{24,0},{28,4},{1,9},{5... | collective-permute-start | bytes 786440 | tf_op jit(solution)/shard_map/ppermute | solution.py:44
  213.1 2.8 %collective-permute-start.27 = (bf16[64,2048]{1,0:T(8,128)(2,1)S(1)}, bf16[64,2048]{1,0:T(8,128)(2,1)S(1)}, u32[]{:S(2)}, u32[]{:S(2)}) collective-permute-start(bf16[64,2048]{1,0:T(8,128)(2,1)S(1)} %bitcast.88), channel_id=1, source_target_pairs={{0,24},{4,28},{8,0},{12,4},{16,8},{20,12},{24,16},{28,20},{1,25},{... | collective-permute-start | bytes 786440 | tf_op jit(solution)/shard_map/ppermute | solution.py:44
  215.9 3.5 %collective-permute-done.25 = bf16[64,2048]{1,0:T(8,128)(2,1)S(1)} collective-permute-done((bf16[64,2048]{1,0:T(8,128)(2,1)S(1)}, bf16[64,2048]{1,0:T(8,128)(2,1)S(1)}, u32[]{:S(2)}, u32[]{:S(2)}) %collective-permute-start.25) | collective-permute-done | bytes 262176 | tf_op jit(solution)/shard_map/ppermute | solution.py:44
  219.4 8.8 %collective-permute-done.26 = bf16[64,2048]{1,0:T(8,128)(2,1)S(1)} collective-permute-done((bf16[64,2048]{1,0:T(8,128)(2,1)S(1)}, bf16[64,2048]{1,0:T(8,128)(2,1)S(1)}, u32[]{:S(2)}, u32[]{:S(2)}) %collective-permute-start.26) | collective-permute-done | bytes 262176 | tf_op jit(solution)/shard_map/ppermute | solution.py:44
  (100 shorter events, 37.9 us)
Async XLA Ops:
  6.3 26.3 %collective-permute-start.3 = (bf16[512,2,1024]{2,1,0:T(2,128)(2,1)}, bf16[512,2,1024]{2,1,0:T(2,128)(2,1)S(1)}, u32[]{:S(2)}, u32[]{:S(2)}) collective-permute-start(bf16[512,2,1024]{2,1,0:T(2,128)(2,1)} %pad_maximum_fusion), channel_id=1, source_target_pairs={{0,1},{1,0},{2,3},{3,2},{4,5},{5,4},{6,7},{7,6},{8,9},{9,8},{10,11... | collective-permute-start | bytes 6291464 | tf_op jit(solution)/shard_map/ppermute | solution.py:34
  6.7 9.5 %collective-permute-start.1 = (bf16[64,2048]{1,0:T(8,128)(2,1)S(1)}, bf16[64,2048]{1,0:T(8,128)(2,1)S(1)}, u32[]{:S(2)}, u32[]{:S(2)}) collective-permute-start(bf16[64,2048]{1,0:T(8,128)(2,1)S(1)} %copy-done.4), channel_id=1, source_target_pairs={{0,2},{1,3},{2,0},{3,1},{4,6},{5,7},{6,4},{7,5},{8,10},{9,11},{10,... | collective-permute-start | bytes 786440 | tf_op jit(solution)/shard_map/ppermute | solution.py:34
  9.2 7.7 %collective-permute-start = (bf16[64,2048]{1,0:T(8,128)(2,1)S(1)}, bf16[64,2048]{1,0:T(8,128)(2,1)S(1)}, u32[]{:S(2)}, u32[]{:S(2)}) collective-permute-start(bf16[64,2048]{1,0:T(8,128)(2,1)S(1)} %copy-done.4), channel_id=1, source_target_pairs={{0,1},{1,0},{2,3},{3,2},{4,5},{5,4},{6,7},{7,6},{8,9},{9,8},{10,11... | collective-permute-start | bytes 786440 | tf_op jit(solution)/shard_map/ppermute | solution.py:34
  24.3 8.3 %collective-permute-start.4 = (bf16[256,512]{1,0:T(8,128)(2,1)S(1)}, bf16[256,512]{1,0:T(8,128)(2,1)S(1)}, u32[]{:S(2)}, u32[]{:S(2)}) collective-permute-start(bf16[256,512]{1,0:T(8,128)(2,1)S(1)} %get-tuple-element.14.q), channel_id=1, source_target_pairs={{0,2},{1,3},{2,0},{3,1},{4,6},{5,7},{6,4},{7,5},{8,10},{9,11},{10,... | collective-permute-start | bytes 786440 | tf_op jit(solution)/shard_map/ppermute | solution.py:34
  41.3 15.1 %collective-permute-start.5 = (bf16[256,640]{1,0:T(8,128)(2,1)S(1)}, bf16[256,640]{1,0:T(8,128)(2,1)S(1)}, u32[]{:S(2)}, u32[]{:S(2)}) collective-permute-start(bf16[256,640]{1,0:T(8,128)(2,1)S(1)} %attend_guest.1), channel_id=1, source_target_pairs={{0,2},{1,3},{2,0},{3,1},{4,6},{5,7},{6,4},{7,5},{8,10},{9,11},{10,... | collective-permute-start | bytes 983048 | tf_op jit(solution)/shard_map/ppermute | solution.py:34
  60.3 8.4 %collective-permute-start.7 = (bf16[64,2048]{1,0:T(8,128)(2,1)S(1)}, bf16[64,2048]{1,0:T(8,128)(2,1)S(1)}, u32[]{:S(2)}, u32[]{:S(2)}) collective-permute-start(bf16[64,2048]{1,0:T(8,128)(2,1)S(1)} %slice.102), channel_id=1, source_target_pairs={{0,2},{1,3},{2,0},{3,1},{4,6},{5,7},{6,4},{7,5},{8,10},{9,11},{10,... | collective-permute-start | bytes 786440 | tf_op jit(solution)/shard_map/ppermute | solution.py:34
  69.4 10.8 %collective-permute-start.8 = (bf16[64,2176]{1,0:T(8,128)(2,1)S(1)}, bf16[64,2176]{1,0:T(8,128)(2,1)S(1)}, u32[]{:S(2)}, u32[]{:S(2)}) collective-permute-start(bf16[64,2176]{1,0:T(8,128)(2,1)S(1)} %get-tuple-element.22), channel_id=1, source_target_pairs={{0,24},{4,28},{8,0},{12,4},{16,8},{20,12},{24,16},{28,20},{1,25},{... | collective-permute-start | bytes 835592 | tf_op jit(solution)/shard_map/ppermute | solution.py:44
  73.0 23.2 %collective-permute-start.9 = (bf16[64,2176]{1,0:T(8,128)(2,1)S(1)}, bf16[64,2176]{1,0:T(8,128)(2,1)S(1)}, u32[]{:S(2)}, u32[]{:S(2)}) collective-permute-start(bf16[64,2176]{1,0:T(8,128)(2,1)S(1)} %get-tuple-element.22), channel_id=1, source_target_pairs={{0,16},{4,20},{8,24},{12,28},{16,0},{20,4},{24,8},{28,12},{1,17},{... | collective-permute-start | bytes 835592 | tf_op jit(solution)/shard_map/ppermute | solution.py:44
  73.0 23.2 %collective-permute-start.10 = (bf16[64,2176]{1,0:T(8,128)(2,1)S(1)}, bf16[64,2176]{1,0:T(8,128)(2,1)S(1)}, u32[]{:S(2)}, u32[]{:S(2)}) collective-permute-start(bf16[64,2176]{1,0:T(8,128)(2,1)S(1)} %get-tuple-element.22), channel_id=1, source_target_pairs={{0,8},{4,12},{8,16},{12,20},{16,24},{20,28},{24,0},{28,4},{1,9},{5... | collective-permute-start | bytes 835592 | tf_op jit(solution)/shard_map/ppermute | solution.py:44
  96.4 24.9 %collective-permute-start.12 = (bf16[4,64,2176]{2,1,0:T(8,128)(2,1)S(1)}, bf16[4,64,2176]{2,1,0:T(8,128)(2,1)S(1)}, u32[]{:S(2)}, u32[]{:S(2)}) collective-permute-start(bf16[4,64,2176]{2,1,0:T(8,128)(2,1)S(1)} %pad_maximum_fusion.1), channel_id=1, source_target_pairs={{0,4},{4,0},{8,12},{12,8},{16,20},{20,16},{24,28},{28,24},{1,5},{5... | collective-permute-start | bytes 3342344 | tf_op jit(solution)/shard_map/ppermute | solution.py:34
  97.9 25.5 %collective-permute-start.11 = (bf16[4,64,2176]{2,1,0:T(8,128)(2,1)S(1)}, bf16[4,64,2176]{2,1,0:T(8,128)(2,1)}, u32[]{:S(2)}, u32[]{:S(2)}) collective-permute-start(bf16[4,64,2176]{2,1,0:T(8,128)(2,1)S(1)} %pad_maximum_fusion.1), channel_id=1, source_target_pairs={{0,2},{1,3},{2,0},{3,1},{4,6},{5,7},{6,4},{7,5},{8,10},{9,11},{10,... | collective-permute-start | bytes 3342344 | tf_op jit(solution)/shard_map/ppermute | solution.py:34
  98.4 37.2 %collective-permute-start.15 = (bf16[4,64,2176]{2,1,0:T(8,128)(2,1)S(1)}, bf16[4,64,2176]{2,1,0:T(8,128)(2,1)}, u32[]{:S(2)}, u32[]{:S(2)}) collective-permute-start(bf16[4,64,2176]{2,1,0:T(8,128)(2,1)S(1)} %pad_maximum_fusion.1), channel_id=1, source_target_pairs={{0,1},{1,0},{2,3},{3,2},{4,5},{5,4},{6,7},{7,6},{8,9},{9,8},{10,11... | collective-permute-start | bytes 3342344 | tf_op jit(solution)/shard_map/ppermute | solution.py:34
  121.3 13.1 %collective-permute-start.13 = (bf16[4,32,2176]{2,1,0:T(8,128)(2,1)S(1)}, bf16[4,32,2176]{2,1,0:T(8,128)(2,1)S(1)}, u32[]{:S(2)}, u32[]{:S(2)}) collective-permute-start(bf16[4,32,2176]{2,1,0:T(8,128)(2,1)S(1)} %slice.78), channel_id=1, source_target_pairs={{0,2},{1,3},{2,0},{3,1},{4,6},{5,7},{6,4},{7,5},{8,10},{9,11},{10,... | collective-permute-start | bytes 1671176 | tf_op jit(solution)/shard_map/ppermute | solution.py:34
  124.6 11.0 %collective-permute-start.14 = (bf16[4,32,2176]{2,1,0:T(8,128)(2,1)S(1)}, bf16[4,32,2176]{2,1,0:T(8,128)(2,1)}, u32[]{:S(2)}, u32[]{:S(2)}) collective-permute-start(bf16[4,32,2176]{2,1,0:T(8,128)(2,1)S(1)} %slice.79), channel_id=1, source_target_pairs={{0,4},{4,0},{8,12},{12,8},{16,20},{20,16},{24,28},{28,24},{1,5},{5... | collective-permute-start | bytes 1671176 | tf_op jit(solution)/shard_map/ppermute | solution.py:34
  124.6 13.2 %collective-permute-start.16 = (bf16[4,64,2176]{2,1,0:T(8,128)(2,1)}, bf16[4,64,2176]{2,1,0:T(8,128)(2,1)}, u32[]{:S(2)}, u32[]{:S(2)}) collective-permute-start(bf16[4,64,2176]{2,1,0:T(8,128)(2,1)} %collective-permute-done.11), channel_id=1, source_target_pairs={{0,1},{1,0},{2,3},{3,2},{4,5},{5,4},{6,7},{7,6},{8,9},{9,8},{10,11... | collective-permute-start | bytes 3342344 | tf_op jit(solution)/shard_map/ppermute | solution.py:34
  124.7 13.2 %collective-permute-start.17 = (bf16[4,64,2176]{2,1,0:T(8,128)(2,1)S(1)}, bf16[4,64,2176]{2,1,0:T(8,128)(2,1)}, u32[]{:S(2)}, u32[]{:S(2)}) collective-permute-start(bf16[4,64,2176]{2,1,0:T(8,128)(2,1)S(1)} %collective-permute-done.12), channel_id=1, source_target_pairs={{0,1},{1,0},{2,3},{3,2},{4,5},{5,4},{6,7},{7,6},{8,9},{9,8},{10,11... | collective-permute-start | bytes 3342344 | tf_op jit(solution)/shard_map/ppermute | solution.py:34
  150.9 12.1 %collective-permute-start.20 = (bf16[1024,2048]{1,0:T(8,128)(2,1)}, bf16[1024,2048]{1,0:T(8,128)(2,1)S(1)}, u32[]{:S(2)}, u32[]{:S(2)}) collective-permute-start(bf16[1024,2048]{1,0:T(8,128)(2,1)} %experts.3), channel_id=1, source_target_pairs={{0,1},{1,0},{2,3},{3,2},{4,5},{5,4},{6,7},{7,6},{8,9},{9,8},{10,11... | collective-permute-start | bytes 12582920 | tf_op jit(solution)/shard_map/ppermute | solution.py:34
  167.6 14.3 %collective-permute-start.21 = (bf16[4,32,2048]{2,1,0:T(8,128)(2,1)S(1)}, bf16[4,32,2048]{2,1,0:T(8,128)(2,1)S(1)}, u32[]{:S(2)}, u32[]{:S(2)}) collective-permute-start(bf16[4,32,2048]{2,1,0:T(8,128)(2,1)S(1)} %bitcast.84), channel_id=1, source_target_pairs={{0,2},{1,3},{2,0},{3,1},{4,6},{5,7},{6,4},{7,5},{8,10},{9,11},{10,... | collective-permute-start | bytes 1572872 | tf_op jit(solution)/shard_map/ppermute | solution.py:34
  168.7 14.4 %collective-permute-start.23 = (bf16[4,32,2048]{2,1,0:T(8,128)(2,1)S(1)}, bf16[4,32,2048]{2,1,0:T(8,128)(2,1)S(1)}, u32[]{:S(2)}, u32[]{:S(2)}) collective-permute-start(bf16[4,32,2048]{2,1,0:T(8,128)(2,1)S(1)} %bitcast.83), channel_id=1, source_target_pairs={{0,4},{4,0},{8,12},{12,8},{16,20},{20,16},{24,28},{28,24},{1,5},{5... | collective-permute-start | bytes 1572872 | tf_op jit(solution)/shard_map/ppermute | solution.py:34
  182.1 24.7 %collective-permute-start.22 = (bf16[4,2,32,2048]{3,2,0,1:T(8,128)(2,1)S(1)}, bf16[4,2,32,2048]{3,2,0,1:T(8,128)(2,1)S(1)}, u32[]{:S(2)}, u32[]{:S(2)}) collective-permute-start(bf16[4,2,32,2048]{3,2,0,1:T(8,128)(2,1)S(1)} %pad_maximum_fusion.2), channel_id=1, source_target_pairs={{0,4},{4,0},{8,12},{12,8},{16,20},{20,16},{24,28},{28,24},{1,5},{5... | collective-permute-start | bytes 3145736 | tf_op jit(solution)/shard_map/ppermute | solution.py:34
  183.3 24.4 %collective-permute-start.24 = (bf16[4,2,32,2048]{3,2,0,1:T(8,128)(2,1)S(1)}, bf16[4,2,32,2048]{3,2,0,1:T(8,128)(2,1)S(1)}, u32[]{:S(2)}, u32[]{:S(2)}) collective-permute-start(bf16[4,2,32,2048]{3,2,0,1:T(8,128)(2,1)S(1)} %pad_maximum_fusion.3), channel_id=1, source_target_pairs={{0,2},{1,3},{2,0},{3,1},{4,6},{5,7},{6,4},{7,5},{8,10},{9,11},{10,... | collective-permute-start | bytes 3145736 | tf_op jit(solution)/shard_map/ppermute | solution.py:34
  208.5 10.9 %collective-permute-start.25 = (bf16[64,2048]{1,0:T(8,128)(2,1)S(1)}, bf16[64,2048]{1,0:T(8,128)(2,1)S(1)}, u32[]{:S(2)}, u32[]{:S(2)}) collective-permute-start(bf16[64,2048]{1,0:T(8,128)(2,1)S(1)} %bitcast.90), channel_id=1, source_target_pairs={{0,8},{4,12},{8,16},{12,20},{16,24},{20,28},{24,0},{28,4},{1,9},{5... | collective-permute-start | bytes 786440 | tf_op jit(solution)/shard_map/ppermute | solution.py:44
  211.1 17.2 %collective-permute-start.26 = (bf16[64,2048]{1,0:T(8,128)(2,1)S(1)}, bf16[64,2048]{1,0:T(8,128)(2,1)S(1)}, u32[]{:S(2)}, u32[]{:S(2)}) collective-permute-start(bf16[64,2048]{1,0:T(8,128)(2,1)S(1)} %bitcast.89), channel_id=1, source_target_pairs={{0,16},{4,20},{8,24},{12,28},{16,0},{20,4},{24,8},{28,12},{1,17},{... | collective-permute-start | bytes 786440 | tf_op jit(solution)/shard_map/ppermute | solution.py:44
  213.1 15.2 %collective-permute-start.27 = (bf16[64,2048]{1,0:T(8,128)(2,1)S(1)}, bf16[64,2048]{1,0:T(8,128)(2,1)S(1)}, u32[]{:S(2)}, u32[]{:S(2)}) collective-permute-start(bf16[64,2048]{1,0:T(8,128)(2,1)S(1)} %bitcast.88), channel_id=1, source_target_pairs={{0,24},{4,28},{8,0},{12,4},{16,8},{20,12},{24,16},{28,20},{1,25},{... | collective-permute-start | bytes 786440 | tf_op jit(solution)/shard_map/ppermute | solution.py:44
  (18 other events, 92.6 us)

commit v2 on v1

--- a/solution.py
+++ b/solution.py
@@ -11,6 +11,7 @@
 PREFIX = 2048
 LANES = 128
 LOG2E = 1.4426950408889634
+CUTS = 2
 rope_base = 10000.0
 norm_eps = 1e-06
 BF = jnp.bfloat16
@@ -46,6 +47,10 @@
 
 def to_z(value, k):
     return from_z(value, -k)
+
+
+def in_hbm(*values):
+    return [pltpu.with_memory_space_constraint(v, pltpu.HBM) for v in values]
 
 
 def project_kernel(t0, t1, t2, t3, gain, cosine, sine, w, q, k, v, normed):
@@ -94,7 +99,7 @@
         + [pl.BlockSpec((1, width, local), lambda i: (i, 0, 0))],
         out_specs=(whole((total, local)),) * 3,
         scratch_shapes=[pltpu.VMEM((total, width), BF)],
-        compiler_params=params(32),
+        compiler_params=params(20),
         cost_estimate=cost(6 * total * width * local, 6 * width * local),
         name="project",
     )(*blocks, gain, cosine, sine, w)
@@ -166,10 +171,10 @@
     out[:, local:] = tail.astype(BF)
 
 
-def kv_specs(depth, first):
+def kv_specs(depth, heads):
     return [
-        pl.BlockSpec((1, depth, 2, HD), lambda i, g: (0, 0, 0, g[0] * 4 + i)),
-        pl.BlockSpec((depth, 2, HD), lambda i, g: (0, 0, first + i)),
+        pl.BlockSpec((1, depth, 2, HD), lambda i, g: (0, 0, 0, g[0] * heads + i)),
+        pl.BlockSpec((depth, 2, HD), lambda i, g: (0, 0, i)),
     ]
 
 
@@ -184,7 +189,7 @@
             num_scalar_prefetch=1,
             grid=(heads,),
             in_specs=[block]
-            + kv_specs(depth, 0)
+            + kv_specs(depth, heads)
             + [block, block, whole((rows, 1)), whole((1, rows))],
             out_specs=(block, whole((rows, LANES))),
         ),
@@ -192,7 +197,7 @@
             jax.ShapeDtypeStruct((rows, local), F32),
             jax.ShapeDtypeStruct((rows, LANES), F32),
         ),
-        compiler_params=params(32),
+        compiler_params=params(20),
         cost_estimate=cost(4 * rows * keys * local, 4 * keys * local, rows * keys * heads),
         name="attend_own",
     )(group, q, kv, kv_there, k, v, seg_row, seg_col)
@@ -211,7 +216,7 @@
             out_specs=whole((rows, local + LANES)),
         ),
         out_shape=jax.ShapeDtypeStruct((rows, local + LANES), BF),
-        compiler_params=params(32),
+        compiler_params=params(20),
         cost_estimate=cost(4 * rows * keys * local, 4 * keys * local, rows * keys * heads),
         name="attend_guest",
     )(group, q, kv, kv_there)
@@ -246,20 +251,19 @@
             jax.ShapeDtypeStruct((rows // 2, width), F32),
             jax.ShapeDtypeStruct((rows // 2, width), BF),
         ),
-        compiler_params=params(32),
+        compiler_params=params(20),
         cost_estimate=cost(2 * rows * local * width, 2 * local * width + 6 * rows * width // 2),
         name="join",
     )(own, own_stats, guest, w)
 
 
-def entry_kernel(me, tokens, keep, arrived, gain, w_router, routes, resid, message):
+def entry_kernel(me, tokens, keep, arrived, gain, w_router, routes, resid, *messages):
     width = tokens.shape[1]
     experts = w_router.shape[1]
     values = tokens[...].astype(F32) + keep[...] + arrived[...].astype(F32)
     resid[...] = values
     mean_sq = jnp.mean(values * values, axis=-1, keepdims=True)
     normed = (values * lax.rsqrt(mean_sq + norm_eps) * gain[...]).astype(BF)
-    message[:, :width] = normed
     logits = jnp.dot(normed, w_router[...], preferred_element_type=F32)
     lane = lax.broadcasted_iota(jnp.int32, logits.shape, 1)
     chosen = lane < 0
@@ -270,13 +274,18 @@
     share = expo / jnp.sum(expo, axis=-1, keepdims=True)
     high = share.astype(BF)
     low = (share - high.astype(F32)).astype(BF)
-    message[:, width:] = jnp.zeros((tokens.shape[0], LANES), BF)
-    message[:, width : width + experts] = high
-    message[:, width + LANES // 2 : width + LANES // 2 + experts] = low
-
-
-def entry(me, tokens, keep, arrived, gain, w_router, routes):
+    some = tokens.shape[0] // len(messages)
+    for i, message in enumerate(messages):
+        part = slice(i * some, (i + 1) * some)
+        message[:, :width] = normed[part]
+        message[:, width:] = jnp.zeros((some, LANES), BF)
+        message[:, width : width + experts] = high[part]
+        message[:, width + LANES // 2 : width + LANES // 2 + experts] = low[part]
+
+
+def entry(me, tokens, keep, arrived, gain, w_router, routes, cuts):
     rows, width = tokens.shape
+    some = rows // cuts
     experts, topk = w_router.shape[1], routes.shape[1]
     return pl.pallas_call(
         entry_kernel,
@@ -291,127 +300,207 @@
                 whole((width, experts)),
                 pl.BlockSpec((rows, topk), lambda i, m: (m[0], 0)),
             ],
-            out_specs=(whole((rows, width)), whole((rows, width + LANES))),
+            out_specs=(whole((rows, width)),) + (whole((some, width + LANES)),) * cuts,
         ),
         out_shape=(
             jax.ShapeDtypeStruct((rows, width), F32),
-            jax.ShapeDtypeStruct((rows, width + LANES), BF),
-        ),
-        compiler_params=params(32),
+        )
+        + (jax.ShapeDtypeStruct((some, width + LANES), BF),) * cuts,
+        compiler_params=params(20),
         cost_estimate=cost(2 * rows * width * LANES, 12 * rows * width),
         name="entry",
     )(me, tokens, keep, arrived, gain, w_router, routes)
 
 
-def expert_kernel(sizes, tile, group, *refs):
+def expert_kernel(sizes, starts, tile, fetch, group, *refs):
     count = len(sizes)
-    pieces, (gate, up, down), out = refs[:count], refs[count : count + 3], refs[count + 3]
-    held, sems = refs[count + 4 :]
-    width = gate.shape[1]
+    pieces, sources, out = refs[:count], refs[count : count + 3], refs[count + 3]
+    if fetch:
+        *on_chip, held, sems, loads = refs[count + 4 :]
+    else:
+        on_chip, (held, sems) = sources, refs[count + 4 :]
+    gate, up, down = on_chip
+    experts, width = gate.shape[0], gate.shape[1]
     step = pl.program_id(0)
 
-    @pl.when(step == 0)
-    def _():
+    def load(e, i):
+        return pltpu.make_async_copy(sources[i].at[e], on_chip[i].at[e], loads.at[e, i])
+
+    def at_first(act):
+        if fetch:
+            pl.when(step == 0)(act)
+
+    def bring():
         start = 0
-        for ref, size in zip(pieces, sizes):
+        for ref, first, size in zip(pieces, starts, sizes):
             done = 0
             while done < size:
                 take = min(size - done, tile - (start + done) % tile)
                 pltpu.make_async_copy(
-                    ref.at[pl.ds(done, take)],
+                    ref.at[pl.ds(first + done, take)],
                     held.at[pl.ds(start + done, take)],
                     sems.at[(start + done) // tile],
                 ).start()
                 done += take
             start += size
 
+    if fetch:
+
+        @pl.when(step == 0)
+        def _():
+            load(0, 0).start()
+            load(0, 1).start()
+
+    pl.when(step == 0)(bring)
     here = pl.ds(pl.multiple_of(step * tile, tile), tile)
     pltpu.make_async_copy(held.at[here], held.at[here], sems.at[step]).wait()
     rows = held[here, :width]
     tail = held[here, width:].astype(F32)
     lane = lax.broadcasted_iota(jnp.int32, tail.shape, 1)
     result = None
-    for e in range(gate.shape[0]):
-        index = group[0] * gate.shape[0] + e
+    for e in range(experts):
+        index = group[0] * experts + e
         hit = (lane == index) | (lane == index + LANES // 2)
         share = jnp.sum(jnp.where(hit, tail, 0.0), axis=1, keepdims=True)
+
+        def before_gate(e=e):
+            load(e, 0).wait()
+            load(e, 2).start()
+            if e + 1 < experts:
+                load(e + 1, 0).start()
+
+        def before_up(e=e):
+            load(e, 1).wait()
+            if e + 1 < experts:
+                load(e + 1, 1).start()
+
+        at_first(before_gate)
         g = jnp.dot(rows, gate[e], preferred_element_type=F32)
+        at_first(before_up)
         u = jnp.dot(rows, up[e], preferred_element_type=F32)
         act = (g * jax.nn.sigmoid(g) * u * share).astype(BF)
+        at_first(lambda e=e: load(e, 2).wait())
         one = jnp.dot(act, down[e], preferred_element_type=F32)
         result = one if result is None else result + one
     out[...] = result.astype(BF)
 
 
-def expert_work(group, pieces, gate, up, down, tile=256):
-    sizes = [p.shape[0] for p in pieces]
+def expert_call(group, pieces, weights, tile, fetch):
+    gate = weights[0]
+    sizes = [size for _, _, size in pieces]
+    starts = [start for _, start, _ in pieces]
     total = sum(sizes)
-    tile = min(tile, total)
-    wide, width = pieces[0].shape[1], gate.shape[1]
+    wide, width = pieces[0][0].shape[1], gate.shape[1]
     flops = 6 * total * gate.shape[0] * width * gate.shape[2]
+    on_chip = pl.BlockSpec(memory_space=pltpu.VMEM)
+    shape = jax.ShapeDtypeStruct((total, width), BF)
+    spec = pl.BlockSpec((tile, width), lambda i, g: (i, 0))
+    scratch = [pltpu.VMEM((total, wide), BF), pltpu.SemaphoreType.DMA((total // tile,))]
     return pl.pallas_call(
-        functools.partial(expert_kernel, sizes, tile),
+        functools.partial(expert_kernel, sizes, starts, tile, fetch),
         grid_spec=pltpu.PrefetchScalarGridSpec(
             num_scalar_prefetch=1,
             grid=(total // tile,),
             in_specs=[pl.BlockSpec(memory_space=pl.ANY)] * len(pieces)
-            + [whole(gate.shape), whole(up.shape), whole(down.shape)],
-            out_specs=pl.BlockSpec((tile, width), lambda i, g: (i, 0)),
-            scratch_shapes=[
-                pltpu.VMEM((total, wide), BF),
-                pltpu.SemaphoreType.DMA((total // tile,)),
-            ],
+            + [pl.BlockSpec(memory_space=pltpu.HBM) if fetch else on_chip] * 3,
+            out_specs=(spec,) + (on_chip,) * 3 if fetch else spec,
+            scratch_shapes=scratch
+            + ([pltpu.SemaphoreType.DMA((gate.shape[0], 3))] if fetch else []),
         ),
-        out_shape=jax.ShapeDtypeStruct((total, width), BF),
-        compiler_params=params(48),
+        out_shape=(shape,) + tuple(jax.ShapeDtypeStruct(w.shape, w.dtype) for w in weights)
+        if fetch
+        else shape,
+        compiler_params=params(20 + (total >> 7)),
         cost_estimate=cost(flops, 4 * total * width + 6 * gate.size),
         name="experts",
-    )(group, *pieces, gate, up, down)
+    )(group, *[array for array, _, _ in pieces], *weights)
+
+
+def expert_part(group, pieces, weights, fetch=False, most=512):
+    total = sum(size for _, _, size in pieces)
+    tile = next(t for t in range(most, 0, -64) if total % t == 0)
+    return expert_call(group, pieces, weights, tile, fetch)
 
 
 def add_bf(*values):
     return functools.reduce(jnp.add, [v.astype(F32) for v in values]).astype(BF)
 
 
-def gather_level(rows):
-    half = rows.shape[1] // 2
-    by_y, by_x = move_y(rows), move_x(rows)
-    corner_a, corner_b = move_y(by_x[:, :half]), move_x(by_y[:, half:])
-    return [rows, by_y, by_x, corner_a, corner_b]
-
-
-def flat(value):
-    return value.reshape(-1, value.shape[-1])
-
-
-def reduce_level(count, half, kept, sent):
-    total = add_bf(kept, move_c(sent))
-    width = total.shape[1]
-    n = count * 2 * half
-    here, by_y, by_x = (total[i * n : (i + 1) * n].reshape(count, 2, half, width) for i in range(3))
-    corner_a = total[3 * n : 3 * n + n // 2].reshape(count, half, width)
-    corner_b = total[3 * n + n // 2 :].reshape(count, half, width)
-    got_a, got_b = move_y(corner_a), move_x(corner_b)
-    to_x = jnp.stack([add_bf(by_x[:, 0], got_a), by_x[:, 1]], axis=1)
-    to_y = jnp.stack([by_y[:, 0], add_bf(by_y[:, 1], got_b)], axis=1)
+def after(value, *others):
+    return lax.optimization_barrier((value, *others))[0]
+
+
+def join_rows(*values):
+    return jnp.concatenate(values, axis=0)
+
+
+def sections(total):
+    n = total.shape[0] // 4
+    return [total[i * n : (i + 1) * n] for i in range(4)]
+
+
+def reduce_corner(total):
+    corner = sections(total)[3]
+    half = corner.shape[0] // 2
+    return move_y(corner[:half]), move_x(corner[half:])
+
+
+def reduce_rest(total, got):
+    here, by_y, by_x, _ = sections(total)
+    half = here.shape[0] // 2
+    to_x = join_rows(add_bf(by_x[:half], got[0]), by_x[half:])
+    to_y = join_rows(by_y[:half], add_bf(by_y[half:], got[1]))
     got_x, got_y = move_x(to_x), move_y(to_y)
     return functools.reduce(jnp.add, [v.astype(F32) for v in (here, got_x, got_y)])
 
 
-def mixture(group, resid, message, gate, up, down):
-    rows, width = resid.shape
+def mixture(group, resid, messages, weights):
+    rows = messages[0].shape[0]
     depth = lax.axis_size("tok") // 2
-    column = [message] + [from_z(message, k) for k in range(1, depth)]
-    pieces = gather_level(jnp.stack(column))
-    theirs = [flat(move_c(p)) for p in pieces]
-    pieces = [flat(p) for p in pieces]
-    sent = expert_work(group, theirs, gate, up, down)
-    kept = expert_work(group, pieces, gate, up, down)
-    sums = reduce_level(depth, rows // 2, kept, sent).reshape(depth, rows, width)
-    total = resid + sums[0]
-    for k in range(1, depth):
-        total = total + to_z(sums[k].astype(BF), k).astype(F32)
-    return total.astype(BF)
+    n, half = depth * rows, depth * rows // 2
+    first, second = messages
+
+    first_z = [from_z(first, k) for k in range(1, depth)]
+    second = after(second, *first_z)
+    second_z = [from_z(second, k) for k in range(1, depth)]
+
+    here_a = join_rows(first, *first_z)
+    here_b = join_rows(second, *second_z)
+    y_a, x_a = move_y(here_a), move_x(here_a)
+    from_y = move_y(join_rows(x_a[:half], here_b))
+    from_x = move_x(join_rows(y_a[half:], here_b))
+    corner_y, corner_x = move_y(from_x[half : 2 * half]), move_x(from_y[2 * half :])
+
+    def pieces_of(arrays, skip):
+        here, by_y, by_x, by_corner_y, by_corner_x = arrays
+        pieces = [(here, 0, n), (by_y, skip, n), (by_x, skip, n)]
+        return pieces + [(by_corner_y, 0, half), (by_corner_x, 0, half)]
+
+    there_y, there_x = move_c(from_y), move_c(from_x)
+    theirs_a = [move_c(v) for v in (here_a, y_a, x_a)] + [there_y, there_x]
+    theirs_b = [move_c(here_b), there_y, there_x, move_c(corner_y), move_c(corner_x)]
+
+    own_a = [here_a, y_a, x_a, from_y, from_x]
+    own_b = [here_b, from_y, from_x, corner_y, corner_x]
+    kept_a, *held = expert_part(group, pieces_of(own_a, 0), in_hbm(*weights), True)
+    theirs_a = after(theirs_a, kept_a, corner_y, corner_x)
+    sent_a = expert_part(group, pieces_of(theirs_a, 0), held)
+    kept_b = expert_part(group, pieces_of(after(own_b, sent_a), half), held)
+    chip_a = add_bf(kept_a, move_c(sent_a))
+    got_a = reduce_corner(chip_a)
+    sent_b = expert_part(group, pieces_of(after(theirs_b, chip_a, kept_b), half), held)
+    sums_a = reduce_rest(chip_a, got_a)
+    chip_b = add_bf(kept_b, move_c(sent_b))
+    sums_b = reduce_rest(chip_b, reduce_corner(chip_b))
+
+    outs = []
+    for i, sums in enumerate((sums_a, sums_b)):
+        total = resid[i * rows : (i + 1) * rows] + sums[:rows]
+        for k in range(1, depth):
+            part = sums[k * rows : (k + 1) * rows].astype(BF)
+            total = total + to_z(part, k).astype(F32)
+        outs.append(total.astype(BF))
+    return jnp.concatenate(outs, axis=0)
 
 
 def request_layout(lengths_row, index):
@@ -444,28 +533,30 @@
     def columns(who):
         return lax.dynamic_slice_in_dim(prefix_kv[0], who * local, local, 2)
 
-    kv_there = move_c(jnp.concatenate([columns(me ^ 1), columns(me ^ 3)], axis=2))
+    later = after(me, by_c)
+    own_there, guest_there = move_c(columns(later ^ 1)), move_c(columns(later ^ 3))
 
     index = ((me ^ jnp.arange(4))[:, None] * dev + jnp.arange(dev)[None, :]).reshape(-1)
     segment, position = request_layout(lengths[0], index)
     cosine, sine = rotation(position)
 
     q, k, v = project(
-        blocks, attn_gain.reshape(1, -1), cosine, sine, jnp.transpose(w_qkv, (1, 0, 2))
+        blocks, attn_gain.reshape(1, -1), cosine, sine, *in_hbm(jnp.transpose(w_qkv, (1, 0, 2)))
     )
     guest_q = move_y(q)
     mine = me.astype(jnp.int32).reshape(1)
+    (cache,) = in_hbm(prefix_kv)
     own, own_stats = attend_own(
-        mine, q, prefix_kv, kv_there, k, v, segment.reshape(-1, 1), segment.reshape(1, -1)
-    )
-    guest = move_y(attend_guest(mine ^ 2, guest_q, prefix_kv, kv_there))
+        mine, q, cache, own_there, k, v, segment.reshape(-1, 1), segment.reshape(1, -1)
+    )
+    guest = move_y(attend_guest(mine ^ 2, guest_q, cache, guest_there))
     keep, send = join(own, own_stats, guest, w_out)
     chip = keep + move_c(send).astype(F32)
     arrived = move_y(chip[dev:].astype(BF))
-    resid, message = entry(
-        mine, tokens, chip[:dev], arrived, moe_gain.reshape(1, -1), w_router, routes
-    )
-    return mixture(group, resid, message, w_gate, w_up, w_down)
+    resid, *messages = entry(
+        mine, tokens, chip[:dev], arrived, moe_gain.reshape(1, -1), w_router, routes, CUTS
+    )
+    return mixture(group, resid, messages, (w_gate, w_up, w_down))
 
 
 def solution(mesh):

time: 233 us -> 193 us (0.83); the launches traced: 229 us -> 193 us
  waiting for transfers between devices: 129 us -> 78.1 us
  starting transfers between devices: 27.8 us -> 51 us
  other arithmetic: 10.6 us -> 6 us
  local copies, waits for them, and re-layouts: 13.1 us -> 8.94 us
    ppermute x22 -> x33, waiting for transfers between devices: 94.8 us -> 63.1 us  [swap(): return lax.ppermute(value, axis, [(i, i ^ bit) for i in range(size)])]
    ppermute x6 -> x12, waiting for transfers between devices: 34.5 us -> 15 us  [from_z(): lax.ppermute(value, 'tok', [(i, (i - 2 * k) % size) for i in range(size)])]
    ppermute x6 -> x12, starting transfers between devices: 12 us -> 27.2 us  [from_z(): lax.ppermute(value, 'tok', [(i, (i - 2 * k) % size) for i in range(size)])]
    ppermute x22 -> x33, starting transfers between devices: 15.8 us -> 23.8 us  [swap(): return lax.ppermute(value, axis, [(i, i ^ bit) for i in range(size)])]
    unnamed x32 -> x22, local copies, waits for them, and re-layouts: 8.09 us -> 2.62 us
    concatenate x1 -> x5, other arithmetic: 3.24 us -> 0.88 us  [the longest x1 0.72 us: mixture(): return jnp.concatenate(outs, axis=0)]
    pallas_call x2 -> x4, Pallas kernels: 24.9 us -> 22.9 us  [expert_call(): pl.pallas_call(functools.partial(expert_kernel, sizes, starts, tile, fetc...]
  transfers between devices with their start and end apart: 28 -> 45, of which waited for: 18 -> 18; matrix products, arithmetic and copies ran while one was open for 1% -> 6% of each run, Pallas kernels for 10% -> 19%
where the time goes in v2:
time: 193 us
  waiting for transfers between devices  78.1 us (40%)
  starting transfers between devices  51 us (26%)
  Pallas kernels  48 us (25%)
  local copies, waits for them, and re-layouts  8.94 us (5%)
  other arithmetic  6 us (3%)
    ppermute x33, waiting for transfers between devices, swap(): return lax.ppermute(value, axis, [(i, i ^ bit) for i in range(size)])  63.1 us
    ppermute x12, starting transfers between devices, from_z(): lax.ppermute(value, 'tok', [(i, (i - 2 * k) % size) for i in range(size)])  27.2 us
    ppermute x33, starting transfers between devices, swap(): return lax.ppermute(value, axis, [(i, i ^ bit) for i in range(size)])  23.8 us
    pallas_call x4, Pallas kernels, expert_call(): pl.pallas_call(functools.partial(expert_kernel, sizes, starts, tile, fetc...  22.9 us
    ppermute x12, waiting for transfers between devices, from_z(): lax.ppermute(value, 'tok', [(i, (i - 2 * k) % size) for i in range(size)])  15 us
    pallas_call x1, Pallas kernels, attend_own(): pl.pallas_call(own_kernel, grid_spec=pltpu.PrefetchScalarGridSpec(num_sca...  9.01 us
    pallas_call x1, Pallas kernels, attend_guest(): pl.pallas_call(guest_kernel, grid_spec=pltpu.PrefetchScalarGridSpec(num_s...  8.52 us
    pallas_call x1, Pallas kernels, project(): pl.pallas_call(project_kernel, grid=(3,), out_shape=(shape,) * 3, in_spec...  5.28 us
  transfers between devices with their start and end apart: 45, of which 18 were waited for; matrix products, arithmetic and copies ran while one was open for 6% of the time, Pallas kernels for 19%

profile of v2, /device:TPU:0, one launch (start us, length us, event | category | flops | bytes accessed | tf_op | source)
XLA Modules:
  0.0 192.6 jit_solution(9230021009736724724)
XLA Ops:
  0.0 3.0 %collective-permute-start.1 = (bf16[64,2048]{1,0:T(8,128)(2,1)}, bf16[64,2048]{1,0:T(8,128)(2,1)S(1)}, u32[]{:S(2)}, u32[]{:S(2)}) collective-permute-start(bf16[64,2048]{1,0:T(8,128)(2,1)} %tokens.1), channel_id=1, source_target_pairs={{0,2},{1,3},{2,0},{3,1},{4,6},{5,7},{6,4},{7,5},{8,10},{9,11},{10,... | collective-permute-start | bytes 786440 | tf_op jit(solution)/shard_map/ppermute | solution.py:35
  4.7 4.1 %dynamic-slice_bitcast_fusion = (bf16[512,2,512]{2,1,0:T(2,128)(2,1)S(1)}, bf16[512,2,512]{2,1,0:T(2,128)(2,1)}) fusion(bf16[1,512,2,2048]{3,2,1,0:T(2,128)(2,1)} %kv_here.3, s32[]{:T(128)S(6)} %select_n.7, s32[]{:T(128)S(6)} %select_n.6), kind=kLoop, calls=%fused_computation.5 | loop fusion | bytes 4194312 | tf_op jit(solution)/shard_map/dynamic_slice | solution.py:534
  13.0 5.3 %project.1 = (bf16[256,512]{1,0:T(8,128)(2,1)S(1)}, bf16[256,512]{1,0:T(8,128)(2,1)S(1)}, bf16[256,512]{1,0:T(8,128)(2,1)S(1)}) custom-call(bf16[64,2048]{1,0:T(8,128)(2,1)S(1)} %copy-done.1, bf16[64,2048]{1,0:T(8,128)(2,1)S(1)} %collective-permute-done.t1, bf16[64,2048]{1,0:T(8,128)(2,1)S(1)} %collective-permute-done.1.t2, ...), custom_call_target="tpu_custom_call" | custom-call | flops 1610612736 | bytes 6291456 | tf_op jit(solution)/shard_map/project/pallas_call | solution.py:93
  18.7 8.2 %collective-permute-done.4.q = bf16[256,512]{1,0:T(8,128)(2,1)S(1)} collective-permute-done((bf16[256,512]{1,0:T(8,128)(2,1)S(1)}, bf16[256,512]{1,0:T(8,128)(2,1)S(1)}, u32[]{:S(2)}, u32[]{:S(2)}) %collective-permute-start.4) | collective-permute-done | bytes 262176 | tf_op jit(solution)/shard_map/ppermute | solution.py:35
  26.9 8.5 %attend_guest.1 = bf16[256,640]{1,0:T(8,128)(2,1)S(1)} custom-call(s32[1]{0:T(128)S(6)} %xor.22.group, bf16[256,512]{1,0:T(8,128)(2,1)S(1)} %collective-permute-done.4.q, bf16[1,512,2,2048]{3,2,1,0:T(2,128)(2,1)} %kv_here.3, bf16[512,2,512]{2,1,0:T(2,128)(2,1)S(1)} %collective-permute-done.5.kv_there), custom_call_target="tpu_custom_call" | custom-call | flops 536870912 | bytes 2097152 | tf_op jit(solution)/shard_map/attend_guest/pallas_call | solution.py:210
  35.9 9.0 %attend_own.1 = (f32[256,512]{1,0:T(8,128)S(1)}, f32[256,128]{1,0:T(8,128)S(1)}) custom-call(s32[1]{0:T(128)} %bitcast.group.me, bf16[256,512]{1,0:T(8,128)(2,1)S(1)} %get-tuple-element.36.q, bf16[1,512,2,2048]{3,2,1,0:T(2,128)(2,1)} %kv_here.3, bf16[512,2,512]{2,1,0:T(2,128)(2,1)S(1)} %collective-permute-done.3.kv_there, ...), custom_call_target="tpu_custom_call" | custom-call | flops 671088640 | bytes 2621440 | tf_op jit(solution)/shard_map/attend_own/pallas_call | solution.py:186
  51.1 6.1 %collective-permute-done.8.arrived = bf16[64,2048]{1,0:T(8,128)(2,1)S(1)} collective-permute-done((bf16[64,2048]{1,0:T(8,128)(2,1)S(1)}, bf16[64,2048]{1,0:T(8,128)(2,1)S(1)}, u32[]{:S(2)}, u32[]{:S(2)}) %collective-permute-start.8) | collective-permute-done | bytes 262176 | tf_op jit(solution)/shard_map/ppermute | solution.py:35
  57.9 3.0 %collective-permute-start.10 = (bf16[32,2176]{1,0:T(8,128)(2,1)S(1)}, bf16[32,2176]{1,0:T(8,128)(2,1)S(1)}, u32[]{:S(2)}, u32[]{:S(2)}) collective-permute-start(bf16[32,2176]{1,0:T(8,128)(2,1)S(1)} %get-tuple-element.45), channel_id=1, source_target_pairs={{0,16},{4,20},{8,24},{12,28},{16,0},{20,4},{24,8},{28,12},{1,17},{... | collective-permute-start | bytes 417800 | tf_op jit(solution)/shard_map/ppermute | solution.py:45
  65.3 6.1 %collective-permute-done.9 = bf16[32,2176]{1,0:T(8,128)(2,1)S(1)} collective-permute-done((bf16[32,2176]{1,0:T(8,128)(2,1)S(1)}, bf16[32,2176]{1,0:T(8,128)(2,1)S(1)}, u32[]{:S(2)}, u32[]{:S(2)}) %collective-permute-start.9) | collective-permute-done | bytes 139296 | tf_op jit(solution)/shard_map/ppermute | solution.py:45
  81.2 4.4 %collective-permute-done.12.refs_1_ = bf16[128,2176]{1,0:T(8,128)(2,1)S(1)} collective-permute-done((bf16[128,2176]{1,0:T(8,128)(2,1)}, bf16[128,2176]{1,0:T(8,128)(2,1)S(1)}, u32[]{:S(2)}, u32[]{:S(2)}) %collective-permute-start.12) | collective-permute-done | bytes 557088 | tf_op jit(solution)/shard_map/ppermute | solution.py:35
  87.1 4.1 %collective-permute-done.15 = bf16[32,2176]{1,0:T(8,128)(2,1)S(1)} collective-permute-done((bf16[32,2176]{1,0:T(8,128)(2,1)S(1)}, bf16[32,2176]{1,0:T(8,128)(2,1)S(1)}, u32[]{:S(2)}, u32[]{:S(2)}) %collective-permute-start.15) | collective-permute-done | bytes 139296 | tf_op jit(solution)/shard_map/ppermute | solution.py:45
  93.1 15.1 %collective-permute-done.17.refs_3_.refs_1_ = bf16[192,2176]{1,0:T(8,128)(2,1)S(1)} collective-permute-done((bf16[192,2176]{1,0:T(8,128)(2,1)S(1)}, bf16[192,2176]{1,0:T(8,128)(2,1)S(1)}, u32[]{:S(2)}, u32[]{:S(2)}) %collective-permute-start.17) | collective-permute-done | bytes 835616 | tf_op jit(solution)/shard_map/ppermute | solution.py:35
  112.2 8.5 %experts.4 = (bf16[512,2048]{1,0:T(8,128)(2,1)S(1)}, bf16[2,2048,256]{2,1,0:T(8,128)(2,1)S(1)}, bf16[2,2048,256]{2,1,0:T(8,128)(2,1)S(1)}, bf16[2,256,2048]{2,1,0:T(8,128)(2,1)S(1)}) custom-call(s32[1]{0:T(128)} %bitcast.11.group, bf16[128,2176]{1,0:T(8,128)(2,1)} %constant_dynamic-update-slice_fusion.refs_0_, ...), custom_call_target="tpu_custom_call" | custom-call | flops 3221225472 | bytes 10485760 | tf_op jit(solution)/shard_map/experts/pallas_call | solution.py:399
  120.7 5.0 %experts.5 = bf16[512,2048]{1,0:T(8,128)(2,1)S(1)} custom-call(s32[1]{0:T(128)} %bitcast.11.group, bf16[128,2176]{1,0:T(8,128)(2,1)} %collective-permute-done.19.refs_0_, bf16[128,2176]{1,0:T(8,128)(2,1)} %collective-permute-done.20.refs_1_, bf16[128,2176]{1,0:T(8,128)(2,1)} %collective-permute-done.21.refs_2_, ...), custom_call_target="tpu_custom_call" | custom-call | flops 3221225472 | bytes 10485760 | tf_op jit(solution)/shard_map/experts/pallas_call | solution.py:399
  126.8 4.6 %experts.6 = bf16[512,2048]{1,0:T(8,128)(2,1)S(1)} custom-call(s32[1]{0:T(128)} %bitcast.11.group, bf16[128,2176]{1,0:T(8,128)(2,1)S(1)} %get-tuple-element.57.refs_0_, bf16[192,2176]{1,0:T(8,128)(2,1)S(1)} %collective-permute-done.17.refs_3_.refs_1_, bf16[192,2176]{1,0:T(8,128)(2,1)} %collective-permute-done.18.refs_4_.refs_2_, ...), custom_call_target="tpu_custom_call" | custom-call | flops 3221225472 | bytes 10485760 | tf_op jit(solution)/shard_map/experts/pallas_call | solution.py:399
  132.4 4.7 %experts.7 = bf16[512,2048]{1,0:T(8,128)(2,1)S(1)} custom-call(s32[1]{0:T(128)} %bitcast.11.group, bf16[128,2176]{1,0:T(8,128)(2,1)S(1)} %collective-permute-done.34.refs_0_, bf16[192,2176]{1,0:T(8,128)(2,1)} %collective-permute-done.22.refs_3_.refs_1_, bf16[192,2176]{1,0:T(8,128)(2,1)} %collective-permute-done.23.refs_4_.refs_2_, ...), custom_call_target="tpu_custom_call" | custom-call | flops 3221225472 | bytes 10485760 | tf_op jit(solution)/shard_map/experts/pallas_call | solution.py:399
  139.6 6.5 %collective-permute-done.27 = bf16[64,2048]{1,0:T(8,128)(2,1)S(1)} collective-permute-done((bf16[64,2048]{1,0:T(8,128)(2,1)S(1)}, bf16[64,2048]{1,0:T(8,128)(2,1)S(1)}, u32[]{:S(2)}, u32[]{:S(2)}) %collective-permute-start.27) | collective-permute-done | bytes 262176 | tf_op jit(solution)/shard_map/ppermute | solution.py:35
  152.0 4.9 %collective-permute-done.38 = bf16[64,2048]{1,0:T(8,128)(2,1)S(1)} collective-permute-done((bf16[64,2048]{1,0:T(8,128)(2,1)S(1)}, bf16[64,2048]{1,0:T(8,128)(2,1)S(1)}, u32[]{:S(2)}, u32[]{:S(2)}) %collective-permute-start.38) | collective-permute-done | bytes 262176 | tf_op jit(solution)/shard_map/ppermute | solution.py:35
  160.8 8.7 %collective-permute-done.28 = bf16[128,2048]{1,0:T(8,128)(2,1)S(1)} collective-permute-done((bf16[128,2048]{1,0:T(8,128)(2,1)S(1)}, bf16[128,2048]{1,0:T(8,128)(2,1)S(1)}, u32[]{:S(2)}, u32[]{:S(2)}) %collective-permute-start.28) | collective-permute-done | bytes 524320 | tf_op jit(solution)/shard_map/ppermute | solution.py:35
  169.9 3.0 %collective-permute-start.31 = (bf16[32,2048]{1,0:T(8,128)(2,1)S(1)}, bf16[32,2048]{1,0:T(8,128)(2,1)S(1)}, u32[]{:S(2)}, u32[]{:S(2)}) collective-permute-start(bf16[32,2048]{1,0:T(8,128)(2,1)S(1)} %get-tuple-element.89), channel_id=1, source_target_pairs={{0,8},{4,12},{8,16},{12,20},{16,24},{20,28},{24,0},{28,4},{1,9},{5... | collective-permute-start | bytes 393224 | tf_op jit(solution)/shard_map/ppermute | solution.py:45
  174.9 2.8 %collective-permute-start.33 = (bf16[32,2048]{1,0:T(8,128)(2,1)S(1)}, bf16[32,2048]{1,0:T(8,128)(2,1)S(1)}, u32[]{:S(2)}, u32[]{:S(2)}) collective-permute-start(bf16[32,2048]{1,0:T(8,128)(2,1)S(1)} %get-tuple-element.90), channel_id=1, source_target_pairs={{0,24},{4,28},{8,0},{12,4},{16,8},{20,12},{24,16},{28,20},{1,25},{... | collective-permute-start | bytes 393224 | tf_op jit(solution)/shard_map/ppermute | solution.py:45
  179.1 3.0 %collective-permute-start.42 = (bf16[32,2048]{1,0:T(8,128)(2,1)S(1)}, bf16[32,2048]{1,0:T(8,128)(2,1)S(1)}, u32[]{:S(2)}, u32[]{:S(2)}) collective-permute-start(bf16[32,2048]{1,0:T(8,128)(2,1)S(1)} %get-tuple-element.92), channel_id=1, source_target_pairs={{0,8},{4,12},{8,16},{12,20},{16,24},{20,28},{24,0},{28,4},{1,9},{5... | collective-permute-start | bytes 393224 | tf_op jit(solution)/shard_map/ppermute | solution.py:45
  184.1 2.8 %collective-permute-start.44 = (bf16[32,2048]{1,0:T(8,128)(2,1)S(1)}, bf16[32,2048]{1,0:T(8,128)(2,1)S(1)}, u32[]{:S(2)}, u32[]{:S(2)}) collective-permute-start(bf16[32,2048]{1,0:T(8,128)(2,1)S(1)} %get-tuple-element.93), channel_id=1, source_target_pairs={{0,24},{4,28},{8,0},{12,4},{16,8},{20,12},{24,16},{28,20},{1,25},{... | collective-permute-start | bytes 393224 | tf_op jit(solution)/shard_map/ppermute | solution.py:45
  187.0 4.7 %collective-permute-done.43 = bf16[32,2048]{1,0:T(8,128)(2,1)S(1)} collective-permute-done((bf16[32,2048]{1,0:T(8,128)(2,1)S(1)}, bf16[32,2048]{1,0:T(8,128)(2,1)S(1)}, u32[]{:S(2)}, u32[]{:S(2)}) %collective-permute-start.43) | collective-permute-done | bytes 131104 | tf_op jit(solution)/shard_map/ppermute | solution.py:45
  (131 shorter events, 55.7 us)
Async XLA Ops:
  8.8 18.1 %collective-permute-start.5 = (bf16[512,2,512]{2,1,0:T(2,128)(2,1)S(1)}, bf16[512,2,512]{2,1,0:T(2,128)(2,1)S(1)}, u32[]{:S(2)}, u32[]{:S(2)}) collective-permute-start(bf16[512,2,512]{2,1,0:T(2,128)(2,1)S(1)} %get-tuple-element.73), channel_id=1, source_target_pairs={{0,1},{1,0},{2,3},{3,2},{4,5},{5,4},{6,7},{7,6},{8,9},{9,8},{10,11... | collective-permute-start | bytes 3145736 | tf_op jit(solution)/shard_map/ppermute | solution.py:35
  9.3 26.6 %collective-permute-start.3 = (bf16[512,2,512]{2,1,0:T(2,128)(2,1)}, bf16[512,2,512]{2,1,0:T(2,128)(2,1)S(1)}, u32[]{:S(2)}, u32[]{:S(2)}) collective-permute-start(bf16[512,2,512]{2,1,0:T(2,128)(2,1)} %get-tuple-element.74), channel_id=1, source_target_pairs={{0,1},{1,0},{2,3},{3,2},{4,5},{5,4},{6,7},{7,6},{8,9},{9,8},{10,11... | collective-permute-start | bytes 3145736 | tf_op jit(solution)/shard_map/ppermute | solution.py:35
  57.9 14.3 %collective-permute-start.10 = (bf16[32,2176]{1,0:T(8,128)(2,1)S(1)}, bf16[32,2176]{1,0:T(8,128)(2,1)S(1)}, u32[]{:S(2)}, u32[]{:S(2)}) collective-permute-start(bf16[32,2176]{1,0:T(8,128)(2,1)S(1)} %get-tuple-element.45), channel_id=1, source_target_pairs={{0,16},{4,20},{8,24},{12,28},{16,0},{20,4},{24,8},{28,12},{1,17},{... | collective-permute-start | bytes 417800 | tf_op jit(solution)/shard_map/ppermute | solution.py:45
  60.9 12.0 %collective-permute-start.11 = (bf16[32,2176]{1,0:T(8,128)(2,1)S(1)}, bf16[32,2176]{1,0:T(8,128)(2,1)S(1)}, u32[]{:S(2)}, u32[]{:S(2)}) collective-permute-start(bf16[32,2176]{1,0:T(8,128)(2,1)S(1)} %get-tuple-element.45), channel_id=1, source_target_pairs={{0,8},{4,12},{8,16},{12,20},{16,24},{20,28},{24,0},{28,4},{1,9},{5... | collective-permute-start | bytes 417800 | tf_op jit(solution)/shard_map/ppermute | solution.py:45
  73.6 12.0 %collective-permute-start.12 = (bf16[128,2176]{1,0:T(8,128)(2,1)}, bf16[128,2176]{1,0:T(8,128)(2,1)S(1)}, u32[]{:S(2)}, u32[]{:S(2)}) collective-permute-start(bf16[128,2176]{1,0:T(8,128)(2,1)} %constant_dynamic-update-slice_fusion.refs_0_), channel_id=1, source_target_pairs={{0,2},{1,3},{2,0},{3,1},{4,6},{5,7},{6,4},{7,5},{8,10},{9,11},{10,... | collective-permute-start | bytes 1671176 | tf_op jit(solution)/shard_map/ppermute | solution.py:35
  75.0 12.0 %collective-permute-start.13 = (bf16[128,2176]{1,0:T(8,128)(2,1)}, bf16[128,2176]{1,0:T(8,128)(2,1)S(1)}, u32[]{:S(2)}, u32[]{:S(2)}) collective-permute-start(bf16[128,2176]{1,0:T(8,128)(2,1)} %constant_dynamic-update-slice_fusion.refs_0_), channel_id=1, source_target_pairs={{0,4},{4,0},{8,12},{12,8},{16,20},{20,16},{24,28},{28,24},{1,5},{5... | collective-permute-start | bytes 1671176 | tf_op jit(solution)/shard_map/ppermute | solution.py:35
  76.5 10.6 %collective-permute-start.14 = (bf16[32,2176]{1,0:T(8,128)(2,1)S(1)}, bf16[32,2176]{1,0:T(8,128)(2,1)S(1)}, u32[]{:S(2)}, u32[]{:S(2)}) collective-permute-start(bf16[32,2176]{1,0:T(8,128)(2,1)S(1)} %get-tuple-element.47), channel_id=1, source_target_pairs={{0,24},{4,28},{8,0},{12,4},{16,8},{20,12},{24,16},{28,20},{1,25},{... | collective-permute-start | bytes 417800 | tf_op jit(solution)/shard_map/ppermute | solution.py:45
  78.4 12.8 %collective-permute-start.15 = (bf16[32,2176]{1,0:T(8,128)(2,1)S(1)}, bf16[32,2176]{1,0:T(8,128)(2,1)S(1)}, u32[]{:S(2)}, u32[]{:S(2)}) collective-permute-start(bf16[32,2176]{1,0:T(8,128)(2,1)S(1)} %get-tuple-element.47), channel_id=1, source_target_pairs={{0,16},{4,20},{8,24},{12,28},{16,0},{20,4},{24,8},{28,12},{1,17},{... | collective-permute-start | bytes 417800 | tf_op jit(solution)/shard_map/ppermute | solution.py:45
  80.0 11.3 %collective-permute-start.16 = (bf16[32,2176]{1,0:T(8,128)(2,1)S(1)}, bf16[32,2176]{1,0:T(8,128)(2,1)S(1)}, u32[]{:S(2)}, u32[]{:S(2)}) collective-permute-start(bf16[32,2176]{1,0:T(8,128)(2,1)S(1)} %get-tuple-element.47), channel_id=1, source_target_pairs={{0,8},{4,12},{8,16},{12,20},{16,24},{20,28},{24,0},{28,4},{1,9},{5... | collective-permute-start | bytes 417800 | tf_op jit(solution)/shard_map/ppermute | solution.py:45
  91.3 16.8 %collective-permute-start.17 = (bf16[192,2176]{1,0:T(8,128)(2,1)S(1)}, bf16[192,2176]{1,0:T(8,128)(2,1)S(1)}, u32[]{:S(2)}, u32[]{:S(2)}) collective-permute-start(bf16[192,2176]{1,0:T(8,128)(2,1)S(1)} %get-tuple-element.97), channel_id=1, source_target_pairs={{0,2},{1,3},{2,0},{3,1},{4,6},{5,7},{6,4},{7,5},{8,10},{9,11},{10,... | collective-permute-start | bytes 2506760 | tf_op jit(solution)/shard_map/ppermute | solution.py:35
  92.1 16.6 %collective-permute-start.18 = (bf16[192,2176]{1,0:T(8,128)(2,1)S(1)}, bf16[192,2176]{1,0:T(8,128)(2,1)}, u32[]{:S(2)}, u32[]{:S(2)}) collective-permute-start(bf16[192,2176]{1,0:T(8,128)(2,1)S(1)} %get-tuple-element.95), channel_id=1, source_target_pairs={{0,4},{4,0},{8,12},{12,8},{16,20},{20,16},{24,28},{28,24},{1,5},{5... | collective-permute-start | bytes 2506760 | tf_op jit(solution)/shard_map/ppermute | solution.py:35
  92.6 17.6 %collective-permute-start.19 = (bf16[128,2176]{1,0:T(8,128)(2,1)}, bf16[128,2176]{1,0:T(8,128)(2,1)}, u32[]{:S(2)}, u32[]{:S(2)}) collective-permute-start(bf16[128,2176]{1,0:T(8,128)(2,1)} %constant_dynamic-update-slice_fusion.refs_0_), channel_id=1, source_target_pairs={{0,1},{1,0},{2,3},{3,2},{4,5},{5,4},{6,7},{7,6},{8,9},{9,8},{10,11... | collective-permute-start | bytes 1671176 | tf_op jit(solution)/shard_map/ppermute | solution.py:35
  92.6 19.0 %collective-permute-start.20 = (bf16[128,2176]{1,0:T(8,128)(2,1)S(1)}, bf16[128,2176]{1,0:T(8,128)(2,1)}, u32[]{:S(2)}, u32[]{:S(2)}) collective-permute-start(bf16[128,2176]{1,0:T(8,128)(2,1)S(1)} %collective-permute-done.12.refs_1_), channel_id=1, source_target_pairs={{0,1},{1,0},{2,3},{3,2},{4,5},{5,4},{6,7},{7,6},{8,9},{9,8},{10,11... | collective-permute-start | bytes 1671176 | tf_op jit(solution)/shard_map/ppermute | solution.py:35
  108.2 12.6 %collective-permute-start.22 = (bf16[192,2176]{1,0:T(8,128)(2,1)S(1)}, bf16[192,2176]{1,0:T(8,128)(2,1)}, u32[]{:S(2)}, u32[]{:S(2)}) collective-permute-start(bf16[192,2176]{1,0:T(8,128)(2,1)S(1)} %collective-permute-done.17.refs_3_.refs_1_), channel_id=1, source_target_pairs={{0,1},{1,0},{2,3},{3,2},{4,5},{5,4},{6,7},{7,6},{8,9},{9,8},{10,11... | collective-permute-start | bytes 2506760 | tf_op jit(solution)/shard_map/ppermute | solution.py:35
  108.7 12.1 %collective-permute-start.23 = (bf16[192,2176]{1,0:T(8,128)(2,1)}, bf16[192,2176]{1,0:T(8,128)(2,1)}, u32[]{:S(2)}, u32[]{:S(2)}) collective-permute-start(bf16[192,2176]{1,0:T(8,128)(2,1)} %collective-permute-done.18.refs_4_.refs_2_), channel_id=1, source_target_pairs={{0,1},{1,0},{2,3},{3,2},{4,5},{5,4},{6,7},{7,6},{8,9},{9,8},{10,11... | collective-permute-start | bytes 2506760 | tf_op jit(solution)/shard_map/ppermute | solution.py:35
  108.7 12.0 %collective-permute-start.21 = (bf16[128,2176]{1,0:T(8,128)(2,1)S(1)}, bf16[128,2176]{1,0:T(8,128)(2,1)}, u32[]{:S(2)}, u32[]{:S(2)}) collective-permute-start(bf16[128,2176]{1,0:T(8,128)(2,1)S(1)} %collective-permute-done.13.refs_2_), channel_id=1, source_target_pairs={{0,1},{1,0},{2,3},{3,2},{4,5},{5,4},{6,7},{7,6},{8,9},{9,8},{10,11... | collective-permute-start | bytes 1671176 | tf_op jit(solution)/shard_map/ppermute | solution.py:35
  110.2 10.5 %collective-permute-start.24 = (bf16[64,2176]{1,0:T(8,128)(2,1)S(1)}, bf16[64,2176]{1,0:T(8,128)(2,1)S(1)}, u32[]{:S(2)}, u32[]{:S(2)}) collective-permute-start(bf16[64,2176]{1,0:T(8,128)(2,1)S(1)} %slice.149), channel_id=1, source_target_pairs={{0,2},{1,3},{2,0},{3,1},{4,6},{5,7},{6,4},{7,5},{8,10},{9,11},{10,... | collective-permute-start | bytes 835592 | tf_op jit(solution)/shard_map/ppermute | solution.py:35
  150.6 19.0 %collective-permute-start.28 = (bf16[128,2048]{1,0:T(8,128)(2,1)S(1)}, bf16[128,2048]{1,0:T(8,128)(2,1)S(1)}, u32[]{:S(2)}, u32[]{:S(2)}) collective-permute-start(bf16[128,2048]{1,0:T(8,128)(2,1)S(1)} %pad_maximum_fusion), channel_id=1, source_target_pairs={{0,4},{4,0},{8,12},{12,8},{16,20},{20,16},{24,28},{28,24},{1,5},{5... | collective-permute-start | bytes 1572872 | tf_op jit(solution)/shard_map/ppermute | solution.py:35
  151.3 18.3 %collective-permute-start.30 = (bf16[128,2048]{1,0:T(8,128)(2,1)S(1)}, bf16[128,2048]{1,0:T(8,128)(2,1)S(1)}, u32[]{:S(2)}, u32[]{:S(2)}) collective-permute-start(bf16[128,2048]{1,0:T(8,128)(2,1)S(1)} %pad_maximum_fusion.1), channel_id=1, source_target_pairs={{0,2},{1,3},{2,0},{3,1},{4,6},{5,7},{6,4},{7,5},{8,10},{9,11},{10,... | collective-permute-start | bytes 1572872 | tf_op jit(solution)/shard_map/ppermute | solution.py:35
  158.5 20.3 %collective-permute-start.39 = (bf16[128,2048]{1,0:T(8,128)(2,1)S(1)}, bf16[128,2048]{1,0:T(8,128)(2,1)S(1)}, u32[]{:S(2)}, u32[]{:S(2)}) collective-permute-start(bf16[128,2048]{1,0:T(8,128)(2,1)S(1)} %pad_maximum_fusion.2), channel_id=1, source_target_pairs={{0,4},{4,0},{8,12},{12,8},{16,20},{20,16},{24,28},{28,24},{1,5},{5... | collective-permute-start | bytes 1572872 | tf_op jit(solution)/shard_map/ppermute | solution.py:35
  160.1 18.7 %collective-permute-start.41 = (bf16[128,2048]{1,0:T(8,128)(2,1)S(1)}, bf16[128,2048]{1,0:T(8,128)(2,1)S(1)}, u32[]{:S(2)}, u32[]{:S(2)}) collective-permute-start(bf16[128,2048]{1,0:T(8,128)(2,1)S(1)} %pad_maximum_fusion.3), channel_id=1, source_target_pairs={{0,2},{1,3},{2,0},{3,1},{4,6},{5,7},{6,4},{7,5},{8,10},{9,11},{10,... | collective-permute-start | bytes 1572872 | tf_op jit(solution)/shard_map/ppermute | solution.py:35
  169.9 14.2 %collective-permute-start.31 = (bf16[32,2048]{1,0:T(8,128)(2,1)S(1)}, bf16[32,2048]{1,0:T(8,128)(2,1)S(1)}, u32[]{:S(2)}, u32[]{:S(2)}) collective-permute-start(bf16[32,2048]{1,0:T(8,128)(2,1)S(1)} %get-tuple-element.89), channel_id=1, source_target_pairs={{0,8},{4,12},{8,16},{12,20},{16,24},{20,28},{24,0},{28,4},{1,9},{5... | collective-permute-start | bytes 393224 | tf_op jit(solution)/shard_map/ppermute | solution.py:45
  172.9 14.1 %collective-permute-start.32 = (bf16[32,2048]{1,0:T(8,128)(2,1)S(1)}, bf16[32,2048]{1,0:T(8,128)(2,1)S(1)}, u32[]{:S(2)}, u32[]{:S(2)}) collective-permute-start(bf16[32,2048]{1,0:T(8,128)(2,1)S(1)} %get-tuple-element.91), channel_id=1, source_target_pairs={{0,16},{4,20},{8,24},{12,28},{16,0},{20,4},{24,8},{28,12},{1,17},{... | collective-permute-start | bytes 393224 | tf_op jit(solution)/shard_map/ppermute | solution.py:45
  174.9 12.1 %collective-permute-start.33 = (bf16[32,2048]{1,0:T(8,128)(2,1)S(1)}, bf16[32,2048]{1,0:T(8,128)(2,1)S(1)}, u32[]{:S(2)}, u32[]{:S(2)}) collective-permute-start(bf16[32,2048]{1,0:T(8,128)(2,1)S(1)} %get-tuple-element.90), channel_id=1, source_target_pairs={{0,24},{4,28},{8,0},{12,4},{16,8},{20,12},{24,16},{28,20},{1,25},{... | collective-permute-start | bytes 393224 | tf_op jit(solution)/shard_map/ppermute | solution.py:45
  (27 other events, 198.3 us)

commit v3 on v2

--- a/solution.py
+++ b/solution.py
@@ -12,6 +12,7 @@
 LANES = 128
 LOG2E = 1.4426950408889634
 CUTS = 2
+OWN_STEPS = 2
 rope_base = 10000.0
 norm_eps = 1e-06
 BF = jnp.bfloat16
@@ -53,38 +54,37 @@
     return [pltpu.with_memory_space_constraint(v, pltpu.HBM) for v in values]
 
 
-def project_kernel(t0, t1, t2, t3, gain, cosine, sine, w, q, k, v, normed):
-    part = pl.program_id(0)
-    rows = t0.shape[0]
-
-    @pl.when(part == 0)
-    def _():
-        for i, ref in enumerate((t0, t1, t2, t3)):
-            values = ref[...].astype(F32)
-            mean_sq = jnp.mean(values * values, axis=-1, keepdims=True)
-            scaled = values * lax.rsqrt(mean_sq + norm_eps) * gain[...]
-            normed[pl.ds(i * rows, rows), :] = scaled.astype(BF)
-
-    out = jnp.dot(normed[...], w[0], preferred_element_type=F32)
-
-    def rotated(ref):
+CHUNKS = 4
+
+
+def project_kernel(t0, t1, t2, t3, gain, cosine, sine, w_hbm, q, k, v, normed, w, sems):
+    rows, width = t0.shape
+    depth = width // CHUNKS
+
+    def load(part, i):
+        cut = pl.ds(i * depth, depth)
+        return pltpu.make_async_copy(w_hbm.at[part, cut], w.at[part, cut], sems.at[part, i])
+
+    for part in range(3):
+        for i in range(CHUNKS):
+            load(part, i).start()
+    for i, ref in enumerate((t0, t1, t2, t3)):
+        values = ref[...].astype(F32)
+        mean_sq = jnp.mean(values * values, axis=-1, keepdims=True)
+        scaled = values * lax.rsqrt(mean_sq + norm_eps) * gain[...]
+        normed[pl.ds(i * rows, rows), :] = scaled.astype(BF)
+    for part, ref in enumerate((q, k, v)):
+        for i in range(CHUNKS):
+            load(part, i).wait()
+        out = jnp.dot(normed[...], w[part], preferred_element_type=F32)
+        if part == 2:
+            ref[...] = out.astype(BF)
+            continue
         for h in range(out.shape[1] // HD):
             one = out[:, h * HD : (h + 1) * HD]
             turned = one * cosine[...] + pltpu.roll(one, HD // 2, 1) * sine[...]
             ref[:, h * HD : (h + 1) * HD] = turned.astype(BF)
 
-    @pl.when(part == 0)
-    def _():
-        rotated(q)
-
-    @pl.when(part == 1)
-    def _():
-        rotated(k)
-
-    @pl.when(part == 2)
-    def _():
-        v[...] = out.astype(BF)
-
 
 def project(blocks, gain, cosine, sine, w):
     rows, width = blocks[0].shape
@@ -92,13 +92,14 @@
     shape = jax.ShapeDtypeStruct((total, local), BF)
     return pl.pallas_call(
         project_kernel,
-        grid=(3,),
         out_shape=(shape,) * 3,
-        in_specs=[whole((rows, width))] * 4
-        + [whole((1, width)), whole((total, HD)), whole((total, HD))]
-        + [pl.BlockSpec((1, width, local), lambda i: (i, 0, 0))],
-        out_specs=(whole((total, local)),) * 3,
-        scratch_shapes=[pltpu.VMEM((total, width), BF)],
+        in_specs=[pl.BlockSpec(memory_space=pltpu.VMEM)] * 7 + [pl.BlockSpec(memory_space=pltpu.HBM)],
+        out_specs=(pl.BlockSpec(memory_space=pltpu.VMEM),) * 3,
+        scratch_shapes=[
+            pltpu.VMEM((total, width), BF),
+            pltpu.VMEM(w.shape, BF),
+            pltpu.SemaphoreType.DMA((3, CHUNKS)),
+        ],
         compiler_params=params(20),
         cost_estimate=cost(6 * total * width * local, 6 * width * local),
         name="project",
@@ -116,80 +117,79 @@
         one = scores_of(q, keys)
         scores.append(one if allowed is None else jnp.where(allowed, one, -1e30))
     top = functools.reduce(jnp.maximum, [jnp.max(s, axis=-1, keepdims=True) for s in scores])
-    total, mixed = 0.0, 0.0
+    mixed = 0.0
     for s, (_, values, _) in zip(scores, pieces):
-        expo = jnp.exp2((s - top) * (scale * LOG2E))
-        total = total + jnp.sum(expo, axis=-1, keepdims=True)
-        mixed = mixed + jnp.dot(expo.astype(BF), values, preferred_element_type=F32)
-    return mixed / total, top * scale + jnp.log(total)
+        expo = jnp.exp2((s - top) * (scale * LOG2E)).astype(BF)
+        wide = jnp.concatenate([values, jnp.ones(values.shape, BF)], axis=1)
+        mixed = mixed + jnp.dot(expo, wide, preferred_element_type=F32)
+    total = mixed[:, HD:]
+    return mixed[:, :HD] / total, top * scale + jnp.log(total[:, :1])
+
+
+def cached(kv_here, kv_there, cols):
+    return [
+        (kv_here[0, :, 0, cols], kv_here[0, :, 1, cols], None),
+        (kv_there[:, 0, cols], kv_there[:, 1, cols], None),
+    ]
 
 
 def own_kernel(group, q, kv_here, kv_there, k, v, seg_row, seg_col, out, stats):
-    h = pl.program_id(0)
+    step = pl.program_id(0)
     same = seg_row[...] == seg_col[...]
-    mixed, level = attend_pieces(
-        q[...],
-        [
-            (kv_here[0, :, 0, :], kv_here[0, :, 1, :], None),
-            (kv_there[:, 0, :], kv_there[:, 1, :], None),
-            (k[...], v[...], same),
-        ],
-    )
-    out[...] = mixed
     lane = lax.broadcasted_iota(jnp.int32, stats.shape, 1)
-
-    @pl.when(h == 0)
+    heads = q.shape[1] // HD
+
+    @pl.when(step == 0)
     def _():
         stats[...] = jnp.zeros_like(stats)
 
-    stats[...] = jnp.where(lane == h, level, stats[...])
+    levels = stats[...]
+    for h in range(heads):
+        cols = slice(h * HD, (h + 1) * HD)
+        pieces = cached(kv_here, kv_there, cols) + [(k[:, cols], v[:, cols], same)]
+        mixed, level = attend_pieces(q[:, cols], pieces)
+        out[:, cols] = mixed
+        levels = jnp.where(lane == step * heads + h, level, levels)
+    stats[...] = levels
 
 
 def guest_kernel(group, q, kv_here, kv_there, out):
-    h = pl.program_id(0)
     local = out.shape[1] - LANES
-    mixed, level = attend_pieces(
-        q[...],
-        [
-            (kv_here[0, :, 0, :], kv_here[0, :, 1, :], None),
-            (kv_there[:, 0, :], kv_there[:, 1, :], None),
-        ],
-    )
-    out[:, pl.ds(pl.multiple_of(h * HD, HD), HD)] = mixed.astype(BF)
     lane = lax.broadcasted_iota(jnp.int32, (out.shape[0], LANES), 1)
-
-    @pl.when(h == 0)
-    def _():
-        out[:, local:] = jnp.zeros((out.shape[0], LANES), BF)
-
-    tail = out[:, local:].astype(F32)
-    rest = jnp.broadcast_to(level, tail.shape)
-    for i in range(3):
-        piece = rest.astype(BF).astype(F32)
-        tail = jnp.where(lane == 3 * h + i, piece, tail)
-        rest = rest - piece
+    tail = jnp.zeros(lane.shape, F32)
+    for h in range(local // HD):
+        cols = slice(h * HD, (h + 1) * HD)
+        mixed, level = attend_pieces(q[:, cols], cached(kv_here, kv_there, cols))
+        out[:, cols] = mixed.astype(BF)
+        rest = jnp.broadcast_to(level, tail.shape)
+        for i in range(3):
+            piece = rest.astype(BF).astype(F32)
+            tail = jnp.where(lane == 3 * h + i, piece, tail)
+            rest = rest - piece
     out[:, local:] = tail.astype(BF)
 
 
-def kv_specs(depth, heads):
+def kv_specs(depth, local, steps):
+    some = local // steps
     return [
-        pl.BlockSpec((1, depth, 2, HD), lambda i, g: (0, 0, 0, g[0] * heads + i)),
-        pl.BlockSpec((depth, 2, HD), lambda i, g: (0, 0, i)),
+        pl.BlockSpec((1, depth, 2, some), lambda i, g: (0, 0, 0, g[0] * steps + i)),
+        pl.BlockSpec((depth, 2, some), lambda i, g: (0, 0, i)),
     ]
 
 
 def attend_own(group, q, kv, kv_there, k, v, seg_row, seg_col):
     rows, local = q.shape
     heads, depth = local // HD, kv.shape[1]
-    block = pl.BlockSpec((rows, HD), lambda i, g: (0, i))
+    steps = OWN_STEPS
+    block = pl.BlockSpec((rows, local // steps), lambda i, g: (0, i))
     keys = 2 * depth + rows
     return pl.pallas_call(
         own_kernel,
         grid_spec=pltpu.PrefetchScalarGridSpec(
             num_scalar_prefetch=1,
-            grid=(heads,),
+            grid=(steps,),
             in_specs=[block]
-            + kv_specs(depth, heads)
+            + kv_specs(depth, local, steps)
             + [block, block, whole((rows, 1)), whole((1, rows))],
             out_specs=(block, whole((rows, LANES))),
         ),
@@ -211,8 +211,8 @@
         guest_kernel,
         grid_spec=pltpu.PrefetchScalarGridSpec(
             num_scalar_prefetch=1,
-            grid=(heads,),
-            in_specs=[pl.BlockSpec((rows, HD), lambda i, g: (0, i))] + kv_specs(depth, heads),
+            grid=(1,),
+            in_specs=[whole((rows, local))] + kv_specs(depth, local, 1),
             out_specs=whole((rows, local + LANES)),
         ),
         out_shape=jax.ShapeDtypeStruct((rows, local + LANES), BF),
@@ -312,46 +312,28 @@
     )(me, tokens, keep, arrived, gain, w_router, routes)
 
 
-def expert_kernel(sizes, starts, tile, fetch, group, *refs):
+def expert_kernel(sizes, tile, group, *refs):
     count = len(sizes)
-    pieces, sources, out = refs[:count], refs[count : count + 3], refs[count + 3]
-    if fetch:
-        *on_chip, held, sems, loads = refs[count + 4 :]
-    else:
-        on_chip, (held, sems) = sources, refs[count + 4 :]
-    gate, up, down = on_chip
+    pieces, (gate, up, down) = refs[:count], refs[count : count + 3]
+    outs, (held, sems) = refs[count + 3 : -2], refs[-2:]
     experts, width = gate.shape[0], gate.shape[1]
     step = pl.program_id(0)
 
-    def load(e, i):
-        return pltpu.make_async_copy(sources[i].at[e], on_chip[i].at[e], loads.at[e, i])
-
-    def at_first(act):
-        if fetch:
-            pl.when(step == 0)(act)
-
-    def bring():
+    @pl.when(step == 0)
+    def _():
         start = 0
-        for ref, first, size in zip(pieces, starts, sizes):
+        for ref, size in zip(pieces, sizes):
             done = 0
             while done < size:
                 take = min(size - done, tile - (start + done) % tile)
                 pltpu.make_async_copy(
-                    ref.at[pl.ds(first + done, take)],
+                    ref.at[pl.ds(done, take)],
                     held.at[pl.ds(start + done, take)],
                     sems.at[(start + done) // tile],
                 ).start()
                 done += take
             start += size
 
-    if fetch:
-
-        @pl.when(step == 0)
-        def _():
-            load(0, 0).start()
-            load(0, 1).start()
-
-    pl.when(step == 0)(bring)
     here = pl.ds(pl.multiple_of(step * tile, tile), tile)
     pltpu.make_async_copy(held.at[here], held.at[here], sems.at[step]).wait()
     rows = held[here, :width]
@@ -362,64 +344,43 @@
         index = group[0] * experts + e
         hit = (lane == index) | (lane == index + LANES // 2)
         share = jnp.sum(jnp.where(hit, tail, 0.0), axis=1, keepdims=True)
-
-        def before_gate(e=e):
-            load(e, 0).wait()
-            load(e, 2).start()
-            if e + 1 < experts:
-                load(e + 1, 0).start()
-
-        def before_up(e=e):
-            load(e, 1).wait()
-            if e + 1 < experts:
-                load(e + 1, 1).start()
-
-        at_first(before_gate)
         g = jnp.dot(rows, gate[e], preferred_element_type=F32)
-        at_first(before_up)
         u = jnp.dot(rows, up[e], preferred_element_type=F32)
         act = (g * jax.nn.sigmoid(g) * u * share).astype(BF)
-        at_first(lambda e=e: load(e, 2).wait())
         one = jnp.dot(act, down[e], preferred_element_type=F32)
         result = one if result is None else result + one
-    out[...] = result.astype(BF)
-
-
-def expert_call(group, pieces, weights, tile, fetch):
+    done = 0
+    for out in outs:
+        out[...] = result[done : done + out.shape[0]].astype(BF)
+        done += out.shape[0]
+
+
+def expert_part(group, pieces, weights, outs=1, most=512):
     gate = weights[0]
-    sizes = [size for _, _, size in pieces]
-    starts = [start for _, start, _ in pieces]
+    sizes = [p.shape[0] for p in pieces]
     total = sum(sizes)
-    wide, width = pieces[0][0].shape[1], gate.shape[1]
+    tile = total if outs > 1 else next(t for t in range(most, 0, -64) if total % t == 0)
+    wide, width = pieces[0].shape[1], gate.shape[1]
+    some = tile // outs
     flops = 6 * total * gate.shape[0] * width * gate.shape[2]
-    on_chip = pl.BlockSpec(memory_space=pltpu.VMEM)
-    shape = jax.ShapeDtypeStruct((total, width), BF)
-    spec = pl.BlockSpec((tile, width), lambda i, g: (i, 0))
-    scratch = [pltpu.VMEM((total, wide), BF), pltpu.SemaphoreType.DMA((total // tile,))]
-    return pl.pallas_call(
-        functools.partial(expert_kernel, sizes, starts, tile, fetch),
+    return pl.pallas_call(
+        functools.partial(expert_kernel, sizes, tile),
         grid_spec=pltpu.PrefetchScalarGridSpec(
             num_scalar_prefetch=1,
             grid=(total // tile,),
             in_specs=[pl.BlockSpec(memory_space=pl.ANY)] * len(pieces)
-            + [pl.BlockSpec(memory_space=pltpu.HBM) if fetch else on_chip] * 3,
-            out_specs=(spec,) + (on_chip,) * 3 if fetch else spec,
-            scratch_shapes=scratch
-            + ([pltpu.SemaphoreType.DMA((gate.shape[0], 3))] if fetch else []),
+            + [pl.BlockSpec(memory_space=pltpu.VMEM)] * 3,
+            out_specs=(pl.BlockSpec((some, width), lambda i, g: (i, 0)),) * outs,
+            scratch_shapes=[
+                pltpu.VMEM((total, wide), BF),
+                pltpu.SemaphoreType.DMA((total // tile,)),
+            ],
         ),
-        out_shape=(shape,) + tuple(jax.ShapeDtypeStruct(w.shape, w.dtype) for w in weights)
-        if fetch
-        else shape,
-        compiler_params=params(20 + (total >> 7)),
+        out_shape=(jax.ShapeDtypeStruct((total // outs, width), BF),) * outs,
+        compiler_params=params(20 + (total >> 6)),
         cost_estimate=cost(flops, 4 * total * width + 6 * gate.size),
         name="experts",
-    )(group, *[array for array, _, _ in pieces], *weights)
-
-
-def expert_part(group, pieces, weights, fetch=False, most=512):
-    total = sum(size for _, _, size in pieces)
-    tile = next(t for t in range(most, 0, -64) if total % t == 0)
-    return expert_call(group, pieces, weights, tile, fetch)
+    )(group, *pieces, *weights)
 
 
 def add_bf(*values):
@@ -434,24 +395,55 @@
     return jnp.concatenate(values, axis=0)
 
 
-def sections(total):
-    n = total.shape[0] // 4
-    return [total[i * n : (i + 1) * n] for i in range(4)]
-
-
-def reduce_corner(total):
-    corner = sections(total)[3]
-    half = corner.shape[0] // 2
-    return move_y(corner[:half]), move_x(corner[half:])
+def reduce_corner(kept, sent):
+    total = add_bf(kept, move_c(sent))
+    half = total.shape[0] // 2
+    return move_y(total[:half]), move_x(total[half:])
 
 
 def reduce_rest(total, got):
-    here, by_y, by_x, _ = sections(total)
-    half = here.shape[0] // 2
+    n = total.shape[0] // 3
+    half = n // 2
+    rows = n // (lax.axis_size("tok") // 2)
+    here, by_y, by_x = (total[i * n : (i + 1) * n] for i in range(3))
     to_x = join_rows(add_bf(by_x[:half], got[0]), by_x[half:])
     to_y = join_rows(by_y[:half], add_bf(by_y[half:], got[1]))
     got_x, got_y = move_x(to_x), move_y(to_y)
-    return functools.reduce(jnp.add, [v.astype(F32) for v in (here, got_x, got_y)])
+    total = functools.reduce(jnp.add, [v.astype(F32) for v in (here, got_x, got_y)])
+    return total[:rows], total[rows:].astype(BF)
+
+
+def hold_kernel(count, *refs):
+    sources, targets, sems = refs[:count], refs[count : 2 * count], refs[-1]
+    copies = []
+    for i in range(count):
+        some = sources[i].shape[1] // sems.shape[2]
+        for e in range(sources[i].shape[0]):
+            for j in range(sems.shape[2]):
+                rows = pl.ds(j * some, some)
+                copies.append(
+                    pltpu.make_async_copy(
+                        sources[i].at[e, rows], targets[i].at[e, rows], sems.at[i, e, j]
+                    )
+                )
+    for copy in copies:
+        copy.start()
+    for copy in copies:
+        copy.wait()
+
+
+def hold(*values):
+    count = len(values)
+    return pl.pallas_call(
+        functools.partial(hold_kernel, count),
+        out_shape=[jax.ShapeDtypeStruct(v.shape, v.dtype) for v in values],
+        in_specs=[pl.BlockSpec(memory_space=pltpu.HBM)] * count,
+        out_specs=[pl.BlockSpec(memory_space=pltpu.VMEM)] * count,
+        scratch_shapes=[pltpu.SemaphoreType.DMA((count, values[0].shape[0], 2))],
+        compiler_params=params(1),
+        cost_estimate=cost(0, sum(4 * v.size for v in values)),
+        name="hold",
+    )(*in_hbm(*values))
 
 
 def mixture(group, resid, messages, weights):
@@ -463,43 +455,44 @@
     first_z = [from_z(first, k) for k in range(1, depth)]
     second = after(second, *first_z)
     second_z = [from_z(second, k) for k in range(1, depth)]
-
     here_a = join_rows(first, *first_z)
     here_b = join_rows(second, *second_z)
     y_a, x_a = move_y(here_a), move_x(here_a)
-    from_y = move_y(join_rows(x_a[:half], here_b))
-    from_x = move_x(join_rows(y_a[half:], here_b))
-    corner_y, corner_x = move_y(from_x[half : 2 * half]), move_x(from_y[2 * half :])
-
-    def pieces_of(arrays, skip):
-        here, by_y, by_x, by_corner_y, by_corner_x = arrays
-        pieces = [(here, 0, n), (by_y, skip, n), (by_x, skip, n)]
-        return pieces + [(by_corner_y, 0, half), (by_corner_x, 0, half)]
-
-    there_y, there_x = move_c(from_y), move_c(from_x)
-    theirs_a = [move_c(v) for v in (here_a, y_a, x_a)] + [there_y, there_x]
-    theirs_b = [move_c(here_b), there_y, there_x, move_c(corner_y), move_c(corner_x)]
-
-    own_a = [here_a, y_a, x_a, from_y, from_x]
-    own_b = [here_b, from_y, from_x, corner_y, corner_x]
-    kept_a, *held = expert_part(group, pieces_of(own_a, 0), in_hbm(*weights), True)
-    theirs_a = after(theirs_a, kept_a, corner_y, corner_x)
-    sent_a = expert_part(group, pieces_of(theirs_a, 0), held)
-    kept_b = expert_part(group, pieces_of(after(own_b, sent_a), half), held)
+    held = hold(*after(weights, y_a, x_a))
+    corner_a = [move_y(x_a[:half]), move_x(y_a[half:])]
+    main_a = [here_a, y_a, x_a]
+    their_main_a, their_corner_a = ([move_c(v) for v in values] for values in (main_a, corner_a))
+    (sent_a,) = expert_part(group, their_main_a, held)
+    leaving_b = after(here_b, *corner_a)
+    y_b, x_b = move_y(leaving_b), move_x(leaving_b)
+    (kept_a,) = expert_part(group, after(main_a, sent_a), held)
+    sent_corner, kept_corner = expert_part(
+        group, after(their_corner_a, kept_a) + corner_a, held, 2
+    )
+    got_a = reduce_corner(after(kept_corner, y_b, x_b), sent_corner)
+
+    corner_b = [move_y(x_b[:half]), move_x(y_b[half:])]
+    main_b = [here_b, y_b, x_b]
+    their_main_b = [move_c(v) for v in main_b]
     chip_a = add_bf(kept_a, move_c(sent_a))
-    got_a = reduce_corner(chip_a)
-    sent_b = expert_part(group, pieces_of(after(theirs_b, chip_a, kept_b), half), held)
+    (sent_b,) = expert_part(group, after(their_main_b, sent_corner), held)
+    (kept_b,) = expert_part(group, after(main_b, sent_b), held)
+    corner_b = after(corner_b, kept_b)
+    their_corner_b = [move_c(v) for v in corner_b]
+    sent_corner, kept_corner = expert_part(group, their_corner_b + corner_b, held, 2)
+    got_b = reduce_corner(kept_corner, sent_corner)
     sums_a = reduce_rest(chip_a, got_a)
     chip_b = add_bf(kept_b, move_c(sent_b))
-    sums_b = reduce_rest(chip_b, reduce_corner(chip_b))
-
-    outs = []
-    for i, sums in enumerate((sums_a, sums_b)):
-        total = resid[i * rows : (i + 1) * rows] + sums[:rows]
-        for k in range(1, depth):
-            part = sums[k * rows : (k + 1) * rows].astype(BF)
-            total = total + to_z(part, k).astype(F32)
-        outs.append(total.astype(BF))
+    sums_b = reduce_rest(chip_b, got_b)
+
+    outs, landed = [], []
+    for i, (own, rest) in enumerate((sums_a, sums_b)):
+        total = resid[i * rows : (i + 1) * rows] + own
+        if landed:
+            rest = after(rest, *landed)
+        parts = [rest[(k - 1) * rows : k * rows] for k in range(1, depth)]
+        landed = [to_z(part, k) for k, part in zip(range(1, depth), parts)]
+        outs.append(functools.reduce(jnp.add, [v.astype(F32) for v in landed], total).astype(BF))
     return jnp.concatenate(outs, axis=0)
 
 

time: 193 us -> 177 us (0.917)
  Pallas kernels: 48 us -> 40.2 us
  starting transfers between devices: 51 us -> 43.7 us
  waiting for transfers between devices: 78.1 us -> 81.9 us
  local copies, waits for them, and re-layouts: 8.94 us -> 5.23 us
    ppermute x12, starting transfers between devices: 27.2 us -> 17.6 us  [from_z(): lax.ppermute(value, 'tok', [(i, (i - 2 * k) % size) for i in range(size)])]
    ppermute x12, waiting for transfers between devices: 15 us -> 23.8 us  [from_z(): lax.ppermute(value, 'tok', [(i, (i - 2 * k) % size) for i in range(size)])]
    pallas_call x5 -> x8, Pallas kernels: 28.1 us -> 23 us  [the longest x6 16 us: expert_part(): pl.pallas_call(functools.partial(expert_kernel, sizes, tile), grid_spec=p...]
    ppermute x33 -> x39, waiting for transfers between devices: 63.1 us -> 58 us  [swap(): return lax.ppermute(value, axis, [(i, i ^ bit) for i in range(size)])]
    ppermute x33 -> x39, starting transfers between devices: 23.8 us -> 26.1 us  [swap(): return lax.ppermute(value, axis, [(i, i ^ bit) for i in range(size)])]
    unnamed x22 -> x20, local copies, waits for them, and re-layouts: 2.62 us -> 0.51 us
  transfers between devices with their start and end apart: 45 -> 51, of which waited for: 18 -> 24; matrix products, arithmetic and copies ran while one was open for 6% -> 6% of each run, Pallas kernels for 19% -> 21%
where the time goes in v3:
time: 177 us
  waiting for transfers between devices  81.9 us (46%)
  starting transfers between devices  43.7 us (25%)
  Pallas kernels  40.2 us (23%)
  other arithmetic  5.66 us (3%)
  local copies, waits for them, and re-layouts  5.23 us (3%)
    ppermute x39, waiting for transfers between devices, swap(): return lax.ppermute(value, axis, [(i, i ^ bit) for i in range(size)])  58 us
    ppermute x39, starting transfers between devices, swap(): return lax.ppermute(value, axis, [(i, i ^ bit) for i in range(size)])  26.1 us
    ppermute x12, waiting for transfers between devices, from_z(): lax.ppermute(value, 'tok', [(i, (i - 2 * k) % size) for i in range(size)])  23.8 us
    ppermute x12, starting transfers between devices, from_z(): lax.ppermute(value, 'tok', [(i, (i - 2 * k) % size) for i in range(size)])  17.6 us
    pallas_call x6, Pallas kernels, expert_part(): pl.pallas_call(functools.partial(expert_kernel, sizes, tile), grid_spec=p...  16 us
    pallas_call x1, Pallas kernels, attend_own(): pl.pallas_call(own_kernel, grid_spec=pltpu.PrefetchScalarGridSpec(num_sca...  7.84 us
    pallas_call x1, Pallas kernels, attend_guest(): pl.pallas_call(guest_kernel, grid_spec=pltpu.PrefetchScalarGridSpec(num_s...  7.05 us
    pallas_call x1, Pallas kernels, project(): pl.pallas_call(project_kernel, out_shape=(shape,) * 3, in_specs=[pl.Block...  4.13 us
  transfers between devices with their start and end apart: 51, of which 24 were waited for; matrix products, arithmetic and copies ran while one was open for 6% of the time, Pallas kernels for 21%

profile of v3, /device:TPU:0, one launch (start us, length us, event | category | flops | bytes accessed | tf_op | source)
XLA Modules:
  0.0 177.2 jit_solution(2426650952326204688)
XLA Ops:
  0.5 2.5 %collective-permute-start.1 = (bf16[64,2048]{1,0:T(8,128)(2,1)}, bf16[64,2048]{1,0:T(8,128)(2,1)S(1)}, u32[]{:S(2)}, u32[]{:S(2)}) collective-permute-start(bf16[64,2048]{1,0:T(8,128)(2,1)} %tokens.1), channel_id=1, source_target_pairs={{0,2},{1,3},{2,0},{3,1},{4,6},{5,7},{6,4},{7,5},{8,10},{9,11},{10,... | collective-permute-start | bytes 786440 | tf_op jit(solution)/shard_map/ppermute | solution.py:36
  4.7 4.1 %dynamic-slice_bitcast_fusion = (bf16[512,2,512]{2,1,0:T(2,128)(2,1)S(1)}, bf16[512,2,512]{2,1,0:T(2,128)(2,1)}) fusion(bf16[1,512,2,2048]{3,2,1,0:T(2,128)(2,1)} %kv_here.3, s32[]{:T(128)S(6)} %select_n.7, s32[]{:T(128)S(6)} %select_n.6), kind=kLoop, calls=%fused_computation.7 | loop fusion | bytes 4194312 | tf_op jit(solution)/shard_map/dynamic_slice | solution.py:527
  12.2 4.1 %project.1 = (bf16[256,512]{1,0:T(8,128)(2,1)S(1)}, bf16[256,512]{1,0:T(8,128)(2,1)S(1)}, bf16[256,512]{1,0:T(8,128)(2,1)S(1)}) custom-call(bf16[64,2048]{1,0:T(8,128)(2,1)S(1)} %copy-done.1, bf16[64,2048]{1,0:T(8,128)(2,1)S(1)} %collective-permute-done.t1, bf16[64,2048]{1,0:T(8,128)(2,1)S(1)} %collective-permute-done.1.t2, ...), custom_call_target="tpu_custom_call" | custom-call | flops 1610612736 | bytes 6291456 | tf_op jit(solution)/shard_map/project/pallas_call | solution.py:93
  17.7 7.2 %collective-permute-done.4.q = bf16[256,512]{1,0:T(8,128)(2,1)S(1)} collective-permute-done((bf16[256,512]{1,0:T(8,128)(2,1)S(1)}, bf16[256,512]{1,0:T(8,128)(2,1)S(1)}, u32[]{:S(2)}, u32[]{:S(2)}) %collective-permute-start.4) | collective-permute-done | bytes 262176 | tf_op jit(solution)/shard_map/ppermute | solution.py:36
  24.9 7.1 %attend_guest.1 = bf16[256,640]{1,0:T(8,128)(2,1)S(1)} custom-call(s32[1]{0:T(128)S(6)} %xor.22.group, bf16[256,512]{1,0:T(8,128)(2,1)S(1)} %collective-permute-done.4.q, bf16[1,512,2,2048]{3,2,1,0:T(2,128)(2,1)} %kv_here.3, bf16[512,2,512]{2,1,0:T(2,128)(2,1)S(1)} %collective-permute-done.5.kv_there), custom_call_target="tpu_custom_call" | custom-call | flops 536870912 | bytes 2097152 | tf_op jit(solution)/shard_map/attend_guest/pallas_call | solution.py:210
  33.6 7.8 %attend_own.1 = (f32[256,512]{1,0:T(8,128)S(1)}, f32[256,128]{1,0:T(8,128)S(1)}) custom-call(s32[1]{0:T(128)} %bitcast.group.me, bf16[256,512]{1,0:T(8,128)(2,1)S(1)} %get-tuple-element.43.q, bf16[1,512,2,2048]{3,2,1,0:T(2,128)(2,1)} %kv_here.3, bf16[512,2,512]{2,1,0:T(2,128)(2,1)S(1)} %collective-permute-done.3.kv_there, ...), custom_call_target="tpu_custom_call" | custom-call | flops 671088640 | bytes 2621440 | tf_op jit(solution)/shard_map/attend_own/pallas_call | solution.py:186
  47.0 6.7 %collective-permute-done.8.arrived = bf16[64,2048]{1,0:T(8,128)(2,1)S(1)} collective-permute-done((bf16[64,2048]{1,0:T(8,128)(2,1)S(1)}, bf16[64,2048]{1,0:T(8,128)(2,1)S(1)}, u32[]{:S(2)}, u32[]{:S(2)}) %collective-permute-start.8) | collective-permute-done | bytes 262176 | tf_op jit(solution)/shard_map/ppermute | solution.py:36
  54.3 4.1 %collective-permute-start.9 = (bf16[32,2176]{1,0:T(8,128)(2,1)S(1)}, bf16[32,2176]{1,0:T(8,128)(2,1)S(1)}, u32[]{:S(2)}, u32[]{:S(2)}) collective-permute-start(bf16[32,2176]{1,0:T(8,128)(2,1)S(1)} %get-tuple-element.52), channel_id=1, source_target_pairs={{0,24},{4,28},{8,0},{12,4},{16,8},{20,12},{24,16},{28,20},{1,25},{... | collective-permute-start | bytes 417800 | tf_op jit(solution)/shard_map/ppermute | solution.py:46
  59.6 3.0 %collective-permute-done.9 = bf16[32,2176]{1,0:T(8,128)(2,1)S(1)} collective-permute-done((bf16[32,2176]{1,0:T(8,128)(2,1)S(1)}, bf16[32,2176]{1,0:T(8,128)(2,1)S(1)}, u32[]{:S(2)}, u32[]{:S(2)}) %collective-permute-start.9) | collective-permute-done | bytes 139296 | tf_op jit(solution)/shard_map/ppermute | solution.py:46
  62.6 7.3 %collective-permute-done.10 = bf16[32,2176]{1,0:T(8,128)(2,1)S(1)} collective-permute-done((bf16[32,2176]{1,0:T(8,128)(2,1)S(1)}, bf16[32,2176]{1,0:T(8,128)(2,1)S(1)}, u32[]{:S(2)}, u32[]{:S(2)}) %collective-permute-start.10) | collective-permute-done | bytes 139296 | tf_op jit(solution)/shard_map/ppermute | solution.py:46
  75.4 3.4 %collective-permute-done.22 = bf16[32,2176]{1,0:T(8,128)(2,1)S(1)} collective-permute-done((bf16[32,2176]{1,0:T(8,128)(2,1)S(1)}, bf16[32,2176]{1,0:T(8,128)(2,1)S(1)}, u32[]{:S(2)}, u32[]{:S(2)}) %collective-permute-start.22) | collective-permute-done | bytes 139296 | tf_op jit(solution)/shard_map/ppermute | solution.py:46
  80.4 4.8 %collective-permute-done.12.refs_1_ = bf16[128,2176]{1,0:T(8,128)(2,1)S(1)} collective-permute-done((bf16[128,2176]{1,0:T(8,128)(2,1)S(1)}, bf16[128,2176]{1,0:T(8,128)(2,1)S(1)}, u32[]{:S(2)}, u32[]{:S(2)}) %collective-permute-start.12) | collective-permute-done | bytes 557088 | tf_op jit(solution)/shard_map/ppermute | solution.py:36
  85.7 2.9 %collective-permute-done.23 = bf16[32,2176]{1,0:T(8,128)(2,1)S(1)} collective-permute-done((bf16[32,2176]{1,0:T(8,128)(2,1)S(1)}, bf16[32,2176]{1,0:T(8,128)(2,1)S(1)}, u32[]{:S(2)}, u32[]{:S(2)}) %collective-permute-start.23) | collective-permute-done | bytes 139296 | tf_op jit(solution)/shard_map/ppermute | solution.py:46
  90.2 2.9 %hold.1 = (bf16[2,2048,256]{2,1,0:T(8,128)(2,1)S(1)}, bf16[2,2048,256]{2,1,0:T(8,128)(2,1)S(1)}, bf16[2,256,2048]{2,1,0:T(8,128)(2,1)S(1)}) custom-call(bf16[2,2048,256]{2,1,0:T(8,128)(2,1)} %refs_0_, bf16[2,2048,256]{2,1,0:T(8,128)(2,1)} %refs_1_, bf16[2,256,2048]{2,1,0:T(8,128)(2,1)} %refs_2_), custom_call_target="tpu_custom_call" | custom-call | bytes 12582912 | tf_op jit(solution)/shard_map/hold/pallas_call | solution.py:437
  93.1 4.1 %collective-permute-done.18.refs_2_ = bf16[64,2176]{1,0:T(8,128)(2,1)S(1)} collective-permute-done((bf16[64,2176]{1,0:T(8,128)(2,1)S(1)}, bf16[64,2176]{1,0:T(8,128)(2,1)S(1)}, u32[]{:S(2)}, u32[]{:S(2)}) %collective-permute-start.18) | collective-permute-done | bytes 278560 | tf_op jit(solution)/shard_map/ppermute | solution.py:36
  100.1 2.9 %experts.6 = bf16[384,2048]{1,0:T(8,128)(2,1)S(1)} custom-call(s32[1]{0:T(128)} %bitcast.11.group, bf16[128,2176]{1,0:T(8,128)(2,1)S(1)} %collective-permute-done.14.refs_0_, bf16[128,2176]{1,0:T(8,128)(2,1)S(1)} %collective-permute-done.15.refs_1_, bf16[128,2176]{1,0:T(8,128)(2,1)S(1)} %collective-permute-done.16.refs_2_, ...), custom_call_target="tpu_custom_call" | custom-call | flops 2415919104 | bytes 9437184 | tf_op jit(solution)/shard_map/experts/pallas_call | solution.py:366
  103.0 2.9 %experts.7 = bf16[384,2048]{1,0:T(8,128)(2,1)S(1)} custom-call(s32[1]{0:T(128)} %bitcast.11.group, bf16[128,2176]{1,0:T(8,128)(2,1)S(1)} %constant_dynamic-update-slice_fusion.refs_0_, bf16[128,2176]{1,0:T(8,128)(2,1)S(1)} %collective-permute-done.12.refs_1_, bf16[128,2176]{1,0:T(8,128)(2,1)S(1)} %collective-permute-done.13.refs_2_, ...), custom_call_target="tpu_custom_call" | custom-call | flops 2415919104 | bytes 9437184 | tf_op jit(solution)/shard_map/experts/pallas_call | solution.py:366
  108.6 2.6 %collective-permute-done.25.refs_1_ = bf16[128,2176]{1,0:T(8,128)(2,1)S(1)} collective-permute-done((bf16[128,2176]{1,0:T(8,128)(2,1)S(1)}, bf16[128,2176]{1,0:T(8,128)(2,1)S(1)}, u32[]{:S(2)}, u32[]{:S(2)}) %collective-permute-start.25) | collective-permute-done | bytes 557088 | tf_op jit(solution)/shard_map/ppermute | solution.py:36
  114.3 2.9 %experts.9 = bf16[384,2048]{1,0:T(8,128)(2,1)S(1)} custom-call(s32[1]{0:T(128)} %bitcast.11.group, bf16[128,2176]{1,0:T(8,128)(2,1)S(1)} %collective-permute-done.35.refs_0_, bf16[128,2176]{1,0:T(8,128)(2,1)S(1)} %collective-permute-done.36.refs_1_, bf16[128,2176]{1,0:T(8,128)(2,1)S(1)} %collective-permute-done.37.refs_2_, ...), custom_call_target="tpu_custom_call" | custom-call | flops 2415919104 | bytes 9437184 | tf_op jit(solution)/shard_map/experts/pallas_call | solution.py:366
  117.2 2.9 %experts.10 = bf16[384,2048]{1,0:T(8,128)(2,1)S(1)} custom-call(s32[1]{0:T(128)} %bitcast.11.group, bf16[128,2176]{1,0:T(8,128)(2,1)S(1)} %constant_dynamic-update-slice_fusion.4.refs_0_, bf16[128,2176]{1,0:T(8,128)(2,1)S(1)} %collective-permute-done.25.refs_1_, bf16[128,2176]{1,0:T(8,128)(2,1)S(1)} %collective-permute-done.26.refs_2_, ...), custom_call_target="tpu_custom_call" | custom-call | flops 2415919104 | bytes 9437184 | tf_op jit(solution)/shard_map/experts/pallas_call | solution.py:366
  127.9 3.0 %collective-permute-done.28 = bf16[64,2048]{1,0:T(8,128)(2,1)S(1)} collective-permute-done((bf16[64,2048]{1,0:T(8,128)(2,1)S(1)}, bf16[64,2048]{1,0:T(8,128)(2,1)S(1)}, u32[]{:S(2)}, u32[]{:S(2)}) %collective-permute-start.28) | collective-permute-done | bytes 262176 | tf_op jit(solution)/shard_map/ppermute | solution.py:36
  137.0 13.3 %collective-permute-done.44 = bf16[64,2048]{1,0:T(8,128)(2,1)S(1)} collective-permute-done((bf16[64,2048]{1,0:T(8,128)(2,1)S(1)}, bf16[64,2048]{1,0:T(8,128)(2,1)S(1)}, u32[]{:S(2)}, u32[]{:S(2)}) %collective-permute-start.44) | collective-permute-done | bytes 262176 | tf_op jit(solution)/shard_map/ppermute | solution.py:36
  156.4 6.4 %collective-permute-done.47 = bf16[128,2048]{1,0:T(8,128)(2,1)S(1)} collective-permute-done((bf16[128,2048]{1,0:T(8,128)(2,1)S(1)}, bf16[128,2048]{1,0:T(8,128)(2,1)S(1)}, u32[]{:S(2)}, u32[]{:S(2)}) %collective-permute-start.47) | collective-permute-done | bytes 524320 | tf_op jit(solution)/shard_map/ppermute | solution.py:36
  169.2 7.1 %collective-permute-done.49 = bf16[32,2048]{1,0:T(8,128)(2,1)S(1)} collective-permute-done((bf16[32,2048]{1,0:T(8,128)(2,1)S(1)}, bf16[32,2048]{1,0:T(8,128)(2,1)S(1)}, u32[]{:S(2)}, u32[]{:S(2)}) %collective-permute-start.49) | collective-permute-done | bytes 131104 | tf_op jit(solution)/shard_map/ppermute | solution.py:46
  (151 shorter events, 60.8 us)
Async XLA Ops:
  8.8 16.1 %collective-permute-start.5 = (bf16[512,2,512]{2,1,0:T(2,128)(2,1)S(1)}, bf16[512,2,512]{2,1,0:T(2,128)(2,1)S(1)}, u32[]{:S(2)}, u32[]{:S(2)}) collective-permute-start(bf16[512,2,512]{2,1,0:T(2,128)(2,1)S(1)} %get-tuple-element.85), channel_id=1, source_target_pairs={{0,1},{1,0},{2,3},{3,2},{4,5},{5,4},{6,7},{7,6},{8,9},{9,8},{10,11... | collective-permute-start | bytes 3145736 | tf_op jit(solution)/shard_map/ppermute | solution.py:36
  9.1 24.5 %collective-permute-start.3 = (bf16[512,2,512]{2,1,0:T(2,128)(2,1)}, bf16[512,2,512]{2,1,0:T(2,128)(2,1)S(1)}, u32[]{:S(2)}, u32[]{:S(2)}) collective-permute-start(bf16[512,2,512]{2,1,0:T(2,128)(2,1)} %get-tuple-element.86), channel_id=1, source_target_pairs={{0,1},{1,0},{2,3},{3,2},{4,5},{5,4},{6,7},{7,6},{8,9},{9,8},{10,11... | collective-permute-start | bytes 3145736 | tf_op jit(solution)/shard_map/ppermute | solution.py:36
  58.5 11.4 %collective-permute-start.10 = (bf16[32,2176]{1,0:T(8,128)(2,1)S(1)}, bf16[32,2176]{1,0:T(8,128)(2,1)S(1)}, u32[]{:S(2)}, u32[]{:S(2)}) collective-permute-start(bf16[32,2176]{1,0:T(8,128)(2,1)S(1)} %get-tuple-element.52), channel_id=1, source_target_pairs={{0,16},{4,20},{8,24},{12,28},{16,0},{20,4},{24,8},{28,12},{1,17},{... | collective-permute-start | bytes 417800 | tf_op jit(solution)/shard_map/ppermute | solution.py:46
  58.6 11.3 %collective-permute-start.11 = (bf16[32,2176]{1,0:T(8,128)(2,1)S(1)}, bf16[32,2176]{1,0:T(8,128)(2,1)S(1)}, u32[]{:S(2)}, u32[]{:S(2)}) collective-permute-start(bf16[32,2176]{1,0:T(8,128)(2,1)S(1)} %get-tuple-element.52), channel_id=1, source_target_pairs={{0,8},{4,12},{8,16},{12,20},{16,24},{20,28},{24,0},{28,4},{1,9},{5... | collective-permute-start | bytes 417800 | tf_op jit(solution)/shard_map/ppermute | solution.py:46
  69.9 15.3 %collective-permute-start.13 = (bf16[128,2176]{1,0:T(8,128)(2,1)S(1)}, bf16[128,2176]{1,0:T(8,128)(2,1)S(1)}, u32[]{:S(2)}, u32[]{:S(2)}) collective-permute-start(bf16[128,2176]{1,0:T(8,128)(2,1)S(1)} %constant_dynamic-update-slice_fusion.refs_0_), channel_id=1, source_target_pairs={{0,4},{4,0},{8,12},{12,8},{16,20},{20,16},{24,28},{28,24},{1,5},{5... | collective-permute-start | bytes 1671176 | tf_op jit(solution)/shard_map/ppermute | solution.py:36
  71.5 13.7 %collective-permute-start.12 = (bf16[128,2176]{1,0:T(8,128)(2,1)S(1)}, bf16[128,2176]{1,0:T(8,128)(2,1)S(1)}, u32[]{:S(2)}, u32[]{:S(2)}) collective-permute-start(bf16[128,2176]{1,0:T(8,128)(2,1)S(1)} %constant_dynamic-update-slice_fusion.refs_0_), channel_id=1, source_target_pairs={{0,2},{1,3},{2,0},{3,1},{4,6},{5,7},{6,4},{7,5},{8,10},{9,11},{10,... | collective-permute-start | bytes 1671176 | tf_op jit(solution)/shard_map/ppermute | solution.py:36
  72.6 26.9 %collective-permute-start.14 = (bf16[128,2176]{1,0:T(8,128)(2,1)S(1)}, bf16[128,2176]{1,0:T(8,128)(2,1)S(1)}, u32[]{:S(2)}, u32[]{:S(2)}) collective-permute-start(bf16[128,2176]{1,0:T(8,128)(2,1)S(1)} %constant_dynamic-update-slice_fusion.refs_0_), channel_id=1, source_target_pairs={{0,1},{1,0},{2,3},{3,2},{4,5},{5,4},{6,7},{7,6},{8,9},{9,8},{10,11... | collective-permute-start | bytes 1671176 | tf_op jit(solution)/shard_map/ppermute | solution.py:36
  74.0 14.5 %collective-permute-start.23 = (bf16[32,2176]{1,0:T(8,128)(2,1)S(1)}, bf16[32,2176]{1,0:T(8,128)(2,1)S(1)}, u32[]{:S(2)}, u32[]{:S(2)}) collective-permute-start(bf16[32,2176]{1,0:T(8,128)(2,1)S(1)} %get-tuple-element.66), channel_id=1, source_target_pairs={{0,16},{4,20},{8,24},{12,28},{16,0},{20,4},{24,8},{28,12},{1,17},{... | collective-permute-start | bytes 417800 | tf_op jit(solution)/shard_map/ppermute | solution.py:46
  78.7 10.9 %collective-permute-start.24 = (bf16[32,2176]{1,0:T(8,128)(2,1)S(1)}, bf16[32,2176]{1,0:T(8,128)(2,1)S(1)}, u32[]{:S(2)}, u32[]{:S(2)}) collective-permute-start(bf16[32,2176]{1,0:T(8,128)(2,1)S(1)} %get-tuple-element.66), channel_id=1, source_target_pairs={{0,8},{4,12},{8,16},{12,20},{16,24},{20,28},{24,0},{28,4},{1,9},{5... | collective-permute-start | bytes 417800 | tf_op jit(solution)/shard_map/ppermute | solution.py:46
  85.2 14.4 %collective-permute-start.15 = (bf16[128,2176]{1,0:T(8,128)(2,1)S(1)}, bf16[128,2176]{1,0:T(8,128)(2,1)S(1)}, u32[]{:S(2)}, u32[]{:S(2)}) collective-permute-start(bf16[128,2176]{1,0:T(8,128)(2,1)S(1)} %collective-permute-done.12.refs_1_), channel_id=1, source_target_pairs={{0,1},{1,0},{2,3},{3,2},{4,5},{5,4},{6,7},{7,6},{8,9},{9,8},{10,11... | collective-permute-start | bytes 1671176 | tf_op jit(solution)/shard_map/ppermute | solution.py:36
  85.2 14.9 %collective-permute-start.16 = (bf16[128,2176]{1,0:T(8,128)(2,1)S(1)}, bf16[128,2176]{1,0:T(8,128)(2,1)S(1)}, u32[]{:S(2)}, u32[]{:S(2)}) collective-permute-start(bf16[128,2176]{1,0:T(8,128)(2,1)S(1)} %collective-permute-done.13.refs_2_), channel_id=1, source_target_pairs={{0,1},{1,0},{2,3},{3,2},{4,5},{5,4},{6,7},{7,6},{8,9},{9,8},{10,11... | collective-permute-start | bytes 1671176 | tf_op jit(solution)/shard_map/ppermute | solution.py:36
  97.9 13.3 %collective-permute-start.25 = (bf16[128,2176]{1,0:T(8,128)(2,1)S(1)}, bf16[128,2176]{1,0:T(8,128)(2,1)S(1)}, u32[]{:S(2)}, u32[]{:S(2)}) collective-permute-start(bf16[128,2176]{1,0:T(8,128)(2,1)S(1)} %constant_dynamic-update-slice_fusion.4.refs_0_), channel_id=1, source_target_pairs={{0,2},{1,3},{2,0},{3,1},{4,6},{5,7},{6,4},{7,5},{8,10},{9,11},{10,... | collective-permute-start | bytes 1671176 | tf_op jit(solution)/shard_map/ppermute | solution.py:36
  99.0 13.0 %collective-permute-start.26 = (bf16[128,2176]{1,0:T(8,128)(2,1)S(1)}, bf16[128,2176]{1,0:T(8,128)(2,1)S(1)}, u32[]{:S(2)}, u32[]{:S(2)}) collective-permute-start(bf16[128,2176]{1,0:T(8,128)(2,1)S(1)} %constant_dynamic-update-slice_fusion.4.refs_0_), channel_id=1, source_target_pairs={{0,4},{4,0},{8,12},{12,8},{16,20},{20,16},{24,28},{28,24},{1,5},{5... | collective-permute-start | bytes 1671176 | tf_op jit(solution)/shard_map/ppermute | solution.py:36
  112.0 15.2 %collective-permute-start.17 = (bf16[384,2048]{1,0:T(8,128)(2,1)S(1)}, bf16[384,2048]{1,0:T(8,128)(2,1)S(1)}, u32[]{:S(2)}, u32[]{:S(2)}) collective-permute-start(bf16[384,2048]{1,0:T(8,128)(2,1)S(1)} %experts.6), channel_id=1, source_target_pairs={{0,1},{1,0},{2,3},{3,2},{4,5},{5,4},{6,7},{7,6},{8,9},{9,8},{10,11... | collective-permute-start | bytes 4718600 | tf_op jit(solution)/shard_map/ppermute | solution.py:36
  124.3 12.1 %collective-permute-start.38 = (bf16[384,2048]{1,0:T(8,128)(2,1)S(1)}, bf16[384,2048]{1,0:T(8,128)(2,1)S(1)}, u32[]{:S(2)}, u32[]{:S(2)}) collective-permute-start(bf16[384,2048]{1,0:T(8,128)(2,1)S(1)} %experts.9), channel_id=1, source_target_pairs={{0,1},{1,0},{2,3},{3,2},{4,5},{5,4},{6,7},{7,6},{8,9},{9,8},{10,11... | collective-permute-start | bytes 4718600 | tf_op jit(solution)/shard_map/ppermute | solution.py:36
  132.0 21.1 %collective-permute-start.31 = (bf16[128,2048]{1,0:T(8,128)(2,1)S(1)}, bf16[128,2048]{1,0:T(8,128)(2,1)S(1)}, u32[]{:S(2)}, u32[]{:S(2)}) collective-permute-start(bf16[128,2048]{1,0:T(8,128)(2,1)S(1)} %pad_maximum_fusion.1), channel_id=1, source_target_pairs={{0,2},{1,3},{2,0},{3,1},{4,6},{5,7},{6,4},{7,5},{8,10},{9,11},{10,... | collective-permute-start | bytes 1572872 | tf_op jit(solution)/shard_map/ppermute | solution.py:36
  133.0 20.1 %collective-permute-start.29 = (bf16[128,2048]{1,0:T(8,128)(2,1)S(1)}, bf16[128,2048]{1,0:T(8,128)(2,1)S(1)}, u32[]{:S(2)}, u32[]{:S(2)}) collective-permute-start(bf16[128,2048]{1,0:T(8,128)(2,1)S(1)} %pad_maximum_fusion), channel_id=1, source_target_pairs={{0,4},{4,0},{8,12},{12,8},{16,20},{20,16},{24,28},{28,24},{1,5},{5... | collective-permute-start | bytes 1572872 | tf_op jit(solution)/shard_map/ppermute | solution.py:36
  133.7 16.6 %collective-permute-start.44 = (bf16[64,2048]{1,0:T(8,128)(2,1)S(1)}, bf16[64,2048]{1,0:T(8,128)(2,1)S(1)}, u32[]{:S(2)}, u32[]{:S(2)}) collective-permute-start(bf16[64,2048]{1,0:T(8,128)(2,1)S(1)} %get-tuple-element.102), channel_id=1, source_target_pairs={{0,2},{1,3},{2,0},{3,1},{4,6},{5,7},{6,4},{7,5},{8,10},{9,11},{10,... | collective-permute-start | bytes 786440 | tf_op jit(solution)/shard_map/ppermute | solution.py:36
  134.9 16.1 %collective-permute-start.46 = (bf16[64,2048]{1,0:T(8,128)(2,1)S(1)}, bf16[64,2048]{1,0:T(8,128)(2,1)S(1)}, u32[]{:S(2)}, u32[]{:S(2)}) collective-permute-start(bf16[64,2048]{1,0:T(8,128)(2,1)S(1)} %get-tuple-element.103), channel_id=1, source_target_pairs={{0,4},{4,0},{8,12},{12,8},{16,20},{20,16},{24,28},{28,24},{1,5},{5... | collective-permute-start | bytes 786440 | tf_op jit(solution)/shard_map/ppermute | solution.py:36
  151.2 11.5 %collective-permute-start.47 = (bf16[128,2048]{1,0:T(8,128)(2,1)S(1)}, bf16[128,2048]{1,0:T(8,128)(2,1)S(1)}, u32[]{:S(2)}, u32[]{:S(2)}) collective-permute-start(bf16[128,2048]{1,0:T(8,128)(2,1)S(1)} %pad_maximum_fusion.3), channel_id=1, source_target_pairs={{0,2},{1,3},{2,0},{3,1},{4,6},{5,7},{6,4},{7,5},{8,10},{9,11},{10,... | collective-permute-start | bytes 1572872 | tf_op jit(solution)/shard_map/ppermute | solution.py:36
  152.5 11.2 %collective-permute-start.45 = (bf16[128,2048]{1,0:T(8,128)(2,1)S(1)}, bf16[128,2048]{1,0:T(8,128)(2,1)S(1)}, u32[]{:S(2)}, u32[]{:S(2)}) collective-permute-start(bf16[128,2048]{1,0:T(8,128)(2,1)S(1)} %pad_maximum_fusion.2), channel_id=1, source_target_pairs={{0,4},{4,0},{8,12},{12,8},{16,20},{20,16},{24,28},{28,24},{1,5},{5... | collective-permute-start | bytes 1572872 | tf_op jit(solution)/shard_map/ppermute | solution.py:36
  153.4 10.6 %collective-permute-start.34 = (bf16[32,2048]{1,0:T(8,128)(2,1)S(1)}, bf16[32,2048]{1,0:T(8,128)(2,1)S(1)}, u32[]{:S(2)}, u32[]{:S(2)}) collective-permute-start(bf16[32,2048]{1,0:T(8,128)(2,1)S(1)} %get-tuple-element.97), channel_id=1, source_target_pairs={{0,24},{4,28},{8,0},{12,4},{16,8},{20,12},{24,16},{28,20},{1,25},{... | collective-permute-start | bytes 393224 | tf_op jit(solution)/shard_map/ppermute | solution.py:46
  153.4 10.6 %collective-permute-start.33 = (bf16[32,2048]{1,0:T(8,128)(2,1)S(1)}, bf16[32,2048]{1,0:T(8,128)(2,1)S(1)}, u32[]{:S(2)}, u32[]{:S(2)}) collective-permute-start(bf16[32,2048]{1,0:T(8,128)(2,1)S(1)} %get-tuple-element.98), channel_id=1, source_target_pairs={{0,16},{4,20},{8,24},{12,28},{16,0},{20,4},{24,8},{28,12},{1,17},{... | collective-permute-start | bytes 393224 | tf_op jit(solution)/shard_map/ppermute | solution.py:46
  165.2 11.2 %collective-permute-start.49 = (bf16[32,2048]{1,0:T(8,128)(2,1)S(1)}, bf16[32,2048]{1,0:T(8,128)(2,1)S(1)}, u32[]{:S(2)}, u32[]{:S(2)}) collective-permute-start(bf16[32,2048]{1,0:T(8,128)(2,1)S(1)} %get-tuple-element.106), channel_id=1, source_target_pairs={{0,16},{4,20},{8,24},{12,28},{16,0},{20,4},{24,8},{28,12},{1,17},{... | collective-permute-start | bytes 393224 | tf_op jit(solution)/shard_map/ppermute | solution.py:46
  (33 other events, 207.1 us)

commit v4 on v3

--- a/solution.py
+++ b/solution.py
@@ -12,7 +12,7 @@
 LANES = 128
 LOG2E = 1.4426950408889634
 CUTS = 2
-OWN_STEPS = 2
+PARTS = 2
 rope_base = 10000.0
 norm_eps = 1e-06
 BF = jnp.bfloat16
@@ -54,52 +54,73 @@
     return [pltpu.with_memory_space_constraint(v, pltpu.HBM) for v in values]
 
 
-CHUNKS = 4
-
-
-def project_kernel(t0, t1, t2, t3, gain, cosine, sine, w_hbm, q, k, v, normed, w, sems):
-    rows, width = t0.shape
-    depth = width // CHUNKS
-
-    def load(part, i):
-        cut = pl.ds(i * depth, depth)
-        return pltpu.make_async_copy(w_hbm.at[part, cut], w.at[part, cut], sems.at[part, i])
-
-    for part in range(3):
-        for i in range(CHUNKS):
-            load(part, i).start()
+def stage_kernel(who, kv, own, guest, sems):
+    local = own.shape[2]
+    some = kv.shape[1] // sems.shape[1]
+    copies = []
+    for i, (bit, target) in enumerate(((1, own), (3, guest))):
+        cols = pl.ds(pl.multiple_of((who[0] ^ bit) * local, local), local)
+        for j in range(sems.shape[1]):
+            rows = pl.ds(j * some, some)
+            copies.append(
+                pltpu.make_async_copy(kv.at[0, rows, :, cols], target.at[rows], sems.at[i, j])
+            )
+    for copy in copies:
+        copy.start()
+    for copy in copies:
+        copy.wait()
+
+
+def stage(who, kv, local):
+    depth = kv.shape[1]
+    piece = jax.ShapeDtypeStruct((depth, 2, local), BF)
+    return pl.pallas_call(
+        stage_kernel,
+        grid_spec=pltpu.PrefetchScalarGridSpec(
+            num_scalar_prefetch=1,
+            grid=(1,),
+            in_specs=[pl.BlockSpec(memory_space=pltpu.HBM)],
+            out_specs=[whole(piece.shape)] * 2,
+            scratch_shapes=[pltpu.SemaphoreType.DMA((2, 4))],
+        ),
+        out_shape=[piece, piece],
+        compiler_params=params(8),
+        cost_estimate=cost(0, 8 * piece.size),
+        name="stage",
+    )(who, *in_hbm(kv))
+
+
+def project_kernel(t0, t1, t2, t3, gain, cosine, sine, w, *refs):
+    *queries, k, v, normed = refs
+    rows = t0.shape[0]
     for i, ref in enumerate((t0, t1, t2, t3)):
         values = ref[...].astype(F32)
         mean_sq = jnp.mean(values * values, axis=-1, keepdims=True)
         scaled = values * lax.rsqrt(mean_sq + norm_eps) * gain[...]
         normed[pl.ds(i * rows, rows), :] = scaled.astype(BF)
-    for part, ref in enumerate((q, k, v)):
-        for i in range(CHUNKS):
-            load(part, i).wait()
+    for part, outs in enumerate((queries, [k], [v])):
         out = jnp.dot(normed[...], w[part], preferred_element_type=F32)
         if part == 2:
-            ref[...] = out.astype(BF)
+            v[...] = out.astype(BF)
             continue
-        for h in range(out.shape[1] // HD):
+        heads = out.shape[1] // HD
+        for h in range(heads):
             one = out[:, h * HD : (h + 1) * HD]
             turned = one * cosine[...] + pltpu.roll(one, HD // 2, 1) * sine[...]
-            ref[:, h * HD : (h + 1) * HD] = turned.astype(BF)
+            some = heads // len(outs)
+            outs[h // some][:, h % some * HD : (h % some + 1) * HD] = turned.astype(BF)
 
 
 def project(blocks, gain, cosine, sine, w):
     rows, width = blocks[0].shape
     total, local = 4 * rows, w.shape[2]
-    shape = jax.ShapeDtypeStruct((total, local), BF)
+    widths = [local // PARTS] * PARTS + [local, local]
     return pl.pallas_call(
         project_kernel,
-        out_shape=(shape,) * 3,
-        in_specs=[pl.BlockSpec(memory_space=pltpu.VMEM)] * 7 + [pl.BlockSpec(memory_space=pltpu.HBM)],
-        out_specs=(pl.BlockSpec(memory_space=pltpu.VMEM),) * 3,
-        scratch_shapes=[
-            pltpu.VMEM((total, width), BF),
-            pltpu.VMEM(w.shape, BF),
-            pltpu.SemaphoreType.DMA((3, CHUNKS)),
-        ],
+        out_shape=[jax.ShapeDtypeStruct((total, one), BF) for one in widths],
+        in_specs=[pl.BlockSpec(memory_space=pltpu.VMEM)] * 8,
+        out_specs=[pl.BlockSpec(memory_space=pltpu.VMEM)] * len(widths),
+        scratch_shapes=[pltpu.VMEM((total, width), BF)],
         compiler_params=params(20),
         cost_estimate=cost(6 * total * width * local, 6 * width * local),
         name="project",
@@ -134,22 +155,15 @@
 
 
 def own_kernel(group, q, kv_here, kv_there, k, v, seg_row, seg_col, out, stats):
-    step = pl.program_id(0)
     same = seg_row[...] == seg_col[...]
     lane = lax.broadcasted_iota(jnp.int32, stats.shape, 1)
-    heads = q.shape[1] // HD
-
-    @pl.when(step == 0)
-    def _():
-        stats[...] = jnp.zeros_like(stats)
-
-    levels = stats[...]
-    for h in range(heads):
+    levels = jnp.zeros(stats.shape, F32)
+    for h in range(q.shape[1] // HD):
         cols = slice(h * HD, (h + 1) * HD)
         pieces = cached(kv_here, kv_there, cols) + [(k[:, cols], v[:, cols], same)]
         mixed, level = attend_pieces(q[:, cols], pieces)
         out[:, cols] = mixed
-        levels = jnp.where(lane == step * heads + h, level, levels)
+        levels = jnp.where(lane == h, level, levels)
     stats[...] = levels
 
 
@@ -169,72 +183,74 @@
     out[:, local:] = tail.astype(BF)
 
 
-def kv_specs(depth, local, steps):
-    some = local // steps
+def kv_specs(depth, some, part):
     return [
-        pl.BlockSpec((1, depth, 2, some), lambda i, g: (0, 0, 0, g[0] * steps + i)),
-        pl.BlockSpec((depth, 2, some), lambda i, g: (0, 0, i)),
+        pl.BlockSpec((1, depth, 2, some), lambda i, g: (0, 0, 0, g[0] * PARTS + part)),
+        pl.BlockSpec((depth, 2, some), lambda i, g: (0, 0, part)),
     ]
 
 
-def attend_own(group, q, kv, kv_there, k, v, seg_row, seg_col):
-    rows, local = q.shape
-    heads, depth = local // HD, kv.shape[1]
-    steps = OWN_STEPS
-    block = pl.BlockSpec((rows, local // steps), lambda i, g: (0, i))
+def attend_own(group, part, q, kv, kv_there, k, v, seg_row, seg_col):
+    rows, some = q.shape
+    depth = kv.shape[1]
+    block = pl.BlockSpec((rows, some), lambda i, g: (0, part))
     keys = 2 * depth + rows
     return pl.pallas_call(
         own_kernel,
         grid_spec=pltpu.PrefetchScalarGridSpec(
             num_scalar_prefetch=1,
-            grid=(steps,),
-            in_specs=[block]
-            + kv_specs(depth, local, steps)
+            grid=(1,),
+            in_specs=[whole((rows, some))]
+            + kv_specs(depth, some, part)
             + [block, block, whole((rows, 1)), whole((1, rows))],
-            out_specs=(block, whole((rows, LANES))),
+            out_specs=(whole((rows, some)), whole((rows, LANES))),
         ),
         out_shape=(
-            jax.ShapeDtypeStruct((rows, local), F32),
+            jax.ShapeDtypeStruct((rows, some), F32),
             jax.ShapeDtypeStruct((rows, LANES), F32),
         ),
         compiler_params=params(20),
-        cost_estimate=cost(4 * rows * keys * local, 4 * keys * local, rows * keys * heads),
+        cost_estimate=cost(4 * rows * keys * some, 4 * keys * some, rows * keys * some // HD),
         name="attend_own",
     )(group, q, kv, kv_there, k, v, seg_row, seg_col)
 
 
-def attend_guest(group, q, kv, kv_there):
-    rows, local = q.shape
-    heads, depth = local // HD, kv.shape[1]
+def attend_guest(group, part, q, kv, kv_there):
+    rows, some = q.shape
+    depth = kv.shape[1]
     keys = 2 * depth
     return pl.pallas_call(
         guest_kernel,
         grid_spec=pltpu.PrefetchScalarGridSpec(
             num_scalar_prefetch=1,
             grid=(1,),
-            in_specs=[whole((rows, local))] + kv_specs(depth, local, 1),
-            out_specs=whole((rows, local + LANES)),
-        ),
-        out_shape=jax.ShapeDtypeStruct((rows, local + LANES), BF),
+            in_specs=[whole((rows, some))] + kv_specs(depth, some, part),
+            out_specs=whole((rows, some + LANES)),
+        ),
+        out_shape=jax.ShapeDtypeStruct((rows, some + LANES), BF),
         compiler_params=params(20),
-        cost_estimate=cost(4 * rows * keys * local, 4 * keys * local, rows * keys * heads),
+        cost_estimate=cost(4 * rows * keys * some, 4 * keys * some, rows * keys * some // HD),
         name="attend_guest",
     )(group, q, kv, kv_there)
 
 
-def join_kernel(own, own_stats, guest, w, keep, send):
-    local = own.shape[1]
+def join_kernel(*refs):
+    owns, levels, guests = (refs[i * PARTS : (i + 1) * PARTS] for i in range(3))
+    w, keep, send = refs[3 * PARTS :]
     dev = keep.shape[0] // 2
     heads = []
-    for h in range(local // HD):
-        cols = slice(h * HD, (h + 1) * HD)
-        first = own_stats[:, h : h + 1]
-        second = functools.reduce(
-            jnp.add, [guest[:, local + 3 * h + i : local + 3 * h + i + 1].astype(F32) for i in range(3)]
-        )
-        top = jnp.maximum(first, second)
-        a, b = jnp.exp(first - top), jnp.exp(second - top)
-        heads.append(((own[:, cols] * a + guest[:, cols].astype(F32) * b) / (a + b)).astype(BF))
+    for own, stats, guest in zip(owns, levels, guests):
+        some = own.shape[1]
+        for h in range(some // HD):
+            cols = slice(h * HD, (h + 1) * HD)
+            first = stats[:, h : h + 1]
+            start = some + 3 * h
+            thirds = [guest[:, start + i : start + i + 1].astype(F32) for i in range(3)]
+            second = functools.reduce(jnp.add, thirds)
+            top = jnp.maximum(first, second)
+            a, b = jnp.exp(first - top), jnp.exp(second - top)
+            both = own[:, cols] * a + guest[:, cols].astype(F32) * b
+            heads.append((both / (a + b)).astype(BF))
     mixed = jnp.concatenate(heads, axis=1)
     out = jnp.dot(mixed, w[...], preferred_element_type=F32)
     for i in range(2):
@@ -242,9 +258,9 @@
         send[pl.ds(i * dev, dev), :] = out[(2 * i + 1) * dev : (2 * i + 2) * dev].astype(BF)
 
 
-def join(own, own_stats, guest, w):
-    rows, local = own.shape
-    width = w.shape[1]
+def join(owns, levels, guests, w):
+    rows = owns[0].shape[0]
+    local, width = w.shape
     return pl.pallas_call(
         join_kernel,
         out_shape=(
@@ -254,7 +270,7 @@
         compiler_params=params(20),
         cost_estimate=cost(2 * rows * local * width, 2 * local * width + 6 * rows * width // 2),
         name="join",
-    )(own, own_stats, guest, w)
+    )(*owns, *levels, *guests, w)
 
 
 def entry_kernel(me, tokens, keep, arrived, gain, w_router, routes, resid, *messages):
@@ -456,14 +472,14 @@
     second = after(second, *first_z)
     second_z = [from_z(second, k) for k in range(1, depth)]
     here_a = join_rows(first, *first_z)
-    here_b = join_rows(second, *second_z)
     y_a, x_a = move_y(here_a), move_x(here_a)
     held = hold(*after(weights, y_a, x_a))
     corner_a = [move_y(x_a[:half]), move_x(y_a[half:])]
     main_a = [here_a, y_a, x_a]
     their_main_a, their_corner_a = ([move_c(v) for v in values] for values in (main_a, corner_a))
     (sent_a,) = expert_part(group, their_main_a, held)
-    leaving_b = after(here_b, *corner_a)
+    here_b = join_rows(second, *after(second_z, *corner_a))
+    leaving_b = here_b
     y_b, x_b = move_y(leaving_b), move_x(leaving_b)
     (kept_a,) = expert_part(group, after(main_a, sent_a), held)
     sent_corner, kept_corner = expert_part(
@@ -521,29 +537,31 @@
     group = lax.axis_index("tok").astype(jnp.int32).reshape(1)
 
     by_c, by_y = move_c(tokens), move_y(tokens)
-    blocks = [tokens, by_c, by_y, move_c(by_y)]
-
-    def columns(who):
-        return lax.dynamic_slice_in_dim(prefix_kv[0], who * local, local, 2)
-
-    later = after(me, by_c)
-    own_there, guest_there = move_c(columns(later ^ 1)), move_c(columns(later ^ 3))
+    mine = me.astype(jnp.int32).reshape(1)
+    own_there, guest_there = stage(mine, prefix_kv, local)
+    (w_held,) = hold(jnp.transpose(w_qkv, (1, 0, 2)))
+    blocks = [tokens, by_c, by_y, move_c(after(by_y, w_held, guest_there))]
+
+    own_there, guest_there = move_c(own_there), move_c(guest_there)
 
     index = ((me ^ jnp.arange(4))[:, None] * dev + jnp.arange(dev)[None, :]).reshape(-1)
     segment, position = request_layout(lengths[0], index)
     cosine, sine = rotation(position)
 
-    q, k, v = project(
-        blocks, attn_gain.reshape(1, -1), cosine, sine, *in_hbm(jnp.transpose(w_qkv, (1, 0, 2)))
-    )
-    guest_q = move_y(q)
-    mine = me.astype(jnp.int32).reshape(1)
+    *queries, k, v = project(blocks, attn_gain.reshape(1, -1), cosine, sine, w_held)
+    guest_queries = [move_y(q) for q in queries]
     (cache,) = in_hbm(prefix_kv)
-    own, own_stats = attend_own(
-        mine, q, cache, own_there, k, v, segment.reshape(-1, 1), segment.reshape(1, -1)
-    )
-    guest = move_y(attend_guest(mine ^ 2, guest_q, cache, guest_there))
-    keep, send = join(own, own_stats, guest, w_out)
+    seg_row, seg_col = segment.reshape(-1, 1), segment.reshape(1, -1)
+    owns, guests, done = [], [], None
+    owns.append(attend_own(mine, 0, queries[0], cache, own_there, k, v, seg_row, seg_col))
+    for part in range(PARTS):
+        q = after(guest_queries[part], owns[0][0])
+        done = attend_guest(mine ^ 2, part, q, cache, guest_there)
+        guests.append(move_y(done))
+    for part in range(1, PARTS):
+        q = after(queries[part], done, *guests[:-1])
+        owns.append(attend_own(mine, part, q, cache, own_there, k, v, seg_row, seg_col))
+    keep, send = join([o for o, _ in owns], [l for _, l in owns], guests, w_out)
     chip = keep + move_c(send).astype(F32)
     arrived = move_y(chip[dev:].astype(BF))
     resid, *messages = entry(

time: 177 us -> 169 us (0.955)
  waiting for transfers between devices: 81.9 us -> 69.1 us
  Pallas kernels: 40.2 us -> 46.5 us
  local copies, waits for them, and re-layouts: 5.23 us -> 1.47 us
  starting transfers between devices: 43.7 us -> 46.3 us
    ppermute x39 -> x41, waiting for transfers between devices: 58 us -> 49.3 us  [swap(): return lax.ppermute(value, axis, [(i, i ^ bit) for i in range(size)])]
    dynamic_slice x1 -> x0, local copies, waits for them, and re-layouts: 4.06 us -> none  [columns(): return lax.dynamic_slice_in_dim(prefix_kv[0], who * local, local, 2)]
    ppermute x12, waiting for transfers between devices: 23.8 us -> 19.8 us  [from_z(): lax.ppermute(value, 'tok', [(i, (i - 2 * k) % size) for i in range(size)])]
    pallas_call x1 -> x2, Pallas kernels: 2.88 us -> 5.86 us  [hold(): pl.pallas_call(functools.partial(hold_kernel, count), out_shape=[jax.Shap...]
    ppermute x39 -> x41, starting transfers between devices: 26.1 us -> 27.4 us  [swap(): return lax.ppermute(value, axis, [(i, i ^ bit) for i in range(size)])]
    pallas_call x1 -> x2, Pallas kernels: 4.13 us -> 5.4 us  [the longest x1 2.96 us: stage(): pl.pallas_call(stage_kernel, grid_spec=pltpu.PrefetchScalarGridSpec(num_s...]
    pallas_call x1 -> x2, Pallas kernels: 7.05 us -> 8.22 us  [attend_guest(): pl.pallas_call(guest_kernel, grid_spec=pltpu.PrefetchScalarGridSpec(num_s...]
    pallas_call x1 -> x2, Pallas kernels: 7.84 us -> 8.62 us  [attend_own(): pl.pallas_call(own_kernel, grid_spec=pltpu.PrefetchScalarGridSpec(num_sca...]
  transfers between devices with their start and end apart: 51 -> 53, of which waited for: 24 -> 25; matrix products, arithmetic and copies ran while one was open for 6% -> 3% of each run, Pallas kernels for 21% -> 26%
where the time goes in v4:
time: 169 us; the launch traced here: 168 us
  waiting for transfers between devices  69.1 us (41%)
  Pallas kernels  46.5 us (28%)
  starting transfers between devices  46.3 us (27%)
  other arithmetic  4.47 us (3%)
    ppermute x41, waiting for transfers between devices, swap(): return lax.ppermute(value, axis, [(i, i ^ bit) for i in range(size)])  49.3 us
    ppermute x41, starting transfers between devices, swap(): return lax.ppermute(value, axis, [(i, i ^ bit) for i in range(size)])  27.4 us
    ppermute x12, waiting for transfers between devices, from_z(): lax.ppermute(value, 'tok', [(i, (i - 2 * k) % size) for i in range(size)])  19.8 us
    ppermute x12, starting transfers between devices, from_z(): lax.ppermute(value, 'tok', [(i, (i - 2 * k) % size) for i in range(size)])  18.9 us
    pallas_call x6, Pallas kernels, expert_part(): pl.pallas_call(functools.partial(expert_kernel, sizes, tile), grid_spec=p...  16.1 us
    pallas_call x2, Pallas kernels, attend_own(): pl.pallas_call(own_kernel, grid_spec=pltpu.PrefetchScalarGridSpec(num_sca...  8.62 us
    pallas_call x2, Pallas kernels, attend_guest(): pl.pallas_call(guest_kernel, grid_spec=pltpu.PrefetchScalarGridSpec(num_s...  8.22 us
    pallas_call x2, Pallas kernels, hold(): pl.pallas_call(functools.partial(hold_kernel, count), out_shape=[jax.Shap...  5.86 us
  transfers between devices with their start and end apart: 53, of which 25 were waited for; matrix products, arithmetic and copies ran while one was open for 3% of the time, Pallas kernels for 26%

profile of v4, /device:TPU:0, one launch (start us, length us, event | category | flops | bytes accessed | tf_op | source)
XLA Modules:
  0.0 168.4 jit_solution(758805489465632022)
XLA Ops:
  0.5 2.5 %collective-permute-start.1 = (bf16[64,2048]{1,0:T(8,128)(2,1)}, bf16[64,2048]{1,0:T(8,128)(2,1)S(1)}, u32[]{:S(2)}, u32[]{:S(2)}) collective-permute-start(bf16[64,2048]{1,0:T(8,128)(2,1)} %tokens.1), channel_id=1, source_target_pairs={{0,2},{1,3},{2,0},{3,1},{4,6},{5,7},{6,4},{7,5},{8,10},{9,11},{10,... | collective-permute-start | bytes 786440 | tf_op jit(solution)/shard_map/ppermute | solution.py:36
  3.0 3.0 %stage.1 = (bf16[512,2,512]{2,1,0:T(2,128)(2,1)}, bf16[512,2,512]{2,1,0:T(2,128)(2,1)}) custom-call(s32[1]{0:T(128)} %bitcast.who.group.me, bf16[1,512,2,2048]{3,2,1,0:T(2,128)(2,1)} %kv_here.7), custom_call_target="tpu_custom_call" | custom-call | bytes 4194304 | tf_op jit(solution)/shard_map/stage/pallas_call | solution.py:77
  7.0 2.9 %hold.2.w = bf16[3,2048,512]{2,1,0:T(8,128)(2,1)S(1)} custom-call(bf16[3,2048,512]{2,1,0:T(8,128)(2,1)} %bitcast.15), custom_call_target="tpu_custom_call" | custom-call | bytes 12582912 | tf_op jit(solution)/shard_map/hold/pallas_call | solution.py:453
  11.7 2.4 %project.1 = (bf16[256,256]{1,0:T(8,128)(2,1)}, bf16[256,256]{1,0:T(8,128)(2,1)}, bf16[256,512]{1,0:T(8,128)(2,1)S(1)}, bf16[256,512]{1,0:T(8,128)(2,1)S(1)}) custom-call(bf16[64,2048]{1,0:T(8,128)(2,1)S(1)} %copy-done.1, bf16[64,2048]{1,0:T(8,128)(2,1)S(1)} %collective-permute-done.t1, bf16[64,2048]{1,0:T(8,128)(2,1)S(1)} %collective-permute-done.1.t2, ...), custom_call_target="tpu_custom_call" | custom-call | flops 1610612736 | bytes 6291456 | tf_op jit(solution)/shard_map/project/pallas_call | solution.py:118
  16.3 4.2 %attend_own.2 = (f32[256,256]{1,0:T(8,128)S(1)}, f32[256,128]{1,0:T(8,128)S(1)}) custom-call(s32[1]{0:T(128)} %bitcast.who.group.me, bf16[256,256]{1,0:T(8,128)(2,1)} %get-tuple-element.55.q, bf16[1,512,2,2048]{3,2,1,0:T(2,128)(2,1)} %kv_here.7, bf16[512,2,512]{2,1,0:T(2,128)(2,1)S(1)} %collective-permute-done.3.kv_there, ...), custom_call_target="tpu_custom_call" | custom-call | flops 335544320 | bytes 1310720 | tf_op jit(solution)/shard_map/attend_own/pallas_call | solution.py:198
  20.7 4.0 %attend_guest.3 = bf16[256,384]{1,0:T(8,128)(2,1)S(1)} custom-call(s32[1]{0:T(128)S(6)} %xor.16.group, bf16[256,256]{1,0:T(8,128)(2,1)S(1)} %collective-permute-done.6.q, bf16[1,512,2,2048]{3,2,1,0:T(2,128)(2,1)} %kv_here.7, bf16[512,2,512]{2,1,0:T(2,128)(2,1)S(1)} %collective-permute-done.5.kv_there), custom_call_target="tpu_custom_call" | custom-call | flops 268435456 | bytes 1048576 | tf_op jit(solution)/shard_map/attend_guest/pallas_call | solution.py:222
  26.5 4.2 %attend_guest.2 = bf16[256,384]{1,0:T(8,128)(2,1)S(1)} custom-call(s32[1]{0:T(128)S(6)} %xor.16.group, bf16[256,256]{1,0:T(8,128)(2,1)S(1)} %collective-permute-done.4.q, bf16[1,512,2,2048]{3,2,1,0:T(2,128)(2,1)} %kv_here.7, bf16[512,2,512]{2,1,0:T(2,128)(2,1)S(1)} %collective-permute-done.5.kv_there), custom_call_target="tpu_custom_call" | custom-call | flops 268435456 | bytes 1048576 | tf_op jit(solution)/shard_map/attend_guest/pallas_call | solution.py:222
  31.1 4.4 %attend_own.3 = (f32[256,256]{1,0:T(8,128)S(1)}, f32[256,128]{1,0:T(8,128)S(1)}) custom-call(s32[1]{0:T(128)} %bitcast.who.group.me, bf16[256,256]{1,0:T(8,128)(2,1)} %get-tuple-element.63.q, bf16[1,512,2,2048]{3,2,1,0:T(2,128)(2,1)} %kv_here.7, bf16[512,2,512]{2,1,0:T(2,128)(2,1)S(1)} %collective-permute-done.3.kv_there, ...), custom_call_target="tpu_custom_call" | custom-call | flops 335544320 | bytes 1310720 | tf_op jit(solution)/shard_map/attend_own/pallas_call | solution.py:198
  41.8 7.3 %collective-permute-done.10.arrived = bf16[64,2048]{1,0:T(8,128)(2,1)S(1)} collective-permute-done((bf16[64,2048]{1,0:T(8,128)(2,1)S(1)}, bf16[64,2048]{1,0:T(8,128)(2,1)S(1)}, u32[]{:S(2)}, u32[]{:S(2)}) %collective-permute-start.10) | collective-permute-done | bytes 262176 | tf_op jit(solution)/shard_map/ppermute | solution.py:36
  49.7 3.6 %collective-permute-start.11 = (bf16[32,2176]{1,0:T(8,128)(2,1)S(1)}, bf16[32,2176]{1,0:T(8,128)(2,1)S(1)}, u32[]{:S(2)}, u32[]{:S(2)}) collective-permute-start(bf16[32,2176]{1,0:T(8,128)(2,1)S(1)} %get-tuple-element.70), channel_id=1, source_target_pairs={{0,24},{4,28},{8,0},{12,4},{16,8},{20,12},{24,16},{28,20},{1,25},{... | collective-permute-start | bytes 417800 | tf_op jit(solution)/shard_map/ppermute | solution.py:46
  54.4 3.0 %collective-permute-done.11 = bf16[32,2176]{1,0:T(8,128)(2,1)S(1)} collective-permute-done((bf16[32,2176]{1,0:T(8,128)(2,1)S(1)}, bf16[32,2176]{1,0:T(8,128)(2,1)S(1)}, u32[]{:S(2)}, u32[]{:S(2)}) %collective-permute-start.11) | collective-permute-done | bytes 139296 | tf_op jit(solution)/shard_map/ppermute | solution.py:46
  57.5 7.3 %collective-permute-done.12 = bf16[32,2176]{1,0:T(8,128)(2,1)S(1)} collective-permute-done((bf16[32,2176]{1,0:T(8,128)(2,1)S(1)}, bf16[32,2176]{1,0:T(8,128)(2,1)S(1)}, u32[]{:S(2)}, u32[]{:S(2)}) %collective-permute-start.12) | collective-permute-done | bytes 139296 | tf_op jit(solution)/shard_map/ppermute | solution.py:46
  71.5 7.3 %collective-permute-done.15.refs_2_ = bf16[128,2176]{1,0:T(8,128)(2,1)S(1)} collective-permute-done((bf16[128,2176]{1,0:T(8,128)(2,1)S(1)}, bf16[128,2176]{1,0:T(8,128)(2,1)S(1)}, u32[]{:S(2)}, u32[]{:S(2)}) %collective-permute-start.15) | collective-permute-done | bytes 557088 | tf_op jit(solution)/shard_map/ppermute | solution.py:36
  81.0 3.0 %hold.3 = (bf16[2,2048,256]{2,1,0:T(8,128)(2,1)S(1)}, bf16[2,2048,256]{2,1,0:T(8,128)(2,1)S(1)}, bf16[2,256,2048]{2,1,0:T(8,128)(2,1)S(1)}) custom-call(bf16[2,2048,256]{2,1,0:T(8,128)(2,1)} %refs_0_, bf16[2,2048,256]{2,1,0:T(8,128)(2,1)} %refs_1_, bf16[2,256,2048]{2,1,0:T(8,128)(2,1)} %refs_2_), custom_call_target="tpu_custom_call" | custom-call | bytes 12582912 | tf_op jit(solution)/shard_map/hold/pallas_call | solution.py:453
  90.0 2.9 %experts.6 = bf16[384,2048]{1,0:T(8,128)(2,1)S(1)} custom-call(s32[1]{0:T(128)} %bitcast.9.group, bf16[128,2176]{1,0:T(8,128)(2,1)S(1)} %collective-permute-done.16.refs_0_, bf16[128,2176]{1,0:T(8,128)(2,1)S(1)} %collective-permute-done.17.refs_1_, bf16[128,2176]{1,0:T(8,128)(2,1)S(1)} %collective-permute-done.18.refs_2_, ...), custom_call_target="tpu_custom_call" | custom-call | flops 2415919104 | bytes 9437184 | tf_op jit(solution)/shard_map/experts/pallas_call | solution.py:382
  92.9 2.9 %experts.7 = bf16[384,2048]{1,0:T(8,128)(2,1)S(1)} custom-call(s32[1]{0:T(128)} %bitcast.9.group, bf16[128,2176]{1,0:T(8,128)(2,1)S(1)} %constant_dynamic-update-slice_fusion.refs_0_, bf16[128,2176]{1,0:T(8,128)(2,1)S(1)} %collective-permute-done.14.refs_1_, bf16[128,2176]{1,0:T(8,128)(2,1)S(1)} %collective-permute-done.15.refs_2_, ...), custom_call_target="tpu_custom_call" | custom-call | flops 2415919104 | bytes 9437184 | tf_op jit(solution)/shard_map/experts/pallas_call | solution.py:382
  103.5 2.9 %experts.9 = bf16[384,2048]{1,0:T(8,128)(2,1)S(1)} custom-call(s32[1]{0:T(128)} %bitcast.9.group, bf16[128,2176]{1,0:T(8,128)(2,1)S(1)} %collective-permute-done.37.refs_0_, bf16[128,2176]{1,0:T(8,128)(2,1)S(1)} %collective-permute-done.38.refs_1_, bf16[128,2176]{1,0:T(8,128)(2,1)S(1)} %collective-permute-done.39.refs_2_, ...), custom_call_target="tpu_custom_call" | custom-call | flops 2415919104 | bytes 9437184 | tf_op jit(solution)/shard_map/experts/pallas_call | solution.py:382
  106.4 2.9 %experts.10 = bf16[384,2048]{1,0:T(8,128)(2,1)S(1)} custom-call(s32[1]{0:T(128)} %bitcast.9.group, bf16[128,2176]{1,0:T(8,128)(2,1)S(1)} %constant_dynamic-update-slice_fusion.4.refs_0_, bf16[128,2176]{1,0:T(8,128)(2,1)S(1)} %collective-permute-done.27.refs_1_, bf16[128,2176]{1,0:T(8,128)(2,1)S(1)} %collective-permute-done.28.refs_2_, ...), custom_call_target="tpu_custom_call" | custom-call | flops 2415919104 | bytes 9437184 | tf_op jit(solution)/shard_map/experts/pallas_call | solution.py:382
  113.4 2.3 %experts.11 = (bf16[128,2048]{1,0:T(8,128)(2,1)S(1)}, bf16[128,2048]{1,0:T(8,128)(2,1)S(1)}) custom-call(s32[1]{0:T(128)} %bitcast.9.group, bf16[64,2176]{1,0:T(8,128)(2,1)S(1)} %collective-permute-done.43.refs_0_, bf16[64,2176]{1,0:T(8,128)(2,1)S(1)} %collective-permute-done.44.refs_1_, bf16[64,2176]{1,0:T(8,128)(2,1)S(1)} %collective-permute-done.41.refs_2_, ...), custom_call_target="tpu_custom_call" | custom-call | flops 1610612736 | bytes 8388608 | tf_op jit(solution)/shard_map/experts/pallas_call | solution.py:382
  116.9 2.9 %collective-permute-done.30 = bf16[64,2048]{1,0:T(8,128)(2,1)S(1)} collective-permute-done((bf16[64,2048]{1,0:T(8,128)(2,1)S(1)}, bf16[64,2048]{1,0:T(8,128)(2,1)S(1)}, u32[]{:S(2)}, u32[]{:S(2)}) %collective-permute-start.30) | collective-permute-done | bytes 262176 | tf_op jit(solution)/shard_map/ppermute | solution.py:36
  126.2 13.1 %collective-permute-done.46 = bf16[64,2048]{1,0:T(8,128)(2,1)S(1)} collective-permute-done((bf16[64,2048]{1,0:T(8,128)(2,1)S(1)}, bf16[64,2048]{1,0:T(8,128)(2,1)S(1)}, u32[]{:S(2)}, u32[]{:S(2)}) %collective-permute-start.46) | collective-permute-done | bytes 262176 | tf_op jit(solution)/shard_map/ppermute | solution.py:36
  147.0 4.7 %collective-permute-done.49 = bf16[128,2048]{1,0:T(8,128)(2,1)S(1)} collective-permute-done((bf16[128,2048]{1,0:T(8,128)(2,1)S(1)}, bf16[128,2048]{1,0:T(8,128)(2,1)S(1)}, u32[]{:S(2)}, u32[]{:S(2)}) %collective-permute-start.49) | collective-permute-done | bytes 524320 | tf_op jit(solution)/shard_map/ppermute | solution.py:36
  154.2 2.5 %collective-permute-start.52 = (bf16[32,2048]{1,0:T(8,128)(2,1)S(1)}, bf16[32,2048]{1,0:T(8,128)(2,1)S(1)}, u32[]{:S(2)}, u32[]{:S(2)}) collective-permute-start(bf16[32,2048]{1,0:T(8,128)(2,1)S(1)} %get-tuple-element.123), channel_id=1, source_target_pairs={{0,24},{4,28},{8,0},{12,4},{16,8},{20,12},{24,16},{28,20},{1,25},{... | collective-permute-start | bytes 393224 | tf_op jit(solution)/shard_map/ppermute | solution.py:46
  160.3 7.2 %collective-permute-done.51 = bf16[32,2048]{1,0:T(8,128)(2,1)S(1)} collective-permute-done((bf16[32,2048]{1,0:T(8,128)(2,1)S(1)}, bf16[32,2048]{1,0:T(8,128)(2,1)S(1)}, u32[]{:S(2)}, u32[]{:S(2)}) %collective-permute-start.51) | collective-permute-done | bytes 131104 | tf_op jit(solution)/shard_map/ppermute | solution.py:46
  (160 shorter events, 64.2 us)
Async XLA Ops:
  0.0 10.9 %collective-permute-start = (bf16[64,2048]{1,0:T(8,128)(2,1)}, bf16[64,2048]{1,0:T(8,128)(2,1)S(1)}, u32[]{:S(2)}, u32[]{:S(2)}) collective-permute-start(bf16[64,2048]{1,0:T(8,128)(2,1)} %tokens.1), channel_id=1, source_target_pairs={{0,1},{1,0},{2,3},{3,2},{4,5},{5,4},{6,7},{7,6},{8,9},{9,8},{10,11... | collective-permute-start | bytes 786440 | tf_op jit(solution)/shard_map/ppermute | solution.py:36
  5.9 10.4 %collective-permute-start.3 = (bf16[512,2,512]{2,1,0:T(2,128)(2,1)}, bf16[512,2,512]{2,1,0:T(2,128)(2,1)S(1)}, u32[]{:S(2)}, u32[]{:S(2)}) collective-permute-start(bf16[512,2,512]{2,1,0:T(2,128)(2,1)} %get-tuple-element.56), channel_id=1, source_target_pairs={{0,1},{1,0},{2,3},{3,2},{4,5},{5,4},{6,7},{7,6},{8,9},{9,8},{10,11... | collective-permute-start | bytes 3145736 | tf_op jit(solution)/shard_map/ppermute | solution.py:36
  6.2 14.5 %collective-permute-start.5 = (bf16[512,2,512]{2,1,0:T(2,128)(2,1)}, bf16[512,2,512]{2,1,0:T(2,128)(2,1)S(1)}, u32[]{:S(2)}, u32[]{:S(2)}) collective-permute-start(bf16[512,2,512]{2,1,0:T(2,128)(2,1)} %get-tuple-element.53), channel_id=1, source_target_pairs={{0,1},{1,0},{2,3},{3,2},{4,5},{5,4},{6,7},{7,6},{8,9},{9,8},{10,11... | collective-permute-start | bytes 3145736 | tf_op jit(solution)/shard_map/ppermute | solution.py:36
  15.9 10.7 %collective-permute-start.4 = (bf16[256,256]{1,0:T(8,128)(2,1)}, bf16[256,256]{1,0:T(8,128)(2,1)S(1)}, u32[]{:S(2)}, u32[]{:S(2)}) collective-permute-start(bf16[256,256]{1,0:T(8,128)(2,1)} %get-tuple-element.63.q), channel_id=1, source_target_pairs={{0,2},{1,3},{2,0},{3,1},{4,6},{5,7},{6,4},{7,5},{8,10},{9,11},{10,... | collective-permute-start | bytes 393224 | tf_op jit(solution)/shard_map/ppermute | solution.py:36
  53.3 11.4 %collective-permute-start.12 = (bf16[32,2176]{1,0:T(8,128)(2,1)S(1)}, bf16[32,2176]{1,0:T(8,128)(2,1)S(1)}, u32[]{:S(2)}, u32[]{:S(2)}) collective-permute-start(bf16[32,2176]{1,0:T(8,128)(2,1)S(1)} %get-tuple-element.70), channel_id=1, source_target_pairs={{0,16},{4,20},{8,24},{12,28},{16,0},{20,4},{24,8},{28,12},{1,17},{... | collective-permute-start | bytes 417800 | tf_op jit(solution)/shard_map/ppermute | solution.py:46
  53.4 11.4 %collective-permute-start.13 = (bf16[32,2176]{1,0:T(8,128)(2,1)S(1)}, bf16[32,2176]{1,0:T(8,128)(2,1)S(1)}, u32[]{:S(2)}, u32[]{:S(2)}) collective-permute-start(bf16[32,2176]{1,0:T(8,128)(2,1)S(1)} %get-tuple-element.70), channel_id=1, source_target_pairs={{0,8},{4,12},{8,16},{12,20},{16,24},{20,28},{24,0},{28,4},{1,9},{5... | collective-permute-start | bytes 417800 | tf_op jit(solution)/shard_map/ppermute | solution.py:46
  64.8 14.1 %collective-permute-start.15 = (bf16[128,2176]{1,0:T(8,128)(2,1)S(1)}, bf16[128,2176]{1,0:T(8,128)(2,1)S(1)}, u32[]{:S(2)}, u32[]{:S(2)}) collective-permute-start(bf16[128,2176]{1,0:T(8,128)(2,1)S(1)} %constant_dynamic-update-slice_fusion.refs_0_), channel_id=1, source_target_pairs={{0,4},{4,0},{8,12},{12,8},{16,20},{20,16},{24,28},{28,24},{1,5},{5... | collective-permute-start | bytes 1671176 | tf_op jit(solution)/shard_map/ppermute | solution.py:36
  66.3 13.7 %collective-permute-start.14 = (bf16[128,2176]{1,0:T(8,128)(2,1)S(1)}, bf16[128,2176]{1,0:T(8,128)(2,1)S(1)}, u32[]{:S(2)}, u32[]{:S(2)}) collective-permute-start(bf16[128,2176]{1,0:T(8,128)(2,1)S(1)} %constant_dynamic-update-slice_fusion.refs_0_), channel_id=1, source_target_pairs={{0,2},{1,3},{2,0},{3,1},{4,6},{5,7},{6,4},{7,5},{8,10},{9,11},{10,... | collective-permute-start | bytes 1671176 | tf_op jit(solution)/shard_map/ppermute | solution.py:36
  66.8 17.1 %collective-permute-start.24 = (bf16[32,2176]{1,0:T(8,128)(2,1)S(1)}, bf16[32,2176]{1,0:T(8,128)(2,1)S(1)}, u32[]{:S(2)}, u32[]{:S(2)}) collective-permute-start(bf16[32,2176]{1,0:T(8,128)(2,1)S(1)} %get-tuple-element.84), channel_id=1, source_target_pairs={{0,24},{4,28},{8,0},{12,4},{16,8},{20,12},{24,16},{28,20},{1,25},{... | collective-permute-start | bytes 417800 | tf_op jit(solution)/shard_map/ppermute | solution.py:46
  68.2 15.8 %collective-permute-start.25 = (bf16[32,2176]{1,0:T(8,128)(2,1)S(1)}, bf16[32,2176]{1,0:T(8,128)(2,1)S(1)}, u32[]{:S(2)}, u32[]{:S(2)}) collective-permute-start(bf16[32,2176]{1,0:T(8,128)(2,1)S(1)} %get-tuple-element.84), channel_id=1, source_target_pairs={{0,16},{4,20},{8,24},{12,28},{16,0},{20,4},{24,8},{28,12},{1,17},{... | collective-permute-start | bytes 417800 | tf_op jit(solution)/shard_map/ppermute | solution.py:46
  69.5 15.1 %collective-permute-start.26 = (bf16[32,2176]{1,0:T(8,128)(2,1)S(1)}, bf16[32,2176]{1,0:T(8,128)(2,1)S(1)}, u32[]{:S(2)}, u32[]{:S(2)}) collective-permute-start(bf16[32,2176]{1,0:T(8,128)(2,1)S(1)} %get-tuple-element.84), channel_id=1, source_target_pairs={{0,8},{4,12},{8,16},{12,20},{16,24},{20,28},{24,0},{28,4},{1,9},{5... | collective-permute-start | bytes 417800 | tf_op jit(solution)/shard_map/ppermute | solution.py:46
  87.0 12.8 %collective-permute-start.27 = (bf16[128,2176]{1,0:T(8,128)(2,1)S(1)}, bf16[128,2176]{1,0:T(8,128)(2,1)S(1)}, u32[]{:S(2)}, u32[]{:S(2)}) collective-permute-start(bf16[128,2176]{1,0:T(8,128)(2,1)S(1)} %constant_dynamic-update-slice_fusion.4.refs_0_), channel_id=1, source_target_pairs={{0,2},{1,3},{2,0},{3,1},{4,6},{5,7},{6,4},{7,5},{8,10},{9,11},{10,... | collective-permute-start | bytes 1671176 | tf_op jit(solution)/shard_map/ppermute | solution.py:36
  88.0 13.0 %collective-permute-start.28 = (bf16[128,2176]{1,0:T(8,128)(2,1)S(1)}, bf16[128,2176]{1,0:T(8,128)(2,1)S(1)}, u32[]{:S(2)}, u32[]{:S(2)}) collective-permute-start(bf16[128,2176]{1,0:T(8,128)(2,1)S(1)} %constant_dynamic-update-slice_fusion.4.refs_0_), channel_id=1, source_target_pairs={{0,4},{4,0},{8,12},{12,8},{16,20},{20,16},{24,28},{28,24},{1,5},{5... | collective-permute-start | bytes 1671176 | tf_op jit(solution)/shard_map/ppermute | solution.py:36
  101.0 15.3 %collective-permute-start.19 = (bf16[384,2048]{1,0:T(8,128)(2,1)S(1)}, bf16[384,2048]{1,0:T(8,128)(2,1)S(1)}, u32[]{:S(2)}, u32[]{:S(2)}) collective-permute-start(bf16[384,2048]{1,0:T(8,128)(2,1)S(1)} %experts.6), channel_id=1, source_target_pairs={{0,1},{1,0},{2,3},{3,2},{4,5},{5,4},{6,7},{7,6},{8,9},{9,8},{10,11... | collective-permute-start | bytes 4718600 | tf_op jit(solution)/shard_map/ppermute | solution.py:36
  113.4 12.1 %collective-permute-start.40 = (bf16[384,2048]{1,0:T(8,128)(2,1)S(1)}, bf16[384,2048]{1,0:T(8,128)(2,1)S(1)}, u32[]{:S(2)}, u32[]{:S(2)}) collective-permute-start(bf16[384,2048]{1,0:T(8,128)(2,1)S(1)} %experts.9), channel_id=1, source_target_pairs={{0,1},{1,0},{2,3},{3,2},{4,5},{5,4},{6,7},{7,6},{8,9},{9,8},{10,11... | collective-permute-start | bytes 4718600 | tf_op jit(solution)/shard_map/ppermute | solution.py:36
  120.9 21.2 %collective-permute-start.33 = (bf16[128,2048]{1,0:T(8,128)(2,1)S(1)}, bf16[128,2048]{1,0:T(8,128)(2,1)S(1)}, u32[]{:S(2)}, u32[]{:S(2)}) collective-permute-start(bf16[128,2048]{1,0:T(8,128)(2,1)S(1)} %pad_maximum_fusion.1), channel_id=1, source_target_pairs={{0,2},{1,3},{2,0},{3,1},{4,6},{5,7},{6,4},{7,5},{8,10},{9,11},{10,... | collective-permute-start | bytes 1572872 | tf_op jit(solution)/shard_map/ppermute | solution.py:36
  121.8 20.3 %collective-permute-start.31 = (bf16[128,2048]{1,0:T(8,128)(2,1)S(1)}, bf16[128,2048]{1,0:T(8,128)(2,1)S(1)}, u32[]{:S(2)}, u32[]{:S(2)}) collective-permute-start(bf16[128,2048]{1,0:T(8,128)(2,1)S(1)} %pad_maximum_fusion), channel_id=1, source_target_pairs={{0,4},{4,0},{8,12},{12,8},{16,20},{20,16},{24,28},{28,24},{1,5},{5... | collective-permute-start | bytes 1572872 | tf_op jit(solution)/shard_map/ppermute | solution.py:36
  123.0 16.3 %collective-permute-start.46 = (bf16[64,2048]{1,0:T(8,128)(2,1)S(1)}, bf16[64,2048]{1,0:T(8,128)(2,1)S(1)}, u32[]{:S(2)}, u32[]{:S(2)}) collective-permute-start(bf16[64,2048]{1,0:T(8,128)(2,1)S(1)} %get-tuple-element.120), channel_id=1, source_target_pairs={{0,2},{1,3},{2,0},{3,1},{4,6},{5,7},{6,4},{7,5},{8,10},{9,11},{10,... | collective-permute-start | bytes 786440 | tf_op jit(solution)/shard_map/ppermute | solution.py:36
  124.0 15.9 %collective-permute-start.48 = (bf16[64,2048]{1,0:T(8,128)(2,1)S(1)}, bf16[64,2048]{1,0:T(8,128)(2,1)S(1)}, u32[]{:S(2)}, u32[]{:S(2)}) collective-permute-start(bf16[64,2048]{1,0:T(8,128)(2,1)S(1)} %get-tuple-element.121), channel_id=1, source_target_pairs={{0,4},{4,0},{8,12},{12,8},{16,20},{20,16},{24,28},{28,24},{1,5},{5... | collective-permute-start | bytes 786440 | tf_op jit(solution)/shard_map/ppermute | solution.py:36
  140.1 11.5 %collective-permute-start.49 = (bf16[128,2048]{1,0:T(8,128)(2,1)S(1)}, bf16[128,2048]{1,0:T(8,128)(2,1)S(1)}, u32[]{:S(2)}, u32[]{:S(2)}) collective-permute-start(bf16[128,2048]{1,0:T(8,128)(2,1)S(1)} %pad_maximum_fusion.3), channel_id=1, source_target_pairs={{0,2},{1,3},{2,0},{3,1},{4,6},{5,7},{6,4},{7,5},{8,10},{9,11},{10,... | collective-permute-start | bytes 1572872 | tf_op jit(solution)/shard_map/ppermute | solution.py:36
  141.5 11.2 %collective-permute-start.47 = (bf16[128,2048]{1,0:T(8,128)(2,1)S(1)}, bf16[128,2048]{1,0:T(8,128)(2,1)S(1)}, u32[]{:S(2)}, u32[]{:S(2)}) collective-permute-start(bf16[128,2048]{1,0:T(8,128)(2,1)S(1)} %pad_maximum_fusion.2), channel_id=1, source_target_pairs={{0,4},{4,0},{8,12},{12,8},{16,20},{20,16},{24,28},{28,24},{1,5},{5... | collective-permute-start | bytes 1572872 | tf_op jit(solution)/shard_map/ppermute | solution.py:36
  142.4 10.6 %collective-permute-start.36 = (bf16[32,2048]{1,0:T(8,128)(2,1)S(1)}, bf16[32,2048]{1,0:T(8,128)(2,1)S(1)}, u32[]{:S(2)}, u32[]{:S(2)}) collective-permute-start(bf16[32,2048]{1,0:T(8,128)(2,1)S(1)} %get-tuple-element.115), channel_id=1, source_target_pairs={{0,24},{4,28},{8,0},{12,4},{16,8},{20,12},{24,16},{28,20},{1,25},{... | collective-permute-start | bytes 393224 | tf_op jit(solution)/shard_map/ppermute | solution.py:46
  143.9 10.3 %collective-permute-start.35 = (bf16[32,2048]{1,0:T(8,128)(2,1)S(1)}, bf16[32,2048]{1,0:T(8,128)(2,1)S(1)}, u32[]{:S(2)}, u32[]{:S(2)}) collective-permute-start(bf16[32,2048]{1,0:T(8,128)(2,1)S(1)} %get-tuple-element.116), channel_id=1, source_target_pairs={{0,16},{4,20},{8,24},{12,28},{16,0},{20,4},{24,8},{28,12},{1,17},{... | collective-permute-start | bytes 393224 | tf_op jit(solution)/shard_map/ppermute | solution.py:46
  156.7 10.8 %collective-permute-start.51 = (bf16[32,2048]{1,0:T(8,128)(2,1)S(1)}, bf16[32,2048]{1,0:T(8,128)(2,1)S(1)}, u32[]{:S(2)}, u32[]{:S(2)}) collective-permute-start(bf16[32,2048]{1,0:T(8,128)(2,1)S(1)} %get-tuple-element.124), channel_id=1, source_target_pairs={{0,16},{4,20},{8,24},{12,28},{16,0},{20,4},{24,8},{28,12},{1,17},{... | collective-permute-start | bytes 393224 | tf_op jit(solution)/shard_map/ppermute | solution.py:46
  (36 other events, 206.0 us)

commit v5 on v4

--- a/solution.py
+++ b/solution.py
@@ -422,11 +422,11 @@
     half = n // 2
     rows = n // (lax.axis_size("tok") // 2)
     here, by_y, by_x = (total[i * n : (i + 1) * n] for i in range(3))
-    to_x = join_rows(add_bf(by_x[:half], got[0]), by_x[half:])
-    to_y = join_rows(by_y[:half], add_bf(by_y[half:], got[1]))
-    got_x, got_y = move_x(to_x), move_y(to_y)
-    total = functools.reduce(jnp.add, [v.astype(F32) for v in (here, got_x, got_y)])
-    return total[:rows], total[rows:].astype(BF)
+    first = add_bf(by_x[:half], got[0])
+    to_x = join_rows(first[rows:], by_x[half:])
+    to_y = join_rows(by_y[rows:half], add_bf(by_y[half:], got[1]))
+    rest = add_bf(here[rows:], move_x(to_x), move_y(to_y))
+    return rest, (here[:rows], by_y[:rows], first[:rows]), (to_x, to_y)
 
 
 def hold_kernel(count, *refs):
@@ -497,19 +497,21 @@
     their_corner_b = [move_c(v) for v in corner_b]
     sent_corner, kept_corner = expert_part(group, their_corner_b + corner_b, held, 2)
     got_b = reduce_corner(kept_corner, sent_corner)
-    sums_a = reduce_rest(chip_a, got_a)
+    rest_a, own_rows_a, _ = reduce_rest(chip_a, got_a)
     chip_b = add_bf(kept_b, move_c(sent_b))
-    sums_b = reduce_rest(chip_b, got_b)
-
-    outs, landed = [], []
-    for i, (own, rest) in enumerate((sums_a, sums_b)):
-        total = resid[i * rows : (i + 1) * rows] + own
-        if landed:
-            rest = after(rest, *landed)
+    rest_b, own_rows_b, moving_b = reduce_rest(chip_b, got_b)
+
+    def along_z(rest):
         parts = [rest[(k - 1) * rows : k * rows] for k in range(1, depth)]
-        landed = [to_z(part, k) for k, part in zip(range(1, depth), parts)]
-        outs.append(functools.reduce(jnp.add, [v.astype(F32) for v in landed], total).astype(BF))
-    return jnp.concatenate(outs, axis=0)
+        return [to_z(part, k) for k, part in zip(range(1, depth), parts)]
+
+    landed_a = along_z(after(rest_a, *moving_b))
+    landed_b = along_z(rest_b)
+    here, to_y, to_x = (join_rows(u, v) for u, v in zip(own_rows_a, own_rows_b))
+    to_y, to_x = after((to_y, to_x), rest_b)
+    landed = [join_rows(u, v) for u, v in zip(landed_a, landed_b)]
+    landed += [here, move_y(to_y), move_x(to_x)]
+    return functools.reduce(jnp.add, [v.astype(F32) for v in landed], resid).astype(BF)
 
 
 def request_layout(lengths_row, index):

time: 169 us -> 163 us (0.964)
  waiting for transfers between devices: 69.1 us -> 55.1 us
  starting transfers between devices: 46.3 us -> 55.4 us
    ppermute x41 -> x43, waiting for transfers between devices: 49.3 us -> 39.7 us  [swap(): return lax.ppermute(value, axis, [(i, i ^ bit) for i in range(size)])]
    ppermute x41 -> x43, starting transfers between devices: 27.4 us -> 32.8 us  [swap(): return lax.ppermute(value, axis, [(i, i ^ bit) for i in range(size)])]
    ppermute x12, waiting for transfers between devices: 19.8 us -> 15.4 us  [from_z(): lax.ppermute(value, 'tok', [(i, (i - 2 * k) % size) for i in range(size)])]
    ppermute x12, starting transfers between devices: 18.9 us -> 22.6 us  [from_z(): lax.ppermute(value, 'tok', [(i, (i - 2 * k) % size) for i in range(size)])]
  transfers between devices with their start and end apart: 53 -> 55, of which waited for: 25 -> 25; matrix products, arithmetic and copies ran while one was open for 3% -> 3% of each run, Pallas kernels for 26% -> 27%
where the time goes in v5:
time: 163 us
  starting transfers between devices  55.4 us (34%)
  waiting for transfers between devices  55.1 us (34%)
  Pallas kernels  46.4 us (28%)
  other arithmetic  4.28 us (3%)
    ppermute x43, waiting for transfers between devices, swap(): return lax.ppermute(value, axis, [(i, i ^ bit) for i in range(size)])  39.7 us
    ppermute x43, starting transfers between devices, swap(): return lax.ppermute(value, axis, [(i, i ^ bit) for i in range(size)])  32.8 us
    ppermute x12, starting transfers between devices, from_z(): lax.ppermute(value, 'tok', [(i, (i - 2 * k) % size) for i in range(size)])  22.6 us
    pallas_call x6, Pallas kernels, expert_part(): pl.pallas_call(functools.partial(expert_kernel, sizes, tile), grid_spec=p...  16.1 us
    ppermute x12, waiting for transfers between devices, from_z(): lax.ppermute(value, 'tok', [(i, (i - 2 * k) % size) for i in range(size)])  15.4 us
    pallas_call x2, Pallas kernels, attend_own(): pl.pallas_call(own_kernel, grid_spec=pltpu.PrefetchScalarGridSpec(num_sca...  8.45 us
    pallas_call x2, Pallas kernels, attend_guest(): pl.pallas_call(guest_kernel, grid_spec=pltpu.PrefetchScalarGridSpec(num_s...  8.22 us
    pallas_call x2, Pallas kernels, hold(): pl.pallas_call(functools.partial(hold_kernel, count), out_shape=[jax.Shap...  5.86 us
  transfers between devices with their start and end apart: 55, of which 25 were waited for; matrix products, arithmetic and copies ran while one was open for 3% of the time, Pallas kernels for 27%

profile of v5, /device:TPU:0, one launch (start us, length us, event | category | flops | bytes accessed | tf_op | source)
XLA Modules:
  0.0 162.9 jit_solution(6266542223923260632)
XLA Ops:
  0.0 3.0 %collective-permute-start.1 = (bf16[64,2048]{1,0:T(8,128)(2,1)}, bf16[64,2048]{1,0:T(8,128)(2,1)S(1)}, u32[]{:S(2)}, u32[]{:S(2)}) collective-permute-start(bf16[64,2048]{1,0:T(8,128)(2,1)} %tokens.1), channel_id=1, source_target_pairs={{0,2},{1,3},{2,0},{3,1},{4,6},{5,7},{6,4},{7,5},{8,10},{9,11},{10,... | collective-permute-start | bytes 786440 | tf_op jit(solution)/shard_map/ppermute | solution.py:36
  3.0 3.0 %stage.1 = (bf16[512,2,512]{2,1,0:T(2,128)(2,1)}, bf16[512,2,512]{2,1,0:T(2,128)(2,1)}) custom-call(s32[1]{0:T(128)} %bitcast.who.group.me, bf16[1,512,2,2048]{3,2,1,0:T(2,128)(2,1)} %kv_here.7), custom_call_target="tpu_custom_call" | custom-call | bytes 4194304 | tf_op jit(solution)/shard_map/stage/pallas_call | solution.py:77
  7.1 2.9 %hold.2.w = bf16[3,2048,512]{2,1,0:T(8,128)(2,1)S(1)} custom-call(bf16[3,2048,512]{2,1,0:T(8,128)(2,1)} %bitcast.15), custom_call_target="tpu_custom_call" | custom-call | bytes 12582912 | tf_op jit(solution)/shard_map/hold/pallas_call | solution.py:453
  11.6 2.5 %project.1 = (bf16[256,256]{1,0:T(8,128)(2,1)}, bf16[256,256]{1,0:T(8,128)(2,1)}, bf16[256,512]{1,0:T(8,128)(2,1)S(1)}, bf16[256,512]{1,0:T(8,128)(2,1)S(1)}) custom-call(bf16[64,2048]{1,0:T(8,128)(2,1)S(1)} %copy-done.1, bf16[64,2048]{1,0:T(8,128)(2,1)S(1)} %collective-permute-done.t1, bf16[64,2048]{1,0:T(8,128)(2,1)S(1)} %collective-permute-done.1.t2, ...), custom_call_target="tpu_custom_call" | custom-call | flops 1610612736 | bytes 6291456 | tf_op jit(solution)/shard_map/project/pallas_call | solution.py:118
  16.3 4.2 %attend_own.2 = (f32[256,256]{1,0:T(8,128)S(1)}, f32[256,128]{1,0:T(8,128)S(1)}) custom-call(s32[1]{0:T(128)} %bitcast.who.group.me, bf16[256,256]{1,0:T(8,128)(2,1)} %get-tuple-element.57.q, bf16[1,512,2,2048]{3,2,1,0:T(2,128)(2,1)} %kv_here.7, bf16[512,2,512]{2,1,0:T(2,128)(2,1)S(1)} %collective-permute-done.3.kv_there, ...), custom_call_target="tpu_custom_call" | custom-call | flops 335544320 | bytes 1310720 | tf_op jit(solution)/shard_map/attend_own/pallas_call | solution.py:198
  20.6 4.0 %attend_guest.3 = bf16[256,384]{1,0:T(8,128)(2,1)S(1)} custom-call(s32[1]{0:T(128)S(6)} %xor.16.group, bf16[256,256]{1,0:T(8,128)(2,1)S(1)} %collective-permute-done.6.q, bf16[1,512,2,2048]{3,2,1,0:T(2,128)(2,1)} %kv_here.7, bf16[512,2,512]{2,1,0:T(2,128)(2,1)S(1)} %collective-permute-done.5.kv_there), custom_call_target="tpu_custom_call" | custom-call | flops 268435456 | bytes 1048576 | tf_op jit(solution)/shard_map/attend_guest/pallas_call | solution.py:222
  25.9 4.2 %attend_guest.2 = bf16[256,384]{1,0:T(8,128)(2,1)S(1)} custom-call(s32[1]{0:T(128)S(6)} %xor.16.group, bf16[256,256]{1,0:T(8,128)(2,1)S(1)} %collective-permute-done.4.q, bf16[1,512,2,2048]{3,2,1,0:T(2,128)(2,1)} %kv_here.7, bf16[512,2,512]{2,1,0:T(2,128)(2,1)S(1)} %collective-permute-done.5.kv_there), custom_call_target="tpu_custom_call" | custom-call | flops 268435456 | bytes 1048576 | tf_op jit(solution)/shard_map/attend_guest/pallas_call | solution.py:222
  31.2 4.2 %attend_own.3 = (f32[256,256]{1,0:T(8,128)S(1)}, f32[256,128]{1,0:T(8,128)S(1)}) custom-call(s32[1]{0:T(128)} %bitcast.who.group.me, bf16[256,256]{1,0:T(8,128)(2,1)} %get-tuple-element.65.q, bf16[1,512,2,2048]{3,2,1,0:T(2,128)(2,1)} %kv_here.7, bf16[512,2,512]{2,1,0:T(2,128)(2,1)S(1)} %collective-permute-done.3.kv_there, ...), custom_call_target="tpu_custom_call" | custom-call | flops 335544320 | bytes 1310720 | tf_op jit(solution)/shard_map/attend_own/pallas_call | solution.py:198
  41.6 6.7 %collective-permute-done.10.arrived = bf16[64,2048]{1,0:T(8,128)(2,1)S(1)} collective-permute-done((bf16[64,2048]{1,0:T(8,128)(2,1)S(1)}, bf16[64,2048]{1,0:T(8,128)(2,1)S(1)}, u32[]{:S(2)}, u32[]{:S(2)}) %collective-permute-start.10) | collective-permute-done | bytes 262176 | tf_op jit(solution)/shard_map/ppermute | solution.py:36
  49.0 3.6 %collective-permute-start.11 = (bf16[32,2176]{1,0:T(8,128)(2,1)S(1)}, bf16[32,2176]{1,0:T(8,128)(2,1)S(1)}, u32[]{:S(2)}, u32[]{:S(2)}) collective-permute-start(bf16[32,2176]{1,0:T(8,128)(2,1)S(1)} %get-tuple-element.72), channel_id=1, source_target_pairs={{0,24},{4,28},{8,0},{12,4},{16,8},{20,12},{24,16},{28,20},{1,25},{... | collective-permute-start | bytes 417800 | tf_op jit(solution)/shard_map/ppermute | solution.py:46
  53.7 3.0 %collective-permute-done.11 = bf16[32,2176]{1,0:T(8,128)(2,1)S(1)} collective-permute-done((bf16[32,2176]{1,0:T(8,128)(2,1)S(1)}, bf16[32,2176]{1,0:T(8,128)(2,1)S(1)}, u32[]{:S(2)}, u32[]{:S(2)}) %collective-permute-start.11) | collective-permute-done | bytes 139296 | tf_op jit(solution)/shard_map/ppermute | solution.py:46
  56.8 7.3 %collective-permute-done.12 = bf16[32,2176]{1,0:T(8,128)(2,1)S(1)} collective-permute-done((bf16[32,2176]{1,0:T(8,128)(2,1)S(1)}, bf16[32,2176]{1,0:T(8,128)(2,1)S(1)}, u32[]{:S(2)}, u32[]{:S(2)}) %collective-permute-start.12) | collective-permute-done | bytes 139296 | tf_op jit(solution)/shard_map/ppermute | solution.py:46
  71.5 6.7 %collective-permute-done.15.refs_2_ = bf16[128,2176]{1,0:T(8,128)(2,1)S(1)} collective-permute-done((bf16[128,2176]{1,0:T(8,128)(2,1)S(1)}, bf16[128,2176]{1,0:T(8,128)(2,1)S(1)}, u32[]{:S(2)}, u32[]{:S(2)}) %collective-permute-start.15) | collective-permute-done | bytes 557088 | tf_op jit(solution)/shard_map/ppermute | solution.py:36
  81.0 3.0 %hold.3 = (bf16[2,2048,256]{2,1,0:T(8,128)(2,1)S(1)}, bf16[2,2048,256]{2,1,0:T(8,128)(2,1)S(1)}, bf16[2,256,2048]{2,1,0:T(8,128)(2,1)S(1)}) custom-call(bf16[2,2048,256]{2,1,0:T(8,128)(2,1)} %refs_0_, bf16[2,2048,256]{2,1,0:T(8,128)(2,1)} %refs_1_, bf16[2,256,2048]{2,1,0:T(8,128)(2,1)} %refs_2_), custom_call_target="tpu_custom_call" | custom-call | bytes 12582912 | tf_op jit(solution)/shard_map/hold/pallas_call | solution.py:453
  89.4 2.9 %experts.6 = bf16[384,2048]{1,0:T(8,128)(2,1)S(1)} custom-call(s32[1]{0:T(128)} %bitcast.9.group, bf16[128,2176]{1,0:T(8,128)(2,1)S(1)} %collective-permute-done.16.refs_0_, bf16[128,2176]{1,0:T(8,128)(2,1)S(1)} %collective-permute-done.17.refs_1_, bf16[128,2176]{1,0:T(8,128)(2,1)S(1)} %collective-permute-done.18.refs_2_, ...), custom_call_target="tpu_custom_call" | custom-call | flops 2415919104 | bytes 9437184 | tf_op jit(solution)/shard_map/experts/pallas_call | solution.py:382
  92.3 2.9 %experts.7 = bf16[384,2048]{1,0:T(8,128)(2,1)S(1)} custom-call(s32[1]{0:T(128)} %bitcast.9.group, bf16[128,2176]{1,0:T(8,128)(2,1)S(1)} %constant_dynamic-update-slice_fusion.refs_0_, bf16[128,2176]{1,0:T(8,128)(2,1)S(1)} %collective-permute-done.14.refs_1_, bf16[128,2176]{1,0:T(8,128)(2,1)S(1)} %collective-permute-done.15.refs_2_, ...), custom_call_target="tpu_custom_call" | custom-call | flops 2415919104 | bytes 9437184 | tf_op jit(solution)/shard_map/experts/pallas_call | solution.py:382
  102.9 2.9 %experts.9 = bf16[384,2048]{1,0:T(8,128)(2,1)S(1)} custom-call(s32[1]{0:T(128)} %bitcast.9.group, bf16[128,2176]{1,0:T(8,128)(2,1)S(1)} %collective-permute-done.34.refs_0_, bf16[128,2176]{1,0:T(8,128)(2,1)S(1)} %collective-permute-done.35.refs_1_, bf16[128,2176]{1,0:T(8,128)(2,1)S(1)} %collective-permute-done.36.refs_2_, ...), custom_call_target="tpu_custom_call" | custom-call | flops 2415919104 | bytes 9437184 | tf_op jit(solution)/shard_map/experts/pallas_call | solution.py:382
  105.8 2.9 %experts.10 = bf16[384,2048]{1,0:T(8,128)(2,1)S(1)} custom-call(s32[1]{0:T(128)} %bitcast.9.group, bf16[128,2176]{1,0:T(8,128)(2,1)S(1)} %constant_dynamic-update-slice_fusion.4.refs_0_, bf16[128,2176]{1,0:T(8,128)(2,1)S(1)} %collective-permute-done.27.refs_1_, bf16[128,2176]{1,0:T(8,128)(2,1)S(1)} %collective-permute-done.28.refs_2_, ...), custom_call_target="tpu_custom_call" | custom-call | flops 2415919104 | bytes 9437184 | tf_op jit(solution)/shard_map/experts/pallas_call | solution.py:382
  112.9 2.3 %experts.11 = (bf16[128,2048]{1,0:T(8,128)(2,1)S(1)}, bf16[128,2048]{1,0:T(8,128)(2,1)S(1)}) custom-call(s32[1]{0:T(128)} %bitcast.9.group, bf16[64,2176]{1,0:T(8,128)(2,1)S(1)} %collective-permute-done.40.refs_0_, bf16[64,2176]{1,0:T(8,128)(2,1)S(1)} %collective-permute-done.41.refs_1_, bf16[64,2176]{1,0:T(8,128)(2,1)S(1)} %collective-permute-done.38.refs_2_, ...), custom_call_target="tpu_custom_call" | custom-call | flops 1610612736 | bytes 8388608 | tf_op jit(solution)/shard_map/experts/pallas_call | solution.py:382
  116.4 3.0 %collective-permute-done.30 = bf16[64,2048]{1,0:T(8,128)(2,1)S(1)} collective-permute-done((bf16[64,2048]{1,0:T(8,128)(2,1)S(1)}, bf16[64,2048]{1,0:T(8,128)(2,1)S(1)}, u32[]{:S(2)}, u32[]{:S(2)}) %collective-permute-start.30) | collective-permute-done | bytes 262176 | tf_op jit(solution)/shard_map/ppermute | solution.py:36
  124.8 7.6 %collective-permute-done.31 = bf16[96,2048]{1,0:T(8,128)(2,1)S(1)} collective-permute-done((bf16[96,2048]{1,0:T(8,128)(2,1)S(1)}, bf16[96,2048]{1,0:T(8,128)(2,1)S(1)}, u32[]{:S(2)}, u32[]{:S(2)}) %collective-permute-start.31) | collective-permute-done | bytes 393248 | tf_op jit(solution)/shard_map/ppermute | solution.py:36
  134.1 2.3 %collective-permute-done.43 = bf16[64,2048]{1,0:T(8,128)(2,1)S(1)} collective-permute-done((bf16[64,2048]{1,0:T(8,128)(2,1)S(1)}, bf16[64,2048]{1,0:T(8,128)(2,1)S(1)}, u32[]{:S(2)}, u32[]{:S(2)}) %collective-permute-start.43) | collective-permute-done | bytes 262176 | tf_op jit(solution)/shard_map/ppermute | solution.py:36
  141.8 2.8 %collective-permute-start.51 = (bf16[32,2048]{1,0:T(8,128)(2,1)S(1)}, bf16[32,2048]{1,0:T(8,128)(2,1)S(1)}, u32[]{:S(2)}, u32[]{:S(2)}) collective-permute-start(bf16[32,2048]{1,0:T(8,128)(2,1)S(1)} %get-tuple-element.121), channel_id=1, source_target_pairs={{0,24},{4,28},{8,0},{12,4},{16,8},{20,12},{24,16},{28,20},{1,25},{... | collective-permute-start | bytes 393224 | tf_op jit(solution)/shard_map/ppermute | solution.py:46
  153.2 5.2 %collective-permute-start.52 = (bf16[32,2048]{1,0:T(8,128)(2,1)S(1)}, bf16[32,2048]{1,0:T(8,128)(2,1)S(1)}, u32[]{:S(2)}, u32[]{:S(2)}) collective-permute-start(bf16[32,2048]{1,0:T(8,128)(2,1)S(1)} %get-tuple-element.124), channel_id=1, source_target_pairs={{0,24},{4,28},{8,0},{12,4},{16,8},{20,12},{24,16},{28,20},{1,25},{... | collective-permute-start | bytes 393224 | tf_op jit(solution)/shard_map/ppermute | solution.py:46
  (168 shorter events, 69.1 us)
Async XLA Ops:
  0.0 10.0 %collective-permute-start.1 = (bf16[64,2048]{1,0:T(8,128)(2,1)}, bf16[64,2048]{1,0:T(8,128)(2,1)S(1)}, u32[]{:S(2)}, u32[]{:S(2)}) collective-permute-start(bf16[64,2048]{1,0:T(8,128)(2,1)} %tokens.1), channel_id=1, source_target_pairs={{0,2},{1,3},{2,0},{3,1},{4,6},{5,7},{6,4},{7,5},{8,10},{9,11},{10,... | collective-permute-start | bytes 786440 | tf_op jit(solution)/shard_map/ppermute | solution.py:36
  5.9 10.3 %collective-permute-start.3 = (bf16[512,2,512]{2,1,0:T(2,128)(2,1)}, bf16[512,2,512]{2,1,0:T(2,128)(2,1)S(1)}, u32[]{:S(2)}, u32[]{:S(2)}) collective-permute-start(bf16[512,2,512]{2,1,0:T(2,128)(2,1)} %get-tuple-element.58), channel_id=1, source_target_pairs={{0,1},{1,0},{2,3},{3,2},{4,5},{5,4},{6,7},{7,6},{8,9},{9,8},{10,11... | collective-permute-start | bytes 3145736 | tf_op jit(solution)/shard_map/ppermute | solution.py:36
  6.5 14.1 %collective-permute-start.5 = (bf16[512,2,512]{2,1,0:T(2,128)(2,1)}, bf16[512,2,512]{2,1,0:T(2,128)(2,1)S(1)}, u32[]{:S(2)}, u32[]{:S(2)}) collective-permute-start(bf16[512,2,512]{2,1,0:T(2,128)(2,1)} %get-tuple-element.55), channel_id=1, source_target_pairs={{0,1},{1,0},{2,3},{3,2},{4,5},{5,4},{6,7},{7,6},{8,9},{9,8},{10,11... | collective-permute-start | bytes 3145736 | tf_op jit(solution)/shard_map/ppermute | solution.py:36
  15.2 10.7 %collective-permute-start.4 = (bf16[256,256]{1,0:T(8,128)(2,1)}, bf16[256,256]{1,0:T(8,128)(2,1)S(1)}, u32[]{:S(2)}, u32[]{:S(2)}) collective-permute-start(bf16[256,256]{1,0:T(8,128)(2,1)} %get-tuple-element.65.q), channel_id=1, source_target_pairs={{0,2},{1,3},{2,0},{3,1},{4,6},{5,7},{6,4},{7,5},{8,10},{9,11},{10,... | collective-permute-start | bytes 393224 | tf_op jit(solution)/shard_map/ppermute | solution.py:36
  52.6 11.4 %collective-permute-start.12 = (bf16[32,2176]{1,0:T(8,128)(2,1)S(1)}, bf16[32,2176]{1,0:T(8,128)(2,1)S(1)}, u32[]{:S(2)}, u32[]{:S(2)}) collective-permute-start(bf16[32,2176]{1,0:T(8,128)(2,1)S(1)} %get-tuple-element.72), channel_id=1, source_target_pairs={{0,16},{4,20},{8,24},{12,28},{16,0},{20,4},{24,8},{28,12},{1,17},{... | collective-permute-start | bytes 417800 | tf_op jit(solution)/shard_map/ppermute | solution.py:46
  52.7 11.3 %collective-permute-start.13 = (bf16[32,2176]{1,0:T(8,128)(2,1)S(1)}, bf16[32,2176]{1,0:T(8,128)(2,1)S(1)}, u32[]{:S(2)}, u32[]{:S(2)}) collective-permute-start(bf16[32,2176]{1,0:T(8,128)(2,1)S(1)} %get-tuple-element.72), channel_id=1, source_target_pairs={{0,8},{4,12},{8,16},{12,20},{16,24},{20,28},{24,0},{28,4},{1,9},{5... | collective-permute-start | bytes 417800 | tf_op jit(solution)/shard_map/ppermute | solution.py:46
  64.1 14.0 %collective-permute-start.15 = (bf16[128,2176]{1,0:T(8,128)(2,1)S(1)}, bf16[128,2176]{1,0:T(8,128)(2,1)S(1)}, u32[]{:S(2)}, u32[]{:S(2)}) collective-permute-start(bf16[128,2176]{1,0:T(8,128)(2,1)S(1)} %constant_dynamic-update-slice_fusion.refs_0_), channel_id=1, source_target_pairs={{0,4},{4,0},{8,12},{12,8},{16,20},{20,16},{24,28},{28,24},{1,5},{5... | collective-permute-start | bytes 1671176 | tf_op jit(solution)/shard_map/ppermute | solution.py:36
  65.7 13.7 %collective-permute-start.14 = (bf16[128,2176]{1,0:T(8,128)(2,1)S(1)}, bf16[128,2176]{1,0:T(8,128)(2,1)S(1)}, u32[]{:S(2)}, u32[]{:S(2)}) collective-permute-start(bf16[128,2176]{1,0:T(8,128)(2,1)S(1)} %constant_dynamic-update-slice_fusion.refs_0_), channel_id=1, source_target_pairs={{0,2},{1,3},{2,0},{3,1},{4,6},{5,7},{6,4},{7,5},{8,10},{9,11},{10,... | collective-permute-start | bytes 1671176 | tf_op jit(solution)/shard_map/ppermute | solution.py:36
  66.8 17.2 %collective-permute-start.24 = (bf16[32,2176]{1,0:T(8,128)(2,1)S(1)}, bf16[32,2176]{1,0:T(8,128)(2,1)S(1)}, u32[]{:S(2)}, u32[]{:S(2)}) collective-permute-start(bf16[32,2176]{1,0:T(8,128)(2,1)S(1)} %get-tuple-element.86), channel_id=1, source_target_pairs={{0,24},{4,28},{8,0},{12,4},{16,8},{20,12},{24,16},{28,20},{1,25},{... | collective-permute-start | bytes 417800 | tf_op jit(solution)/shard_map/ppermute | solution.py:46
  68.2 15.8 %collective-permute-start.25 = (bf16[32,2176]{1,0:T(8,128)(2,1)S(1)}, bf16[32,2176]{1,0:T(8,128)(2,1)S(1)}, u32[]{:S(2)}, u32[]{:S(2)}) collective-permute-start(bf16[32,2176]{1,0:T(8,128)(2,1)S(1)} %get-tuple-element.86), channel_id=1, source_target_pairs={{0,16},{4,20},{8,24},{12,28},{16,0},{20,4},{24,8},{28,12},{1,17},{... | collective-permute-start | bytes 417800 | tf_op jit(solution)/shard_map/ppermute | solution.py:46
  69.4 15.1 %collective-permute-start.26 = (bf16[32,2176]{1,0:T(8,128)(2,1)S(1)}, bf16[32,2176]{1,0:T(8,128)(2,1)S(1)}, u32[]{:S(2)}, u32[]{:S(2)}) collective-permute-start(bf16[32,2176]{1,0:T(8,128)(2,1)S(1)} %get-tuple-element.86), channel_id=1, source_target_pairs={{0,8},{4,12},{8,16},{12,20},{16,24},{20,28},{24,0},{28,4},{1,9},{5... | collective-permute-start | bytes 417800 | tf_op jit(solution)/shard_map/ppermute | solution.py:46
  86.4 13.3 %collective-permute-start.27 = (bf16[128,2176]{1,0:T(8,128)(2,1)S(1)}, bf16[128,2176]{1,0:T(8,128)(2,1)S(1)}, u32[]{:S(2)}, u32[]{:S(2)}) collective-permute-start(bf16[128,2176]{1,0:T(8,128)(2,1)S(1)} %constant_dynamic-update-slice_fusion.4.refs_0_), channel_id=1, source_target_pairs={{0,2},{1,3},{2,0},{3,1},{4,6},{5,7},{6,4},{7,5},{8,10},{9,11},{10,... | collective-permute-start | bytes 1671176 | tf_op jit(solution)/shard_map/ppermute | solution.py:36
  87.5 12.8 %collective-permute-start.28 = (bf16[128,2176]{1,0:T(8,128)(2,1)S(1)}, bf16[128,2176]{1,0:T(8,128)(2,1)S(1)}, u32[]{:S(2)}, u32[]{:S(2)}) collective-permute-start(bf16[128,2176]{1,0:T(8,128)(2,1)S(1)} %constant_dynamic-update-slice_fusion.4.refs_0_), channel_id=1, source_target_pairs={{0,4},{4,0},{8,12},{12,8},{16,20},{20,16},{24,28},{28,24},{1,5},{5... | collective-permute-start | bytes 1671176 | tf_op jit(solution)/shard_map/ppermute | solution.py:36
  100.4 15.4 %collective-permute-start.19 = (bf16[384,2048]{1,0:T(8,128)(2,1)S(1)}, bf16[384,2048]{1,0:T(8,128)(2,1)S(1)}, u32[]{:S(2)}, u32[]{:S(2)}) collective-permute-start(bf16[384,2048]{1,0:T(8,128)(2,1)S(1)} %experts.6), channel_id=1, source_target_pairs={{0,1},{1,0},{2,3},{3,2},{4,5},{5,4},{6,7},{7,6},{8,9},{9,8},{10,11... | collective-permute-start | bytes 4718600 | tf_op jit(solution)/shard_map/ppermute | solution.py:36
  112.9 20.5 %collective-permute-start.37 = (bf16[384,2048]{1,0:T(8,128)(2,1)S(1)}, bf16[384,2048]{1,0:T(8,128)(2,1)S(1)}, u32[]{:S(2)}, u32[]{:S(2)}) collective-permute-start(bf16[384,2048]{1,0:T(8,128)(2,1)S(1)} %experts.9), channel_id=1, source_target_pairs={{0,1},{1,0},{2,3},{3,2},{4,5},{5,4},{6,7},{7,6},{8,9},{9,8},{10,11... | collective-permute-start | bytes 4718600 | tf_op jit(solution)/shard_map/ppermute | solution.py:36
  120.3 12.1 %collective-permute-start.31 = (bf16[96,2048]{1,0:T(8,128)(2,1)S(1)}, bf16[96,2048]{1,0:T(8,128)(2,1)S(1)}, u32[]{:S(2)}, u32[]{:S(2)}) collective-permute-start(bf16[96,2048]{1,0:T(8,128)(2,1)S(1)} %pad_maximum_fusion), channel_id=1, source_target_pairs={{0,4},{4,0},{8,12},{12,8},{16,20},{20,16},{24,28},{28,24},{1,5},{5... | collective-permute-start | bytes 1179656 | tf_op jit(solution)/shard_map/ppermute | solution.py:36
  121.1 12.1 %collective-permute-start.33 = (bf16[96,2048]{1,0:T(8,128)(2,1)S(1)}, bf16[96,2048]{1,0:T(8,128)(2,1)S(1)}, u32[]{:S(2)}, u32[]{:S(2)}) collective-permute-start(bf16[96,2048]{1,0:T(8,128)(2,1)S(1)} %pad_maximum_fusion.1), channel_id=1, source_target_pairs={{0,2},{1,3},{2,0},{3,1},{4,6},{5,7},{6,4},{7,5},{8,10},{9,11},{10,... | collective-permute-start | bytes 1179656 | tf_op jit(solution)/shard_map/ppermute | solution.py:36
  122.3 14.0 %collective-permute-start.43 = (bf16[64,2048]{1,0:T(8,128)(2,1)S(1)}, bf16[64,2048]{1,0:T(8,128)(2,1)S(1)}, u32[]{:S(2)}, u32[]{:S(2)}) collective-permute-start(bf16[64,2048]{1,0:T(8,128)(2,1)S(1)} %get-tuple-element.120), channel_id=1, source_target_pairs={{0,2},{1,3},{2,0},{3,1},{4,6},{5,7},{6,4},{7,5},{8,10},{9,11},{10,... | collective-permute-start | bytes 786440 | tf_op jit(solution)/shard_map/ppermute | solution.py:36
  123.5 12.9 %collective-permute-start.44 = (bf16[64,2048]{1,0:T(8,128)(2,1)S(1)}, bf16[64,2048]{1,0:T(8,128)(2,1)S(1)}, u32[]{:S(2)}, u32[]{:S(2)}) collective-permute-start(bf16[64,2048]{1,0:T(8,128)(2,1)S(1)} %get-tuple-element.119), channel_id=1, source_target_pairs={{0,4},{4,0},{8,12},{12,8},{16,20},{20,16},{24,28},{28,24},{1,5},{5... | collective-permute-start | bytes 786440 | tf_op jit(solution)/shard_map/ppermute | solution.py:36
  139.2 9.8 %collective-permute-start.45 = (bf16[32,2048]{1,0:T(8,128)(2,1)S(1)}, bf16[32,2048]{1,0:T(8,128)(2,1)S(1)}, u32[]{:S(2)}, u32[]{:S(2)}) collective-permute-start(bf16[32,2048]{1,0:T(8,128)(2,1)S(1)} %get-tuple-element.123), channel_id=1, source_target_pairs={{0,8},{4,12},{8,16},{12,20},{16,24},{20,28},{24,0},{28,4},{1,9},{5... | collective-permute-start | bytes 393224 | tf_op jit(solution)/shard_map/ppermute | solution.py:46
  139.8 12.9 %collective-permute-start.49 = (bf16[32,2048]{1,0:T(8,128)(2,1)S(1)}, bf16[32,2048]{1,0:T(8,128)(2,1)S(1)}, u32[]{:S(2)}, u32[]{:S(2)}) collective-permute-start(bf16[32,2048]{1,0:T(8,128)(2,1)S(1)} %get-tuple-element.122), channel_id=1, source_target_pairs={{0,16},{4,20},{8,24},{12,28},{16,0},{20,4},{24,8},{28,12},{1,17},{... | collective-permute-start | bytes 393224 | tf_op jit(solution)/shard_map/ppermute | solution.py:46
  141.8 11.4 %collective-permute-start.51 = (bf16[32,2048]{1,0:T(8,128)(2,1)S(1)}, bf16[32,2048]{1,0:T(8,128)(2,1)S(1)}, u32[]{:S(2)}, u32[]{:S(2)}) collective-permute-start(bf16[32,2048]{1,0:T(8,128)(2,1)S(1)} %get-tuple-element.121), channel_id=1, source_target_pairs={{0,24},{4,28},{8,0},{12,4},{16,8},{20,12},{24,16},{28,20},{1,25},{... | collective-permute-start | bytes 393224 | tf_op jit(solution)/shard_map/ppermute | solution.py:46
  147.3 14.7 %collective-permute-start.53 = (bf16[64,2048]{1,0:T(8,128)(2,1)S(1)}, bf16[64,2048]{1,0:T(8,128)(2,1)S(1)}, u32[]{:S(2)}, u32[]{:S(2)}) collective-permute-start(bf16[64,2048]{1,0:T(8,128)(2,1)S(1)} %pad_maximum_fusion.4), channel_id=1, source_target_pairs={{0,2},{1,3},{2,0},{3,1},{4,6},{5,7},{6,4},{7,5},{8,10},{9,11},{10,... | collective-permute-start | bytes 786440 | tf_op jit(solution)/shard_map/ppermute | solution.py:36
  148.4 13.5 %collective-permute-start.54 = (bf16[64,2048]{1,0:T(8,128)(2,1)S(1)}, bf16[64,2048]{1,0:T(8,128)(2,1)S(1)}, u32[]{:S(2)}, u32[]{:S(2)}) collective-permute-start(bf16[64,2048]{1,0:T(8,128)(2,1)S(1)} %pad_maximum_fusion.5), channel_id=1, source_target_pairs={{0,4},{4,0},{8,12},{12,8},{16,20},{20,16},{24,28},{28,24},{1,5},{5... | collective-permute-start | bytes 786440 | tf_op jit(solution)/shard_map/ppermute | solution.py:36
  (38 other events, 220.7 us)

commit v6 on v5

--- a/solution.py
+++ b/solution.py
@@ -497,8 +497,8 @@
     their_corner_b = [move_c(v) for v in corner_b]
     sent_corner, kept_corner = expert_part(group, their_corner_b + corner_b, held, 2)
     got_b = reduce_corner(kept_corner, sent_corner)
-    rest_a, own_rows_a, _ = reduce_rest(chip_a, got_a)
     chip_b = add_bf(kept_b, move_c(sent_b))
+    rest_a, own_rows_a, _ = reduce_rest(chip_a, after(got_a, chip_b))
     rest_b, own_rows_b, moving_b = reduce_rest(chip_b, got_b)
 
     def along_z(rest):

time: 163 us -> 161 us (0.988)
  waiting for transfers between devices: 55.1 us -> 50.8 us
    ppermute x43, waiting for transfers between devices: 39.7 us -> 36.1 us  [swap(): return lax.ppermute(value, axis, [(i, i ^ bit) for i in range(size)])]
  transfers between devices with their start and end apart: 55 -> 55, of which waited for: 25 -> 23; matrix products, arithmetic and copies ran while one was open for 3% -> 3% of each run, Pallas kernels for 27% -> 28%
where the time goes in v6:
time: 161 us; the launch traced here: 160 us
  starting transfers between devices  56.3 us (35%)
  waiting for transfers between devices  50.8 us (32%)
  Pallas kernels  46.4 us (29%)
  other arithmetic  4.39 us (3%)
    ppermute x43, waiting for transfers between devices, swap(): return lax.ppermute(value, axis, [(i, i ^ bit) for i in range(size)])  36.1 us
    ppermute x43, starting transfers between devices, swap(): return lax.ppermute(value, axis, [(i, i ^ bit) for i in range(size)])  33.5 us
    ppermute x12, starting transfers between devices, from_z(): lax.ppermute(value, 'tok', [(i, (i - 2 * k) % size) for i in range(size)])  22.8 us
    pallas_call x6, Pallas kernels, expert_part(): pl.pallas_call(functools.partial(expert_kernel, sizes, tile), grid_spec=p...  16.1 us
    ppermute x12, waiting for transfers between devices, from_z(): lax.ppermute(value, 'tok', [(i, (i - 2 * k) % size) for i in range(size)])  14.7 us
    pallas_call x2, Pallas kernels, attend_own(): pl.pallas_call(own_kernel, grid_spec=pltpu.PrefetchScalarGridSpec(num_sca...  8.45 us
    pallas_call x2, Pallas kernels, attend_guest(): pl.pallas_call(guest_kernel, grid_spec=pltpu.PrefetchScalarGridSpec(num_s...  8.22 us
    pallas_call x2, Pallas kernels, hold(): pl.pallas_call(functools.partial(hold_kernel, count), out_shape=[jax.Shap...  5.86 us
  transfers between devices with their start and end apart: 55, of which 23 were waited for; matrix products, arithmetic and copies ran while one was open for 3% of the time, Pallas kernels for 28%

profile of v6, /device:TPU:0, one launch (start us, length us, event | category | flops | bytes accessed | tf_op | source)
XLA Modules:
  0.0 159.7 jit_solution(12105175704559879559)
XLA Ops:
  0.0 3.0 %collective-permute-start.1 = (bf16[64,2048]{1,0:T(8,128)(2,1)}, bf16[64,2048]{1,0:T(8,128)(2,1)S(1)}, u32[]{:S(2)}, u32[]{:S(2)}) collective-permute-start(bf16[64,2048]{1,0:T(8,128)(2,1)} %tokens.1), channel_id=1, source_target_pairs={{0,2},{1,3},{2,0},{3,1},{4,6},{5,7},{6,4},{7,5},{8,10},{9,11},{10,... | collective-permute-start | bytes 786440 | tf_op jit(solution)/shard_map/ppermute | solution.py:36
  3.0 3.0 %stage.1 = (bf16[512,2,512]{2,1,0:T(2,128)(2,1)}, bf16[512,2,512]{2,1,0:T(2,128)(2,1)}) custom-call(s32[1]{0:T(128)} %bitcast.who.group.me, bf16[1,512,2,2048]{3,2,1,0:T(2,128)(2,1)} %kv_here.7), custom_call_target="tpu_custom_call" | custom-call | bytes 4194304 | tf_op jit(solution)/shard_map/stage/pallas_call | solution.py:77
  7.1 2.9 %hold.2.w = bf16[3,2048,512]{2,1,0:T(8,128)(2,1)S(1)} custom-call(bf16[3,2048,512]{2,1,0:T(8,128)(2,1)} %bitcast.15), custom_call_target="tpu_custom_call" | custom-call | bytes 12582912 | tf_op jit(solution)/shard_map/hold/pallas_call | solution.py:453
  11.6 2.5 %project.1 = (bf16[256,256]{1,0:T(8,128)(2,1)}, bf16[256,256]{1,0:T(8,128)(2,1)}, bf16[256,512]{1,0:T(8,128)(2,1)S(1)}, bf16[256,512]{1,0:T(8,128)(2,1)S(1)}) custom-call(bf16[64,2048]{1,0:T(8,128)(2,1)S(1)} %copy-done.1, bf16[64,2048]{1,0:T(8,128)(2,1)S(1)} %collective-permute-done.t1, bf16[64,2048]{1,0:T(8,128)(2,1)S(1)} %collective-permute-done.1.t2, ...), custom_call_target="tpu_custom_call" | custom-call | flops 1610612736 | bytes 6291456 | tf_op jit(solution)/shard_map/project/pallas_call | solution.py:118
  16.3 4.2 %attend_own.2 = (f32[256,256]{1,0:T(8,128)S(1)}, f32[256,128]{1,0:T(8,128)S(1)}) custom-call(s32[1]{0:T(128)} %bitcast.who.group.me, bf16[256,256]{1,0:T(8,128)(2,1)} %get-tuple-element.59.q, bf16[1,512,2,2048]{3,2,1,0:T(2,128)(2,1)} %kv_here.7, bf16[512,2,512]{2,1,0:T(2,128)(2,1)S(1)} %collective-permute-done.3.kv_there, ...), custom_call_target="tpu_custom_call" | custom-call | flops 335544320 | bytes 1310720 | tf_op jit(solution)/shard_map/attend_own/pallas_call | solution.py:198
  20.6 4.0 %attend_guest.3 = bf16[256,384]{1,0:T(8,128)(2,1)S(1)} custom-call(s32[1]{0:T(128)S(6)} %xor.16.group, bf16[256,256]{1,0:T(8,128)(2,1)S(1)} %collective-permute-done.6.q, bf16[1,512,2,2048]{3,2,1,0:T(2,128)(2,1)} %kv_here.7, bf16[512,2,512]{2,1,0:T(2,128)(2,1)S(1)} %collective-permute-done.5.kv_there), custom_call_target="tpu_custom_call" | custom-call | flops 268435456 | bytes 1048576 | tf_op jit(solution)/shard_map/attend_guest/pallas_call | solution.py:222
  25.9 4.2 %attend_guest.2 = bf16[256,384]{1,0:T(8,128)(2,1)S(1)} custom-call(s32[1]{0:T(128)S(6)} %xor.16.group, bf16[256,256]{1,0:T(8,128)(2,1)S(1)} %collective-permute-done.4.q, bf16[1,512,2,2048]{3,2,1,0:T(2,128)(2,1)} %kv_here.7, bf16[512,2,512]{2,1,0:T(2,128)(2,1)S(1)} %collective-permute-done.5.kv_there), custom_call_target="tpu_custom_call" | custom-call | flops 268435456 | bytes 1048576 | tf_op jit(solution)/shard_map/attend_guest/pallas_call | solution.py:222
  31.2 4.2 %attend_own.3 = (f32[256,256]{1,0:T(8,128)S(1)}, f32[256,128]{1,0:T(8,128)S(1)}) custom-call(s32[1]{0:T(128)} %bitcast.who.group.me, bf16[256,256]{1,0:T(8,128)(2,1)} %get-tuple-element.67.q, bf16[1,512,2,2048]{3,2,1,0:T(2,128)(2,1)} %kv_here.7, bf16[512,2,512]{2,1,0:T(2,128)(2,1)S(1)} %collective-permute-done.3.kv_there, ...), custom_call_target="tpu_custom_call" | custom-call | flops 335544320 | bytes 1310720 | tf_op jit(solution)/shard_map/attend_own/pallas_call | solution.py:198
  41.6 6.7 %collective-permute-done.10.arrived = bf16[64,2048]{1,0:T(8,128)(2,1)S(1)} collective-permute-done((bf16[64,2048]{1,0:T(8,128)(2,1)S(1)}, bf16[64,2048]{1,0:T(8,128)(2,1)S(1)}, u32[]{:S(2)}, u32[]{:S(2)}) %collective-permute-start.10) | collective-permute-done | bytes 262176 | tf_op jit(solution)/shard_map/ppermute | solution.py:36
  49.0 3.6 %collective-permute-start.11 = (bf16[32,2176]{1,0:T(8,128)(2,1)S(1)}, bf16[32,2176]{1,0:T(8,128)(2,1)S(1)}, u32[]{:S(2)}, u32[]{:S(2)}) collective-permute-start(bf16[32,2176]{1,0:T(8,128)(2,1)S(1)} %get-tuple-element.74), channel_id=1, source_target_pairs={{0,24},{4,28},{8,0},{12,4},{16,8},{20,12},{24,16},{28,20},{1,25},{... | collective-permute-start | bytes 417800 | tf_op jit(solution)/shard_map/ppermute | solution.py:46
  53.7 3.0 %collective-permute-done.11 = bf16[32,2176]{1,0:T(8,128)(2,1)S(1)} collective-permute-done((bf16[32,2176]{1,0:T(8,128)(2,1)S(1)}, bf16[32,2176]{1,0:T(8,128)(2,1)S(1)}, u32[]{:S(2)}, u32[]{:S(2)}) %collective-permute-start.11) | collective-permute-done | bytes 139296 | tf_op jit(solution)/shard_map/ppermute | solution.py:46
  56.8 7.3 %collective-permute-done.12 = bf16[32,2176]{1,0:T(8,128)(2,1)S(1)} collective-permute-done((bf16[32,2176]{1,0:T(8,128)(2,1)S(1)}, bf16[32,2176]{1,0:T(8,128)(2,1)S(1)}, u32[]{:S(2)}, u32[]{:S(2)}) %collective-permute-start.12) | collective-permute-done | bytes 139296 | tf_op jit(solution)/shard_map/ppermute | solution.py:46
  71.5 6.7 %collective-permute-done.15.refs_2_ = bf16[128,2176]{1,0:T(8,128)(2,1)S(1)} collective-permute-done((bf16[128,2176]{1,0:T(8,128)(2,1)S(1)}, bf16[128,2176]{1,0:T(8,128)(2,1)S(1)}, u32[]{:S(2)}, u32[]{:S(2)}) %collective-permute-start.15) | collective-permute-done | bytes 557088 | tf_op jit(solution)/shard_map/ppermute | solution.py:36
  81.0 3.0 %hold.3 = (bf16[2,2048,256]{2,1,0:T(8,128)(2,1)S(1)}, bf16[2,2048,256]{2,1,0:T(8,128)(2,1)S(1)}, bf16[2,256,2048]{2,1,0:T(8,128)(2,1)S(1)}) custom-call(bf16[2,2048,256]{2,1,0:T(8,128)(2,1)} %refs_0_, bf16[2,2048,256]{2,1,0:T(8,128)(2,1)} %refs_1_, bf16[2,256,2048]{2,1,0:T(8,128)(2,1)} %refs_2_), custom_call_target="tpu_custom_call" | custom-call | bytes 12582912 | tf_op jit(solution)/shard_map/hold/pallas_call | solution.py:453
  89.4 2.9 %experts.6 = bf16[384,2048]{1,0:T(8,128)(2,1)S(1)} custom-call(s32[1]{0:T(128)} %bitcast.9.group, bf16[128,2176]{1,0:T(8,128)(2,1)S(1)} %collective-permute-done.16.refs_0_, bf16[128,2176]{1,0:T(8,128)(2,1)S(1)} %collective-permute-done.17.refs_1_, bf16[128,2176]{1,0:T(8,128)(2,1)S(1)} %collective-permute-done.18.refs_2_, ...), custom_call_target="tpu_custom_call" | custom-call | flops 2415919104 | bytes 9437184 | tf_op jit(solution)/shard_map/experts/pallas_call | solution.py:382
  92.3 2.9 %experts.7 = bf16[384,2048]{1,0:T(8,128)(2,1)S(1)} custom-call(s32[1]{0:T(128)} %bitcast.9.group, bf16[128,2176]{1,0:T(8,128)(2,1)S(1)} %constant_dynamic-update-slice_fusion.refs_0_, bf16[128,2176]{1,0:T(8,128)(2,1)S(1)} %collective-permute-done.14.refs_1_, bf16[128,2176]{1,0:T(8,128)(2,1)S(1)} %collective-permute-done.15.refs_2_, ...), custom_call_target="tpu_custom_call" | custom-call | flops 2415919104 | bytes 9437184 | tf_op jit(solution)/shard_map/experts/pallas_call | solution.py:382
  102.9 2.9 %experts.9 = bf16[384,2048]{1,0:T(8,128)(2,1)S(1)} custom-call(s32[1]{0:T(128)} %bitcast.9.group, bf16[128,2176]{1,0:T(8,128)(2,1)S(1)} %collective-permute-done.32.refs_0_, bf16[128,2176]{1,0:T(8,128)(2,1)S(1)} %collective-permute-done.33.refs_1_, bf16[128,2176]{1,0:T(8,128)(2,1)S(1)} %collective-permute-done.34.refs_2_, ...), custom_call_target="tpu_custom_call" | custom-call | flops 2415919104 | bytes 9437184 | tf_op jit(solution)/shard_map/experts/pallas_call | solution.py:382
  105.8 2.9 %experts.10 = bf16[384,2048]{1,0:T(8,128)(2,1)S(1)} custom-call(s32[1]{0:T(128)} %bitcast.9.group, bf16[128,2176]{1,0:T(8,128)(2,1)S(1)} %constant_dynamic-update-slice_fusion.4.refs_0_, bf16[128,2176]{1,0:T(8,128)(2,1)S(1)} %collective-permute-done.27.refs_1_, bf16[128,2176]{1,0:T(8,128)(2,1)S(1)} %collective-permute-done.28.refs_2_, ...), custom_call_target="tpu_custom_call" | custom-call | flops 2415919104 | bytes 9437184 | tf_op jit(solution)/shard_map/experts/pallas_call | solution.py:382
  112.9 2.3 %experts.11 = (bf16[128,2048]{1,0:T(8,128)(2,1)S(1)}, bf16[128,2048]{1,0:T(8,128)(2,1)S(1)}) custom-call(s32[1]{0:T(128)} %bitcast.9.group, bf16[64,2176]{1,0:T(8,128)(2,1)S(1)} %collective-permute-done.40.refs_0_, bf16[64,2176]{1,0:T(8,128)(2,1)S(1)} %collective-permute-done.41.refs_1_, bf16[64,2176]{1,0:T(8,128)(2,1)S(1)} %collective-permute-done.38.refs_2_, ...), custom_call_target="tpu_custom_call" | custom-call | flops 1610612736 | bytes 8388608 | tf_op jit(solution)/shard_map/experts/pallas_call | solution.py:382
  122.8 3.9 %collective-permute-done.43 = bf16[64,2048]{1,0:T(8,128)(2,1)S(1)} collective-permute-done((bf16[64,2048]{1,0:T(8,128)(2,1)S(1)}, bf16[64,2048]{1,0:T(8,128)(2,1)S(1)}, u32[]{:S(2)}, u32[]{:S(2)}) %collective-permute-start.43) | collective-permute-done | bytes 262176 | tf_op jit(solution)/shard_map/ppermute | solution.py:36
  130.5 5.6 %collective-permute-done.36 = bf16[96,2048]{1,0:T(8,128)(2,1)S(1)} collective-permute-done((bf16[96,2048]{1,0:T(8,128)(2,1)S(1)}, bf16[96,2048]{1,0:T(8,128)(2,1)S(1)}, u32[]{:S(2)}, u32[]{:S(2)}) %collective-permute-start.36) | collective-permute-done | bytes 393248 | tf_op jit(solution)/shard_map/ppermute | solution.py:36
  139.0 2.8 %collective-permute-start.51 = (bf16[32,2048]{1,0:T(8,128)(2,1)S(1)}, bf16[32,2048]{1,0:T(8,128)(2,1)S(1)}, u32[]{:S(2)}, u32[]{:S(2)}) collective-permute-start(bf16[32,2048]{1,0:T(8,128)(2,1)S(1)} %get-tuple-element.125), channel_id=1, source_target_pairs={{0,24},{4,28},{8,0},{12,4},{16,8},{20,12},{24,16},{28,20},{1,25},{... | collective-permute-start | bytes 393224 | tf_op jit(solution)/shard_map/ppermute | solution.py:46
  149.7 4.6 %collective-permute-start.52 = (bf16[32,2048]{1,0:T(8,128)(2,1)S(1)}, bf16[32,2048]{1,0:T(8,128)(2,1)S(1)}, u32[]{:S(2)}, u32[]{:S(2)}) collective-permute-start(bf16[32,2048]{1,0:T(8,128)(2,1)S(1)} %get-tuple-element.128), channel_id=1, source_target_pairs={{0,24},{4,28},{8,0},{12,4},{16,8},{20,12},{24,16},{28,20},{1,25},{... | collective-permute-start | bytes 393224 | tf_op jit(solution)/shard_map/ppermute | solution.py:46
  154.6 3.9 %collective-permute-done.50 = bf16[32,2048]{1,0:T(8,128)(2,1)S(1)} collective-permute-done((bf16[32,2048]{1,0:T(8,128)(2,1)S(1)}, bf16[32,2048]{1,0:T(8,128)(2,1)S(1)}, u32[]{:S(2)}, u32[]{:S(2)}) %collective-permute-start.50) | collective-permute-done | bytes 131104 | tf_op jit(solution)/shard_map/ppermute | solution.py:46
  (168 shorter events, 65.9 us)
Async XLA Ops:
  0.0 10.0 %collective-permute-start.1 = (bf16[64,2048]{1,0:T(8,128)(2,1)}, bf16[64,2048]{1,0:T(8,128)(2,1)S(1)}, u32[]{:S(2)}, u32[]{:S(2)}) collective-permute-start(bf16[64,2048]{1,0:T(8,128)(2,1)} %tokens.1), channel_id=1, source_target_pairs={{0,2},{1,3},{2,0},{3,1},{4,6},{5,7},{6,4},{7,5},{8,10},{9,11},{10,... | collective-permute-start | bytes 786440 | tf_op jit(solution)/shard_map/ppermute | solution.py:36
  5.9 10.3 %collective-permute-start.3 = (bf16[512,2,512]{2,1,0:T(2,128)(2,1)}, bf16[512,2,512]{2,1,0:T(2,128)(2,1)S(1)}, u32[]{:S(2)}, u32[]{:S(2)}) collective-permute-start(bf16[512,2,512]{2,1,0:T(2,128)(2,1)} %get-tuple-element.60), channel_id=1, source_target_pairs={{0,1},{1,0},{2,3},{3,2},{4,5},{5,4},{6,7},{7,6},{8,9},{9,8},{10,11... | collective-permute-start | bytes 3145736 | tf_op jit(solution)/shard_map/ppermute | solution.py:36
  6.5 14.1 %collective-permute-start.5 = (bf16[512,2,512]{2,1,0:T(2,128)(2,1)}, bf16[512,2,512]{2,1,0:T(2,128)(2,1)S(1)}, u32[]{:S(2)}, u32[]{:S(2)}) collective-permute-start(bf16[512,2,512]{2,1,0:T(2,128)(2,1)} %get-tuple-element.57), channel_id=1, source_target_pairs={{0,1},{1,0},{2,3},{3,2},{4,5},{5,4},{6,7},{7,6},{8,9},{9,8},{10,11... | collective-permute-start | bytes 3145736 | tf_op jit(solution)/shard_map/ppermute | solution.py:36
  15.2 10.7 %collective-permute-start.4 = (bf16[256,256]{1,0:T(8,128)(2,1)}, bf16[256,256]{1,0:T(8,128)(2,1)S(1)}, u32[]{:S(2)}, u32[]{:S(2)}) collective-permute-start(bf16[256,256]{1,0:T(8,128)(2,1)} %get-tuple-element.67.q), channel_id=1, source_target_pairs={{0,2},{1,3},{2,0},{3,1},{4,6},{5,7},{6,4},{7,5},{8,10},{9,11},{10,... | collective-permute-start | bytes 393224 | tf_op jit(solution)/shard_map/ppermute | solution.py:36
  52.6 11.4 %collective-permute-start.12 = (bf16[32,2176]{1,0:T(8,128)(2,1)S(1)}, bf16[32,2176]{1,0:T(8,128)(2,1)S(1)}, u32[]{:S(2)}, u32[]{:S(2)}) collective-permute-start(bf16[32,2176]{1,0:T(8,128)(2,1)S(1)} %get-tuple-element.74), channel_id=1, source_target_pairs={{0,16},{4,20},{8,24},{12,28},{16,0},{20,4},{24,8},{28,12},{1,17},{... | collective-permute-start | bytes 417800 | tf_op jit(solution)/shard_map/ppermute | solution.py:46
  52.7 11.3 %collective-permute-start.13 = (bf16[32,2176]{1,0:T(8,128)(2,1)S(1)}, bf16[32,2176]{1,0:T(8,128)(2,1)S(1)}, u32[]{:S(2)}, u32[]{:S(2)}) collective-permute-start(bf16[32,2176]{1,0:T(8,128)(2,1)S(1)} %get-tuple-element.74), channel_id=1, source_target_pairs={{0,8},{4,12},{8,16},{12,20},{16,24},{20,28},{24,0},{28,4},{1,9},{5... | collective-permute-start | bytes 417800 | tf_op jit(solution)/shard_map/ppermute | solution.py:46
  64.1 14.0 %collective-permute-start.15 = (bf16[128,2176]{1,0:T(8,128)(2,1)S(1)}, bf16[128,2176]{1,0:T(8,128)(2,1)S(1)}, u32[]{:S(2)}, u32[]{:S(2)}) collective-permute-start(bf16[128,2176]{1,0:T(8,128)(2,1)S(1)} %constant_dynamic-update-slice_fusion.refs_0_), channel_id=1, source_target_pairs={{0,4},{4,0},{8,12},{12,8},{16,20},{20,16},{24,28},{28,24},{1,5},{5... | collective-permute-start | bytes 1671176 | tf_op jit(solution)/shard_map/ppermute | solution.py:36
  65.7 13.7 %collective-permute-start.14 = (bf16[128,2176]{1,0:T(8,128)(2,1)S(1)}, bf16[128,2176]{1,0:T(8,128)(2,1)S(1)}, u32[]{:S(2)}, u32[]{:S(2)}) collective-permute-start(bf16[128,2176]{1,0:T(8,128)(2,1)S(1)} %constant_dynamic-update-slice_fusion.refs_0_), channel_id=1, source_target_pairs={{0,2},{1,3},{2,0},{3,1},{4,6},{5,7},{6,4},{7,5},{8,10},{9,11},{10,... | collective-permute-start | bytes 1671176 | tf_op jit(solution)/shard_map/ppermute | solution.py:36
  66.8 17.2 %collective-permute-start.24 = (bf16[32,2176]{1,0:T(8,128)(2,1)S(1)}, bf16[32,2176]{1,0:T(8,128)(2,1)S(1)}, u32[]{:S(2)}, u32[]{:S(2)}) collective-permute-start(bf16[32,2176]{1,0:T(8,128)(2,1)S(1)} %get-tuple-element.88), channel_id=1, source_target_pairs={{0,24},{4,28},{8,0},{12,4},{16,8},{20,12},{24,16},{28,20},{1,25},{... | collective-permute-start | bytes 417800 | tf_op jit(solution)/shard_map/ppermute | solution.py:46
  68.2 15.8 %collective-permute-start.25 = (bf16[32,2176]{1,0:T(8,128)(2,1)S(1)}, bf16[32,2176]{1,0:T(8,128)(2,1)S(1)}, u32[]{:S(2)}, u32[]{:S(2)}) collective-permute-start(bf16[32,2176]{1,0:T(8,128)(2,1)S(1)} %get-tuple-element.88), channel_id=1, source_target_pairs={{0,16},{4,20},{8,24},{12,28},{16,0},{20,4},{24,8},{28,12},{1,17},{... | collective-permute-start | bytes 417800 | tf_op jit(solution)/shard_map/ppermute | solution.py:46
  69.4 15.1 %collective-permute-start.26 = (bf16[32,2176]{1,0:T(8,128)(2,1)S(1)}, bf16[32,2176]{1,0:T(8,128)(2,1)S(1)}, u32[]{:S(2)}, u32[]{:S(2)}) collective-permute-start(bf16[32,2176]{1,0:T(8,128)(2,1)S(1)} %get-tuple-element.88), channel_id=1, source_target_pairs={{0,8},{4,12},{8,16},{12,20},{16,24},{20,28},{24,0},{28,4},{1,9},{5... | collective-permute-start | bytes 417800 | tf_op jit(solution)/shard_map/ppermute | solution.py:46
  86.4 13.3 %collective-permute-start.27 = (bf16[128,2176]{1,0:T(8,128)(2,1)S(1)}, bf16[128,2176]{1,0:T(8,128)(2,1)S(1)}, u32[]{:S(2)}, u32[]{:S(2)}) collective-permute-start(bf16[128,2176]{1,0:T(8,128)(2,1)S(1)} %constant_dynamic-update-slice_fusion.4.refs_0_), channel_id=1, source_target_pairs={{0,2},{1,3},{2,0},{3,1},{4,6},{5,7},{6,4},{7,5},{8,10},{9,11},{10,... | collective-permute-start | bytes 1671176 | tf_op jit(solution)/shard_map/ppermute | solution.py:36
  87.5 12.8 %collective-permute-start.28 = (bf16[128,2176]{1,0:T(8,128)(2,1)S(1)}, bf16[128,2176]{1,0:T(8,128)(2,1)S(1)}, u32[]{:S(2)}, u32[]{:S(2)}) collective-permute-start(bf16[128,2176]{1,0:T(8,128)(2,1)S(1)} %constant_dynamic-update-slice_fusion.4.refs_0_), channel_id=1, source_target_pairs={{0,4},{4,0},{8,12},{12,8},{16,20},{20,16},{24,28},{28,24},{1,5},{5... | collective-permute-start | bytes 1671176 | tf_op jit(solution)/shard_map/ppermute | solution.py:36
  100.4 15.4 %collective-permute-start.19 = (bf16[384,2048]{1,0:T(8,128)(2,1)S(1)}, bf16[384,2048]{1,0:T(8,128)(2,1)S(1)}, u32[]{:S(2)}, u32[]{:S(2)}) collective-permute-start(bf16[384,2048]{1,0:T(8,128)(2,1)S(1)} %experts.6), channel_id=1, source_target_pairs={{0,1},{1,0},{2,3},{3,2},{4,5},{5,4},{6,7},{7,6},{8,9},{9,8},{10,11... | collective-permute-start | bytes 4718600 | tf_op jit(solution)/shard_map/ppermute | solution.py:36
  121.0 15.2 %collective-permute-start.36 = (bf16[96,2048]{1,0:T(8,128)(2,1)S(1)}, bf16[96,2048]{1,0:T(8,128)(2,1)S(1)}, u32[]{:S(2)}, u32[]{:S(2)}) collective-permute-start(bf16[96,2048]{1,0:T(8,128)(2,1)S(1)} %pad_maximum_fusion), channel_id=1, source_target_pairs={{0,4},{4,0},{8,12},{12,8},{16,20},{20,16},{24,28},{28,24},{1,5},{5... | collective-permute-start | bytes 1179656 | tf_op jit(solution)/shard_map/ppermute | solution.py:36
  121.6 14.5 %collective-permute-start.37 = (bf16[96,2048]{1,0:T(8,128)(2,1)S(1)}, bf16[96,2048]{1,0:T(8,128)(2,1)S(1)}, u32[]{:S(2)}, u32[]{:S(2)}) collective-permute-start(bf16[96,2048]{1,0:T(8,128)(2,1)S(1)} %pad_maximum_fusion.1), channel_id=1, source_target_pairs={{0,2},{1,3},{2,0},{3,1},{4,6},{5,7},{6,4},{7,5},{8,10},{9,11},{10,... | collective-permute-start | bytes 1179656 | tf_op jit(solution)/shard_map/ppermute | solution.py:36
  127.9 15.8 %collective-permute-start.46 = (bf16[96,2048]{1,0:T(8,128)(2,1)S(1)}, bf16[96,2048]{1,0:T(8,128)(2,1)S(1)}, u32[]{:S(2)}, u32[]{:S(2)}) collective-permute-start(bf16[96,2048]{1,0:T(8,128)(2,1)S(1)} %pad_maximum_fusion.2), channel_id=1, source_target_pairs={{0,4},{4,0},{8,12},{12,8},{16,20},{20,16},{24,28},{28,24},{1,5},{5... | collective-permute-start | bytes 1179656 | tf_op jit(solution)/shard_map/ppermute | solution.py:36
  129.5 14.2 %collective-permute-start.47 = (bf16[96,2048]{1,0:T(8,128)(2,1)S(1)}, bf16[96,2048]{1,0:T(8,128)(2,1)S(1)}, u32[]{:S(2)}, u32[]{:S(2)}) collective-permute-start(bf16[96,2048]{1,0:T(8,128)(2,1)S(1)} %pad_maximum_fusion.3), channel_id=1, source_target_pairs={{0,2},{1,3},{2,0},{3,1},{4,6},{5,7},{6,4},{7,5},{8,10},{9,11},{10,... | collective-permute-start | bytes 1179656 | tf_op jit(solution)/shard_map/ppermute | solution.py:36
  136.3 10.0 %collective-permute-start.45 = (bf16[32,2048]{1,0:T(8,128)(2,1)S(1)}, bf16[32,2048]{1,0:T(8,128)(2,1)S(1)}, u32[]{:S(2)}, u32[]{:S(2)}) collective-permute-start(bf16[32,2048]{1,0:T(8,128)(2,1)S(1)} %get-tuple-element.127), channel_id=1, source_target_pairs={{0,8},{4,12},{8,16},{12,20},{16,24},{20,28},{24,0},{28,4},{1,9},{5... | collective-permute-start | bytes 393224 | tf_op jit(solution)/shard_map/ppermute | solution.py:46
  137.0 10.8 %collective-permute-start.49 = (bf16[32,2048]{1,0:T(8,128)(2,1)S(1)}, bf16[32,2048]{1,0:T(8,128)(2,1)S(1)}, u32[]{:S(2)}, u32[]{:S(2)}) collective-permute-start(bf16[32,2048]{1,0:T(8,128)(2,1)S(1)} %get-tuple-element.126), channel_id=1, source_target_pairs={{0,16},{4,20},{8,24},{12,28},{16,0},{20,4},{24,8},{28,12},{1,17},{... | collective-permute-start | bytes 393224 | tf_op jit(solution)/shard_map/ppermute | solution.py:46
  139.0 10.7 %collective-permute-start.51 = (bf16[32,2048]{1,0:T(8,128)(2,1)S(1)}, bf16[32,2048]{1,0:T(8,128)(2,1)S(1)}, u32[]{:S(2)}, u32[]{:S(2)}) collective-permute-start(bf16[32,2048]{1,0:T(8,128)(2,1)S(1)} %get-tuple-element.125), channel_id=1, source_target_pairs={{0,24},{4,28},{8,0},{12,4},{16,8},{20,12},{24,16},{28,20},{1,25},{... | collective-permute-start | bytes 393224 | tf_op jit(solution)/shard_map/ppermute | solution.py:46
  143.9 14.9 %collective-permute-start.53 = (bf16[64,2048]{1,0:T(8,128)(2,1)S(1)}, bf16[64,2048]{1,0:T(8,128)(2,1)S(1)}, u32[]{:S(2)}, u32[]{:S(2)}) collective-permute-start(bf16[64,2048]{1,0:T(8,128)(2,1)S(1)} %pad_maximum_fusion.4), channel_id=1, source_target_pairs={{0,2},{1,3},{2,0},{3,1},{4,6},{5,7},{6,4},{7,5},{8,10},{9,11},{10,... | collective-permute-start | bytes 786440 | tf_op jit(solution)/shard_map/ppermute | solution.py:36
  145.0 13.7 %collective-permute-start.54 = (bf16[64,2048]{1,0:T(8,128)(2,1)S(1)}, bf16[64,2048]{1,0:T(8,128)(2,1)S(1)}, u32[]{:S(2)}, u32[]{:S(2)}) collective-permute-start(bf16[64,2048]{1,0:T(8,128)(2,1)S(1)} %pad_maximum_fusion.5), channel_id=1, source_target_pairs={{0,4},{4,0},{8,12},{12,8},{16,20},{20,16},{24,28},{28,24},{1,5},{5... | collective-permute-start | bytes 786440 | tf_op jit(solution)/shard_map/ppermute | solution.py:36
  147.8 10.7 %collective-permute-start.50 = (bf16[32,2048]{1,0:T(8,128)(2,1)S(1)}, bf16[32,2048]{1,0:T(8,128)(2,1)S(1)}, u32[]{:S(2)}, u32[]{:S(2)}) collective-permute-start(bf16[32,2048]{1,0:T(8,128)(2,1)S(1)} %get-tuple-element.129), channel_id=1, source_target_pairs={{0,16},{4,20},{8,24},{12,28},{16,0},{20,4},{24,8},{28,12},{1,17},{... | collective-permute-start | bytes 393224 | tf_op jit(solution)/shard_map/ppermute | solution.py:46
  (38 other events, 217.7 us)

commit v7 on v6

--- a/solution.py
+++ b/solution.py
@@ -414,7 +414,8 @@
 def reduce_corner(kept, sent):
     total = add_bf(kept, move_c(sent))
     half = total.shape[0] // 2
-    return move_y(total[:half]), move_x(total[half:])
+    leaving = total[:half], total[half:]
+    return (move_y(leaving[0]), move_x(leaving[1])), leaving
 
 
 def reduce_rest(total, got):
@@ -485,7 +486,7 @@
     sent_corner, kept_corner = expert_part(
         group, after(their_corner_a, kept_a) + corner_a, held, 2
     )
-    got_a = reduce_corner(after(kept_corner, y_b, x_b), sent_corner)
+    got_a, _ = reduce_corner(after(kept_corner, y_b, x_b), sent_corner)
 
     corner_b = [move_y(x_b[:half]), move_x(y_b[half:])]
     main_b = [here_b, y_b, x_b]
@@ -496,9 +497,9 @@
     corner_b = after(corner_b, kept_b)
     their_corner_b = [move_c(v) for v in corner_b]
     sent_corner, kept_corner = expert_part(group, their_corner_b + corner_b, held, 2)
-    got_b = reduce_corner(kept_corner, sent_corner)
+    got_b, leaving_b = reduce_corner(kept_corner, sent_corner)
     chip_b = add_bf(kept_b, move_c(sent_b))
-    rest_a, own_rows_a, _ = reduce_rest(chip_a, after(got_a, chip_b))
+    rest_a, own_rows_a, _ = reduce_rest(chip_a, after(got_a, chip_b, *leaving_b))
     rest_b, own_rows_b, moving_b = reduce_rest(chip_b, got_b)
 
     def along_z(rest):

time: 161 us -> 161 us (level)
  no operation moved by 1% of the time
where the time goes in v7:
time: 161 us; the launch traced here: 160 us
  starting transfers between devices  56.3 us (35%)
  waiting for transfers between devices  50.8 us (32%)
  Pallas kernels  46.4 us (29%)
  other arithmetic  4.39 us (3%)
    ppermute x43, waiting for transfers between devices, swap(): return lax.ppermute(value, axis, [(i, i ^ bit) for i in range(size)])  36.1 us
    ppermute x43, starting transfers between devices, swap(): return lax.ppermute(value, axis, [(i, i ^ bit) for i in range(size)])  33.5 us
    ppermute x12, starting transfers between devices, from_z(): lax.ppermute(value, 'tok', [(i, (i - 2 * k) % size) for i in range(size)])  22.8 us
    pallas_call x6, Pallas kernels, expert_part(): pl.pallas_call(functools.partial(expert_kernel, sizes, tile), grid_spec=p...  16.1 us
    ppermute x12, waiting for transfers between devices, from_z(): lax.ppermute(value, 'tok', [(i, (i - 2 * k) % size) for i in range(size)])  14.7 us
    pallas_call x2, Pallas kernels, attend_own(): pl.pallas_call(own_kernel, grid_spec=pltpu.PrefetchScalarGridSpec(num_sca...  8.45 us
    pallas_call x2, Pallas kernels, attend_guest(): pl.pallas_call(guest_kernel, grid_spec=pltpu.PrefetchScalarGridSpec(num_s...  8.22 us
    pallas_call x2, Pallas kernels, hold(): pl.pallas_call(functools.partial(hold_kernel, count), out_shape=[jax.Shap...  5.86 us
  transfers between devices with their start and end apart: 55, of which 23 were waited for; matrix products, arithmetic and copies ran while one was open for 3% of the time, Pallas kernels for 28%

profile of v7, /device:TPU:0, one launch (start us, length us, event | category | flops | bytes accessed | tf_op | source)
XLA Modules:
  0.0 159.7 jit_solution(12105175704559879559)
XLA Ops:
  0.0 3.0 %collective-permute-start.1 = (bf16[64,2048]{1,0:T(8,128)(2,1)}, bf16[64,2048]{1,0:T(8,128)(2,1)S(1)}, u32[]{:S(2)}, u32[]{:S(2)}) collective-permute-start(bf16[64,2048]{1,0:T(8,128)(2,1)} %tokens.1), channel_id=1, source_target_pairs={{0,2},{1,3},{2,0},{3,1},{4,6},{5,7},{6,4},{7,5},{8,10},{9,11},{10,... | collective-permute-start | bytes 786440 | tf_op jit(solution)/shard_map/ppermute | solution.py:36
  3.0 3.0 %stage.1 = (bf16[512,2,512]{2,1,0:T(2,128)(2,1)}, bf16[512,2,512]{2,1,0:T(2,128)(2,1)}) custom-call(s32[1]{0:T(128)} %bitcast.who.group.me, bf16[1,512,2,2048]{3,2,1,0:T(2,128)(2,1)} %kv_here.7), custom_call_target="tpu_custom_call" | custom-call | bytes 4194304 | tf_op jit(solution)/shard_map/stage/pallas_call | solution.py:77
  7.1 2.9 %hold.2.w = bf16[3,2048,512]{2,1,0:T(8,128)(2,1)S(1)} custom-call(bf16[3,2048,512]{2,1,0:T(8,128)(2,1)} %bitcast.15), custom_call_target="tpu_custom_call" | custom-call | bytes 12582912 | tf_op jit(solution)/shard_map/hold/pallas_call | solution.py:454
  11.6 2.5 %project.1 = (bf16[256,256]{1,0:T(8,128)(2,1)}, bf16[256,256]{1,0:T(8,128)(2,1)}, bf16[256,512]{1,0:T(8,128)(2,1)S(1)}, bf16[256,512]{1,0:T(8,128)(2,1)S(1)}) custom-call(bf16[64,2048]{1,0:T(8,128)(2,1)S(1)} %copy-done.1, bf16[64,2048]{1,0:T(8,128)(2,1)S(1)} %collective-permute-done.t1, bf16[64,2048]{1,0:T(8,128)(2,1)S(1)} %collective-permute-done.1.t2, ...), custom_call_target="tpu_custom_call" | custom-call | flops 1610612736 | bytes 6291456 | tf_op jit(solution)/shard_map/project/pallas_call | solution.py:118
  16.3 4.2 %attend_own.2 = (f32[256,256]{1,0:T(8,128)S(1)}, f32[256,128]{1,0:T(8,128)S(1)}) custom-call(s32[1]{0:T(128)} %bitcast.who.group.me, bf16[256,256]{1,0:T(8,128)(2,1)} %get-tuple-element.59.q, bf16[1,512,2,2048]{3,2,1,0:T(2,128)(2,1)} %kv_here.7, bf16[512,2,512]{2,1,0:T(2,128)(2,1)S(1)} %collective-permute-done.3.kv_there, ...), custom_call_target="tpu_custom_call" | custom-call | flops 335544320 | bytes 1310720 | tf_op jit(solution)/shard_map/attend_own/pallas_call | solution.py:198
  20.6 4.0 %attend_guest.3 = bf16[256,384]{1,0:T(8,128)(2,1)S(1)} custom-call(s32[1]{0:T(128)S(6)} %xor.16.group, bf16[256,256]{1,0:T(8,128)(2,1)S(1)} %collective-permute-done.6.q, bf16[1,512,2,2048]{3,2,1,0:T(2,128)(2,1)} %kv_here.7, bf16[512,2,512]{2,1,0:T(2,128)(2,1)S(1)} %collective-permute-done.5.kv_there), custom_call_target="tpu_custom_call" | custom-call | flops 268435456 | bytes 1048576 | tf_op jit(solution)/shard_map/attend_guest/pallas_call | solution.py:222
  25.9 4.2 %attend_guest.2 = bf16[256,384]{1,0:T(8,128)(2,1)S(1)} custom-call(s32[1]{0:T(128)S(6)} %xor.16.group, bf16[256,256]{1,0:T(8,128)(2,1)S(1)} %collective-permute-done.4.q, bf16[1,512,2,2048]{3,2,1,0:T(2,128)(2,1)} %kv_here.7, bf16[512,2,512]{2,1,0:T(2,128)(2,1)S(1)} %collective-permute-done.5.kv_there), custom_call_target="tpu_custom_call" | custom-call | flops 268435456 | bytes 1048576 | tf_op jit(solution)/shard_map/attend_guest/pallas_call | solution.py:222
  31.2 4.2 %attend_own.3 = (f32[256,256]{1,0:T(8,128)S(1)}, f32[256,128]{1,0:T(8,128)S(1)}) custom-call(s32[1]{0:T(128)} %bitcast.who.group.me, bf16[256,256]{1,0:T(8,128)(2,1)} %get-tuple-element.67.q, bf16[1,512,2,2048]{3,2,1,0:T(2,128)(2,1)} %kv_here.7, bf16[512,2,512]{2,1,0:T(2,128)(2,1)S(1)} %collective-permute-done.3.kv_there, ...), custom_call_target="tpu_custom_call" | custom-call | flops 335544320 | bytes 1310720 | tf_op jit(solution)/shard_map/attend_own/pallas_call | solution.py:198
  41.6 6.7 %collective-permute-done.10.arrived = bf16[64,2048]{1,0:T(8,128)(2,1)S(1)} collective-permute-done((bf16[64,2048]{1,0:T(8,128)(2,1)S(1)}, bf16[64,2048]{1,0:T(8,128)(2,1)S(1)}, u32[]{:S(2)}, u32[]{:S(2)}) %collective-permute-start.10) | collective-permute-done | bytes 262176 | tf_op jit(solution)/shard_map/ppermute | solution.py:36
  49.0 3.6 %collective-permute-start.11 = (bf16[32,2176]{1,0:T(8,128)(2,1)S(1)}, bf16[32,2176]{1,0:T(8,128)(2,1)S(1)}, u32[]{:S(2)}, u32[]{:S(2)}) collective-permute-start(bf16[32,2176]{1,0:T(8,128)(2,1)S(1)} %get-tuple-element.74), channel_id=1, source_target_pairs={{0,24},{4,28},{8,0},{12,4},{16,8},{20,12},{24,16},{28,20},{1,25},{... | collective-permute-start | bytes 417800 | tf_op jit(solution)/shard_map/ppermute | solution.py:46
  53.7 3.0 %collective-permute-done.11 = bf16[32,2176]{1,0:T(8,128)(2,1)S(1)} collective-permute-done((bf16[32,2176]{1,0:T(8,128)(2,1)S(1)}, bf16[32,2176]{1,0:T(8,128)(2,1)S(1)}, u32[]{:S(2)}, u32[]{:S(2)}) %collective-permute-start.11) | collective-permute-done | bytes 139296 | tf_op jit(solution)/shard_map/ppermute | solution.py:46
  56.8 7.3 %collective-permute-done.12 = bf16[32,2176]{1,0:T(8,128)(2,1)S(1)} collective-permute-done((bf16[32,2176]{1,0:T(8,128)(2,1)S(1)}, bf16[32,2176]{1,0:T(8,128)(2,1)S(1)}, u32[]{:S(2)}, u32[]{:S(2)}) %collective-permute-start.12) | collective-permute-done | bytes 139296 | tf_op jit(solution)/shard_map/ppermute | solution.py:46
  71.5 6.7 %collective-permute-done.15.refs_2_ = bf16[128,2176]{1,0:T(8,128)(2,1)S(1)} collective-permute-done((bf16[128,2176]{1,0:T(8,128)(2,1)S(1)}, bf16[128,2176]{1,0:T(8,128)(2,1)S(1)}, u32[]{:S(2)}, u32[]{:S(2)}) %collective-permute-start.15) | collective-permute-done | bytes 557088 | tf_op jit(solution)/shard_map/ppermute | solution.py:36
  81.0 3.0 %hold.3 = (bf16[2,2048,256]{2,1,0:T(8,128)(2,1)S(1)}, bf16[2,2048,256]{2,1,0:T(8,128)(2,1)S(1)}, bf16[2,256,2048]{2,1,0:T(8,128)(2,1)S(1)}) custom-call(bf16[2,2048,256]{2,1,0:T(8,128)(2,1)} %refs_0_, bf16[2,2048,256]{2,1,0:T(8,128)(2,1)} %refs_1_, bf16[2,256,2048]{2,1,0:T(8,128)(2,1)} %refs_2_), custom_call_target="tpu_custom_call" | custom-call | bytes 12582912 | tf_op jit(solution)/shard_map/hold/pallas_call | solution.py:454
  89.4 2.9 %experts.6 = bf16[384,2048]{1,0:T(8,128)(2,1)S(1)} custom-call(s32[1]{0:T(128)} %bitcast.9.group, bf16[128,2176]{1,0:T(8,128)(2,1)S(1)} %collective-permute-done.16.refs_0_, bf16[128,2176]{1,0:T(8,128)(2,1)S(1)} %collective-permute-done.17.refs_1_, bf16[128,2176]{1,0:T(8,128)(2,1)S(1)} %collective-permute-done.18.refs_2_, ...), custom_call_target="tpu_custom_call" | custom-call | flops 2415919104 | bytes 9437184 | tf_op jit(solution)/shard_map/experts/pallas_call | solution.py:382
  92.3 2.9 %experts.7 = bf16[384,2048]{1,0:T(8,128)(2,1)S(1)} custom-call(s32[1]{0:T(128)} %bitcast.9.group, bf16[128,2176]{1,0:T(8,128)(2,1)S(1)} %constant_dynamic-update-slice_fusion.refs_0_, bf16[128,2176]{1,0:T(8,128)(2,1)S(1)} %collective-permute-done.14.refs_1_, bf16[128,2176]{1,0:T(8,128)(2,1)S(1)} %collective-permute-done.15.refs_2_, ...), custom_call_target="tpu_custom_call" | custom-call | flops 2415919104 | bytes 9437184 | tf_op jit(solution)/shard_map/experts/pallas_call | solution.py:382
  102.9 2.9 %experts.9 = bf16[384,2048]{1,0:T(8,128)(2,1)S(1)} custom-call(s32[1]{0:T(128)} %bitcast.9.group, bf16[128,2176]{1,0:T(8,128)(2,1)S(1)} %collective-permute-done.32.refs_0_, bf16[128,2176]{1,0:T(8,128)(2,1)S(1)} %collective-permute-done.33.refs_1_, bf16[128,2176]{1,0:T(8,128)(2,1)S(1)} %collective-permute-done.34.refs_2_, ...), custom_call_target="tpu_custom_call" | custom-call | flops 2415919104 | bytes 9437184 | tf_op jit(solution)/shard_map/experts/pallas_call | solution.py:382
  105.8 2.9 %experts.10 = bf16[384,2048]{1,0:T(8,128)(2,1)S(1)} custom-call(s32[1]{0:T(128)} %bitcast.9.group, bf16[128,2176]{1,0:T(8,128)(2,1)S(1)} %constant_dynamic-update-slice_fusion.4.refs_0_, bf16[128,2176]{1,0:T(8,128)(2,1)S(1)} %collective-permute-done.27.refs_1_, bf16[128,2176]{1,0:T(8,128)(2,1)S(1)} %collective-permute-done.28.refs_2_, ...), custom_call_target="tpu_custom_call" | custom-call | flops 2415919104 | bytes 9437184 | tf_op jit(solution)/shard_map/experts/pallas_call | solution.py:382
  112.9 2.3 %experts.11 = (bf16[128,2048]{1,0:T(8,128)(2,1)S(1)}, bf16[128,2048]{1,0:T(8,128)(2,1)S(1)}) custom-call(s32[1]{0:T(128)} %bitcast.9.group, bf16[64,2176]{1,0:T(8,128)(2,1)S(1)} %collective-permute-done.38.refs_0_, bf16[64,2176]{1,0:T(8,128)(2,1)S(1)} %collective-permute-done.39.refs_1_, bf16[64,2176]{1,0:T(8,128)(2,1)S(1)} %collective-permute-done.36.refs_2_, ...), custom_call_target="tpu_custom_call" | custom-call | flops 1610612736 | bytes 8388608 | tf_op jit(solution)/shard_map/experts/pallas_call | solution.py:382
  122.8 3.9 %collective-permute-done.43 = bf16[64,2048]{1,0:T(8,128)(2,1)S(1)} collective-permute-done((bf16[64,2048]{1,0:T(8,128)(2,1)S(1)}, bf16[64,2048]{1,0:T(8,128)(2,1)S(1)}, u32[]{:S(2)}, u32[]{:S(2)}) %collective-permute-start.43) | collective-permute-done | bytes 262176 | tf_op jit(solution)/shard_map/ppermute | solution.py:36
  130.5 5.6 %collective-permute-done.41 = bf16[96,2048]{1,0:T(8,128)(2,1)S(1)} collective-permute-done((bf16[96,2048]{1,0:T(8,128)(2,1)S(1)}, bf16[96,2048]{1,0:T(8,128)(2,1)S(1)}, u32[]{:S(2)}, u32[]{:S(2)}) %collective-permute-start.41) | collective-permute-done | bytes 393248 | tf_op jit(solution)/shard_map/ppermute | solution.py:36
  139.0 2.8 %collective-permute-start.51 = (bf16[32,2048]{1,0:T(8,128)(2,1)S(1)}, bf16[32,2048]{1,0:T(8,128)(2,1)S(1)}, u32[]{:S(2)}, u32[]{:S(2)}) collective-permute-start(bf16[32,2048]{1,0:T(8,128)(2,1)S(1)} %get-tuple-element.125), channel_id=1, source_target_pairs={{0,24},{4,28},{8,0},{12,4},{16,8},{20,12},{24,16},{28,20},{1,25},{... | collective-permute-start | bytes 393224 | tf_op jit(solution)/shard_map/ppermute | solution.py:46
  149.7 4.6 %collective-permute-start.52 = (bf16[32,2048]{1,0:T(8,128)(2,1)S(1)}, bf16[32,2048]{1,0:T(8,128)(2,1)S(1)}, u32[]{:S(2)}, u32[]{:S(2)}) collective-permute-start(bf16[32,2048]{1,0:T(8,128)(2,1)S(1)} %get-tuple-element.128), channel_id=1, source_target_pairs={{0,24},{4,28},{8,0},{12,4},{16,8},{20,12},{24,16},{28,20},{1,25},{... | collective-permute-start | bytes 393224 | tf_op jit(solution)/shard_map/ppermute | solution.py:46
  154.6 3.9 %collective-permute-done.50 = bf16[32,2048]{1,0:T(8,128)(2,1)S(1)} collective-permute-done((bf16[32,2048]{1,0:T(8,128)(2,1)S(1)}, bf16[32,2048]{1,0:T(8,128)(2,1)S(1)}, u32[]{:S(2)}, u32[]{:S(2)}) %collective-permute-start.50) | collective-permute-done | bytes 131104 | tf_op jit(solution)/shard_map/ppermute | solution.py:46
  (168 shorter events, 65.9 us)
Async XLA Ops:
  0.0 10.0 %collective-permute-start.1 = (bf16[64,2048]{1,0:T(8,128)(2,1)}, bf16[64,2048]{1,0:T(8,128)(2,1)S(1)}, u32[]{:S(2)}, u32[]{:S(2)}) collective-permute-start(bf16[64,2048]{1,0:T(8,128)(2,1)} %tokens.1), channel_id=1, source_target_pairs={{0,2},{1,3},{2,0},{3,1},{4,6},{5,7},{6,4},{7,5},{8,10},{9,11},{10,... | collective-permute-start | bytes 786440 | tf_op jit(solution)/shard_map/ppermute | solution.py:36
  5.9 10.3 %collective-permute-start.3 = (bf16[512,2,512]{2,1,0:T(2,128)(2,1)}, bf16[512,2,512]{2,1,0:T(2,128)(2,1)S(1)}, u32[]{:S(2)}, u32[]{:S(2)}) collective-permute-start(bf16[512,2,512]{2,1,0:T(2,128)(2,1)} %get-tuple-element.60), channel_id=1, source_target_pairs={{0,1},{1,0},{2,3},{3,2},{4,5},{5,4},{6,7},{7,6},{8,9},{9,8},{10,11... | collective-permute-start | bytes 3145736 | tf_op jit(solution)/shard_map/ppermute | solution.py:36
  6.5 14.1 %collective-permute-start.5 = (bf16[512,2,512]{2,1,0:T(2,128)(2,1)}, bf16[512,2,512]{2,1,0:T(2,128)(2,1)S(1)}, u32[]{:S(2)}, u32[]{:S(2)}) collective-permute-start(bf16[512,2,512]{2,1,0:T(2,128)(2,1)} %get-tuple-element.57), channel_id=1, source_target_pairs={{0,1},{1,0},{2,3},{3,2},{4,5},{5,4},{6,7},{7,6},{8,9},{9,8},{10,11... | collective-permute-start | bytes 3145736 | tf_op jit(solution)/shard_map/ppermute | solution.py:36
  15.2 10.7 %collective-permute-start.4 = (bf16[256,256]{1,0:T(8,128)(2,1)}, bf16[256,256]{1,0:T(8,128)(2,1)S(1)}, u32[]{:S(2)}, u32[]{:S(2)}) collective-permute-start(bf16[256,256]{1,0:T(8,128)(2,1)} %get-tuple-element.67.q), channel_id=1, source_target_pairs={{0,2},{1,3},{2,0},{3,1},{4,6},{5,7},{6,4},{7,5},{8,10},{9,11},{10,... | collective-permute-start | bytes 393224 | tf_op jit(solution)/shard_map/ppermute | solution.py:36
  52.6 11.4 %collective-permute-start.12 = (bf16[32,2176]{1,0:T(8,128)(2,1)S(1)}, bf16[32,2176]{1,0:T(8,128)(2,1)S(1)}, u32[]{:S(2)}, u32[]{:S(2)}) collective-permute-start(bf16[32,2176]{1,0:T(8,128)(2,1)S(1)} %get-tuple-element.74), channel_id=1, source_target_pairs={{0,16},{4,20},{8,24},{12,28},{16,0},{20,4},{24,8},{28,12},{1,17},{... | collective-permute-start | bytes 417800 | tf_op jit(solution)/shard_map/ppermute | solution.py:46
  52.7 11.3 %collective-permute-start.13 = (bf16[32,2176]{1,0:T(8,128)(2,1)S(1)}, bf16[32,2176]{1,0:T(8,128)(2,1)S(1)}, u32[]{:S(2)}, u32[]{:S(2)}) collective-permute-start(bf16[32,2176]{1,0:T(8,128)(2,1)S(1)} %get-tuple-element.74), channel_id=1, source_target_pairs={{0,8},{4,12},{8,16},{12,20},{16,24},{20,28},{24,0},{28,4},{1,9},{5... | collective-permute-start | bytes 417800 | tf_op jit(solution)/shard_map/ppermute | solution.py:46
  64.1 14.0 %collective-permute-start.15 = (bf16[128,2176]{1,0:T(8,128)(2,1)S(1)}, bf16[128,2176]{1,0:T(8,128)(2,1)S(1)}, u32[]{:S(2)}, u32[]{:S(2)}) collective-permute-start(bf16[128,2176]{1,0:T(8,128)(2,1)S(1)} %constant_dynamic-update-slice_fusion.refs_0_), channel_id=1, source_target_pairs={{0,4},{4,0},{8,12},{12,8},{16,20},{20,16},{24,28},{28,24},{1,5},{5... | collective-permute-start | bytes 1671176 | tf_op jit(solution)/shard_map/ppermute | solution.py:36
  65.7 13.7 %collective-permute-start.14 = (bf16[128,2176]{1,0:T(8,128)(2,1)S(1)}, bf16[128,2176]{1,0:T(8,128)(2,1)S(1)}, u32[]{:S(2)}, u32[]{:S(2)}) collective-permute-start(bf16[128,2176]{1,0:T(8,128)(2,1)S(1)} %constant_dynamic-update-slice_fusion.refs_0_), channel_id=1, source_target_pairs={{0,2},{1,3},{2,0},{3,1},{4,6},{5,7},{6,4},{7,5},{8,10},{9,11},{10,... | collective-permute-start | bytes 1671176 | tf_op jit(solution)/shard_map/ppermute | solution.py:36
  66.8 17.2 %collective-permute-start.24 = (bf16[32,2176]{1,0:T(8,128)(2,1)S(1)}, bf16[32,2176]{1,0:T(8,128)(2,1)S(1)}, u32[]{:S(2)}, u32[]{:S(2)}) collective-permute-start(bf16[32,2176]{1,0:T(8,128)(2,1)S(1)} %get-tuple-element.88), channel_id=1, source_target_pairs={{0,24},{4,28},{8,0},{12,4},{16,8},{20,12},{24,16},{28,20},{1,25},{... | collective-permute-start | bytes 417800 | tf_op jit(solution)/shard_map/ppermute | solution.py:46
  68.2 15.8 %collective-permute-start.25 = (bf16[32,2176]{1,0:T(8,128)(2,1)S(1)}, bf16[32,2176]{1,0:T(8,128)(2,1)S(1)}, u32[]{:S(2)}, u32[]{:S(2)}) collective-permute-start(bf16[32,2176]{1,0:T(8,128)(2,1)S(1)} %get-tuple-element.88), channel_id=1, source_target_pairs={{0,16},{4,20},{8,24},{12,28},{16,0},{20,4},{24,8},{28,12},{1,17},{... | collective-permute-start | bytes 417800 | tf_op jit(solution)/shard_map/ppermute | solution.py:46
  69.4 15.1 %collective-permute-start.26 = (bf16[32,2176]{1,0:T(8,128)(2,1)S(1)}, bf16[32,2176]{1,0:T(8,128)(2,1)S(1)}, u32[]{:S(2)}, u32[]{:S(2)}) collective-permute-start(bf16[32,2176]{1,0:T(8,128)(2,1)S(1)} %get-tuple-element.88), channel_id=1, source_target_pairs={{0,8},{4,12},{8,16},{12,20},{16,24},{20,28},{24,0},{28,4},{1,9},{5... | collective-permute-start | bytes 417800 | tf_op jit(solution)/shard_map/ppermute | solution.py:46
  86.4 13.3 %collective-permute-start.27 = (bf16[128,2176]{1,0:T(8,128)(2,1)S(1)}, bf16[128,2176]{1,0:T(8,128)(2,1)S(1)}, u32[]{:S(2)}, u32[]{:S(2)}) collective-permute-start(bf16[128,2176]{1,0:T(8,128)(2,1)S(1)} %constant_dynamic-update-slice_fusion.4.refs_0_), channel_id=1, source_target_pairs={{0,2},{1,3},{2,0},{3,1},{4,6},{5,7},{6,4},{7,5},{8,10},{9,11},{10,... | collective-permute-start | bytes 1671176 | tf_op jit(solution)/shard_map/ppermute | solution.py:36
  87.5 12.8 %collective-permute-start.28 = (bf16[128,2176]{1,0:T(8,128)(2,1)S(1)}, bf16[128,2176]{1,0:T(8,128)(2,1)S(1)}, u32[]{:S(2)}, u32[]{:S(2)}) collective-permute-start(bf16[128,2176]{1,0:T(8,128)(2,1)S(1)} %constant_dynamic-update-slice_fusion.4.refs_0_), channel_id=1, source_target_pairs={{0,4},{4,0},{8,12},{12,8},{16,20},{20,16},{24,28},{28,24},{1,5},{5... | collective-permute-start | bytes 1671176 | tf_op jit(solution)/shard_map/ppermute | solution.py:36
  100.4 15.4 %collective-permute-start.19 = (bf16[384,2048]{1,0:T(8,128)(2,1)S(1)}, bf16[384,2048]{1,0:T(8,128)(2,1)S(1)}, u32[]{:S(2)}, u32[]{:S(2)}) collective-permute-start(bf16[384,2048]{1,0:T(8,128)(2,1)S(1)} %experts.6), channel_id=1, source_target_pairs={{0,1},{1,0},{2,3},{3,2},{4,5},{5,4},{6,7},{7,6},{8,9},{9,8},{10,11... | collective-permute-start | bytes 4718600 | tf_op jit(solution)/shard_map/ppermute | solution.py:36
  121.0 15.2 %collective-permute-start.41 = (bf16[96,2048]{1,0:T(8,128)(2,1)S(1)}, bf16[96,2048]{1,0:T(8,128)(2,1)S(1)}, u32[]{:S(2)}, u32[]{:S(2)}) collective-permute-start(bf16[96,2048]{1,0:T(8,128)(2,1)S(1)} %pad_maximum_fusion), channel_id=1, source_target_pairs={{0,4},{4,0},{8,12},{12,8},{16,20},{20,16},{24,28},{28,24},{1,5},{5... | collective-permute-start | bytes 1179656 | tf_op jit(solution)/shard_map/ppermute | solution.py:36
  121.6 14.5 %collective-permute-start.42 = (bf16[96,2048]{1,0:T(8,128)(2,1)S(1)}, bf16[96,2048]{1,0:T(8,128)(2,1)S(1)}, u32[]{:S(2)}, u32[]{:S(2)}) collective-permute-start(bf16[96,2048]{1,0:T(8,128)(2,1)S(1)} %pad_maximum_fusion.1), channel_id=1, source_target_pairs={{0,2},{1,3},{2,0},{3,1},{4,6},{5,7},{6,4},{7,5},{8,10},{9,11},{10,... | collective-permute-start | bytes 1179656 | tf_op jit(solution)/shard_map/ppermute | solution.py:36
  127.9 15.8 %collective-permute-start.46 = (bf16[96,2048]{1,0:T(8,128)(2,1)S(1)}, bf16[96,2048]{1,0:T(8,128)(2,1)S(1)}, u32[]{:S(2)}, u32[]{:S(2)}) collective-permute-start(bf16[96,2048]{1,0:T(8,128)(2,1)S(1)} %pad_maximum_fusion.2), channel_id=1, source_target_pairs={{0,4},{4,0},{8,12},{12,8},{16,20},{20,16},{24,28},{28,24},{1,5},{5... | collective-permute-start | bytes 1179656 | tf_op jit(solution)/shard_map/ppermute | solution.py:36
  129.5 14.2 %collective-permute-start.47 = (bf16[96,2048]{1,0:T(8,128)(2,1)S(1)}, bf16[96,2048]{1,0:T(8,128)(2,1)S(1)}, u32[]{:S(2)}, u32[]{:S(2)}) collective-permute-start(bf16[96,2048]{1,0:T(8,128)(2,1)S(1)} %pad_maximum_fusion.3), channel_id=1, source_target_pairs={{0,2},{1,3},{2,0},{3,1},{4,6},{5,7},{6,4},{7,5},{8,10},{9,11},{10,... | collective-permute-start | bytes 1179656 | tf_op jit(solution)/shard_map/ppermute | solution.py:36
  136.3 10.0 %collective-permute-start.45 = (bf16[32,2048]{1,0:T(8,128)(2,1)S(1)}, bf16[32,2048]{1,0:T(8,128)(2,1)S(1)}, u32[]{:S(2)}, u32[]{:S(2)}) collective-permute-start(bf16[32,2048]{1,0:T(8,128)(2,1)S(1)} %get-tuple-element.127), channel_id=1, source_target_pairs={{0,8},{4,12},{8,16},{12,20},{16,24},{20,28},{24,0},{28,4},{1,9},{5... | collective-permute-start | bytes 393224 | tf_op jit(solution)/shard_map/ppermute | solution.py:46
  137.0 10.8 %collective-permute-start.49 = (bf16[32,2048]{1,0:T(8,128)(2,1)S(1)}, bf16[32,2048]{1,0:T(8,128)(2,1)S(1)}, u32[]{:S(2)}, u32[]{:S(2)}) collective-permute-start(bf16[32,2048]{1,0:T(8,128)(2,1)S(1)} %get-tuple-element.126), channel_id=1, source_target_pairs={{0,16},{4,20},{8,24},{12,28},{16,0},{20,4},{24,8},{28,12},{1,17},{... | collective-permute-start | bytes 393224 | tf_op jit(solution)/shard_map/ppermute | solution.py:46
  139.0 10.7 %collective-permute-start.51 = (bf16[32,2048]{1,0:T(8,128)(2,1)S(1)}, bf16[32,2048]{1,0:T(8,128)(2,1)S(1)}, u32[]{:S(2)}, u32[]{:S(2)}) collective-permute-start(bf16[32,2048]{1,0:T(8,128)(2,1)S(1)} %get-tuple-element.125), channel_id=1, source_target_pairs={{0,24},{4,28},{8,0},{12,4},{16,8},{20,12},{24,16},{28,20},{1,25},{... | collective-permute-start | bytes 393224 | tf_op jit(solution)/shard_map/ppermute | solution.py:46
  143.9 14.9 %collective-permute-start.53 = (bf16[64,2048]{1,0:T(8,128)(2,1)S(1)}, bf16[64,2048]{1,0:T(8,128)(2,1)S(1)}, u32[]{:S(2)}, u32[]{:S(2)}) collective-permute-start(bf16[64,2048]{1,0:T(8,128)(2,1)S(1)} %pad_maximum_fusion.4), channel_id=1, source_target_pairs={{0,2},{1,3},{2,0},{3,1},{4,6},{5,7},{6,4},{7,5},{8,10},{9,11},{10,... | collective-permute-start | bytes 786440 | tf_op jit(solution)/shard_map/ppermute | solution.py:36
  145.0 13.7 %collective-permute-start.54 = (bf16[64,2048]{1,0:T(8,128)(2,1)S(1)}, bf16[64,2048]{1,0:T(8,128)(2,1)S(1)}, u32[]{:S(2)}, u32[]{:S(2)}) collective-permute-start(bf16[64,2048]{1,0:T(8,128)(2,1)S(1)} %pad_maximum_fusion.5), channel_id=1, source_target_pairs={{0,4},{4,0},{8,12},{12,8},{16,20},{20,16},{24,28},{28,24},{1,5},{5... | collective-permute-start | bytes 786440 | tf_op jit(solution)/shard_map/ppermute | solution.py:36
  147.8 10.7 %collective-permute-start.50 = (bf16[32,2048]{1,0:T(8,128)(2,1)S(1)}, bf16[32,2048]{1,0:T(8,128)(2,1)S(1)}, u32[]{:S(2)}, u32[]{:S(2)}) collective-permute-start(bf16[32,2048]{1,0:T(8,128)(2,1)S(1)} %get-tuple-element.129), channel_id=1, source_target_pairs={{0,16},{4,20},{8,24},{12,28},{16,0},{20,4},{24,8},{28,12},{1,17},{... | collective-permute-start | bytes 393224 | tf_op jit(solution)/shard_map/ppermute | solution.py:46
  (38 other events, 217.7 us)
